TPU v7x, 32 devices: a whole 2x2x4 slice. The times are simulated.
32 devices in a mesh: fam: 2 (over x), tm: 8 (over z, y), chan: 2 (over core).
Axes of the slice: x: 2, y: 2, z: 4, core: 2. Of those that a mesh axis runs over, the one named last changes fastest.
Arguments:
- records: float32 [3072, 4096], P(('fam', 'tm', 'chan')), parts along dimension 0, may hold values from -6 to 6
- row_dest: int32 [3072], P(('fam', 'tm', 'chan')), parts along dimension 0, may hold values from -1 to 7, as said below
- row_chan: int32 [3072], P(('fam', 'tm', 'chan')), parts along dimension 0, may hold values from 0 to 47, as said below
- row_len: int32 [3072], P(('fam', 'tm', 'chan')), parts along dimension 0, may hold values from 2048 to 4096
- templates: float32 [64, 16, 256], P(('fam', 'tm'), 'chan'), parts along dimension 0, may hold values from -6 to 6
- tmpl_chan: int32 [64, 16], P(('fam', 'tm'), 'chan'), parts along dimension 0, may hold values from 0 to 47
- tmpl_off: int32 [64, 16], P(('fam', 'tm'), 'chan'), parts along dimension 0, may hold values from 0 to 255
Outputs:
- detection: float32 [16, 4, 4, 3584], P(('fam', 'tm'), None, None, 'chan'), parts along dimension 0
There are 2 independent parts, one for each index of `fam`. A program takes and returns all parts, laid end to end along the dimension named above; each array names one. Nothing has to cross between parts.
Inputs may be any that keep to these rules, and one draw needn't show every extreme that they name: `row_dest`: within the slots of the owners in one channel half, every pair of a time segment and a channel appears exactly once; one owner holds at most 12 rows of one time segment, and some owner holds exactly 12 of each. `row_chan`: 0 on empty slots.
All inputs are finite; a program needn't handle non-finite values.
Results may differ from a plain program's by a relative error of at most 0.0003.
Values sent between devices are 32-bit elements; how exact they have to be, the bound alone decides.
No kernel may reach another device: no remote copies, remote signals or barrier semaphores. Data moves between devices by JAX's collectives and lax.ppermute only.
A program may use at most 128 MiB of HBM per device.

v0:
```python
import jax
import jax.numpy as jnp
from jax import lax
from jax.sharding import PartitionSpec as P

TCH = 16
MAXOFF = 256
STOPS = 4


FLOOR_SHARE = 0.25
TEMPLATE_EPS = 1e-06
highest = lax.Precision.HIGHEST


def shifted(x, axis, by):
    devices = lax.axis_size(axis)
    return lax.ppermute(x, axis, [(i, (i + by) % devices) for i in range(devices)])


def normalized(template_rows):
    centred = template_rows - jnp.mean(template_rows, axis=-1, keepdims=True)
    energy = jnp.sum(centred * centred, axis=-1, keepdims=True)
    return centred / jnp.sqrt(energy + template_rows.shape[-1] * TEMPLATE_EPS)


def window_scale(waveform, tap_count):
    channel_count, sample_count = waveform.shape
    blocks = waveform.reshape(channel_count, sample_count // tap_count, tap_count)
    paired = jnp.concatenate([blocks[:, :-1], blocks[:, 1:]], axis=2)
    rows_idx = lax.broadcasted_iota(jnp.int32, (2 * tap_count, tap_count), 0)
    cols_idx = lax.broadcasted_iota(jnp.int32, (2 * tap_count, tap_count), 1)
    band = ((rows_idx >= cols_idx) & (rows_idx < cols_idx + tap_count)).astype(jnp.float32)
    win_sum = jnp.einsum("cbu,ur->cbr", paired, band, precision=highest).reshape(channel_count, -1)
    win_sq = jnp.einsum("cbu,ur->cbr", paired * paired, band, precision=highest).reshape(
        channel_count, -1
    )
    variance = win_sq - win_sum * win_sum / tap_count
    return 1.0 / jnp.sqrt(jnp.maximum(variance, FLOOR_SHARE * tap_count))


def toeplitz_table(pair_rows, block_width):
    pair_count, tap_count = pair_rows.shape
    window = tap_count + block_width
    padded = jnp.pad(pair_rows, ((0, 0), (0, window + 1 - tap_count)))
    tiled = jnp.tile(padded, (1, block_width))[:, : block_width * window]
    return tiled.reshape(pair_count, block_width, window)


def correlate(waveform, inv_sigma, unit_rows, chan_map, offsets):
    template_count, half_taps, tap_count = unit_rows.shape
    block_width = tap_count // 4
    shift_count = tap_count // block_width
    lag_count = waveform.shape[1] - tap_count - MAXOFF
    block_count = lag_count // block_width
    pair_rows = unit_rows.reshape(-1, tap_count)
    pair_chan = chan_map.reshape(-1)
    pair_off = offsets.reshape(-1)

    def cut_segment(channel, offset):
        return lax.dynamic_slice(waveform, (channel, offset), (1, lag_count + tap_count))[0]

    def cut_scale(channel, offset):
        return lax.dynamic_slice(inv_sigma, (channel, offset), (1, lag_count))[0]

    segments = jax.vmap(cut_segment)(pair_chan, pair_off)
    pieces = segments.reshape(segments.shape[0], -1, block_width)
    windows = jnp.concatenate(
        [pieces[:, shift : block_count + shift] for shift in range(shift_count + 1)], axis=2
    )
    toeplitz = toeplitz_table(pair_rows, block_width)
    correlation = jnp.einsum("pbu,pru->pbr", windows, toeplitz, precision=highest).reshape(
        -1, lag_count
    )
    scales = jax.vmap(cut_scale)(pair_chan, pair_off)
    ratios = (correlation * scales).reshape(template_count, half_taps, lag_count)
    stack_gain = jnp.sqrt(jnp.float32(tap_count * TCH)) / TCH
    return stack_gain * jnp.sum(ratios, axis=1)


def local(records, row_dest, row_chan, row_len, templates, tmpl_chan, tmpl_off):
    slot_count, sample_count = records.shape
    loop_size = lax.axis_size("tm")
    capacity = slot_count // loop_size
    tap_count = templates.shape[-1]
    positions = lax.broadcasted_iota(jnp.int32, records.shape, 1)
    masked = jnp.where(positions < row_len[:, None], records, jnp.zeros_like(records))
    slot_ids = jnp.arange(slot_count, dtype=jnp.int32)
    earlier = (row_dest[:, None] == row_dest[None, :]) & (slot_ids[None, :] < slot_ids[:, None])
    rank_within = jnp.sum(earlier.astype(jnp.int32), axis=1)
    target = jnp.where(row_dest >= 0, row_dest * capacity + rank_within, slot_count)
    outgoing = (
        jnp.zeros_like(masked)
        .at[target]
        .set(masked, mode="drop")
        .reshape(loop_size, capacity, sample_count)
    )
    outgoing_ids = (
        jnp.full((slot_count,), -1, jnp.int32)
        .at[target]
        .set(row_chan, mode="drop")
        .reshape(loop_size, capacity)
    )
    channel_count = slot_count // 2
    arrived, arrived_ids = (
        lax.all_to_all(outgoing, "tm", split_axis=0, concat_axis=0, tiled=True),
        lax.all_to_all(outgoing_ids, "tm", split_axis=0, concat_axis=0, tiled=True),
    )
    arrived = arrived.reshape(slot_count, sample_count)
    arrived_ids = arrived_ids.reshape(slot_count)
    places = jnp.where(arrived_ids >= 0, arrived_ids, channel_count)
    waveform = (
        jnp.zeros((channel_count, sample_count), jnp.float32).at[places].set(arrived, mode="drop")
    )
    inv_sigma = window_scale(waveform, tap_count)
    visit_start = (normalized(templates), tmpl_chan, tmpl_off)
    visiting = visit_start
    partials = []
    for stop_index in range(STOPS):
        if stop_index > 0:
            visiting = shifted((visiting[0], visiting[1], visiting[2]), "tm", 1)
        partials.append(correlate(waveform, inv_sigma, visiting[0], visiting[1], visiting[2]))
    summed = lax.psum_scatter(jnp.stack(partials), "chan", scatter_dimension=2, tiled=True)
    return summed[None]


def solution(mesh):
    in_specs = (
        P(("fam", "tm", "chan"), None),
        P(("fam", "tm", "chan")),
        P(("fam", "tm", "chan")),
        P(("fam", "tm", "chan")),
        P(("fam", "tm"), "chan", None),
        P(("fam", "tm"), "chan"),
        P(("fam", "tm"), "chan"),
    )
    out_specs = P(("fam", "tm"), None, None, "chan")
    return jax.shard_map(local, mesh=mesh, in_specs=in_specs, out_specs=out_specs, check_vma=False)
```

profile of v0, /device:TPU:0, one launch (start us, length us, event | category | flops | bytes accessed | tf_op | source)
XLA Modules:
  0.0 952.9 jit_solution(1680050459382184153)
XLA Ops:
  9.8 7.3 all-to-all-start
  26.3 2.9 scatter_custom_fusion.1
  30.7 4.7 all-to-all-start.1
  35.7 2.7 tile.17
  40.1 2.6 reshape.508
  46.5 26.4 %collective-permute-done.3 = s32[4,8]{1,0:T(4,128)S(1)} collective-permute-done((s32[4,8]{1,0:T(4,128)S(1)}, s32[4,8]{1,0:T(4,128)S(1)}, u32[]{:S(2)}, u32[]{:S(2)}) %collective-permute-start.3) | collective-permute-done | bytes 160 | tf_op jit(solution)/shard_map/ppermute | solution.py:18
  73.3 5.9 collective-permute-done.6
  79.5 6.1 collective-permute-start.5
  87.2 3.5 collective-permute-start.8
  90.9 2.7 tile.19
  95.4 2.7 reshape.514
  98.3 2.8 tile.41
  102.8 2.7 reshape.519
  105.8 2.7 tile.43
  110.2 2.7 reshape.524
  116.7 62.3 %while.14 = (s32[]{:T(128)}, f32[48,4096]{1,0:T(8,128)S(1)}, s32[32,2]{0,1:T(2,128)S(1)}, f32[32,1,3840]{2,1,0:T(1,128)S(1)}, s32[]{:T(128)}) while((s32[]{:T(128)}, f32[48,4096]{1,0:T(8,128)S(1)}, s32[32,2]{0,1:T(2,128)S(1)}, f32[32,1,3840]{2,1,0:T(1,128)S(1)}, s32[]{:T(128)}) %tuple.144), condition=%wide.while_cond.6, body=%wide.while_body.6.sunk | while | flops 2 | bytes 30837 | solution.py:61
  183.7 4.9 concatenate.50
  188.6 6.4 fusion.44
  201.5 72.3 %while.15 = (s32[]{:T(128)}, f32[48,3840]{1,0:T(8,128)S(1)}, s32[32,2]{0,1:T(2,128)S(1)}, f32[32,1,3584]{2,0,1:T(8,128)S(1)}, s32[]{:T(128)}, /*index=5*/s32[]{:T(128)}) while((s32[]{:T(128)}, f32[48,3840]{1,0:T(8,128)S(1)}, s32[32,2]{0,1:T(2,128)S(1)}, f32[32,1,3584]{2,0,1:T(8,128)S(1)}, s32[]{:T(128)}, /*index=5*/s32[]{:T(128)}) %tuple.173), condition=%wide.while_cond.7, body=%wide.while_body.7.sunk | while | flops 2 | bytes 57469 | solution.py:64
  275.8 92.8 %while.12 = (s32[]{:T(128)}, f32[48,4096]{1,0:T(8,128)}, s32[32,2]{0,1:T(2,128)S(1)}, f32[32,1,3840]{2,1,0:T(1,128)S(1)}, s32[]{:T(128)}) while((s32[]{:T(128)}, f32[48,4096]{1,0:T(8,128)}, s32[32,2]{0,1:T(2,128)S(1)}, f32[32,1,3840]{2,1,0:T(1,128)S(1)}, s32[]{:T(128)}) %tuple.170), condition=%wide.while_cond.4, body=%wide.while_body.4.sunk | while | flops 2 | bytes 30837 | solution.py:61
  372.4 4.9 concatenate.47
  377.3 6.3 fusion.43
  385.9 103.7 %while.13 = (s32[]{:T(128)}, f32[48,3840]{1,0:T(8,128)}, s32[32,2]{0,1:T(2,128)S(1)}, f32[32,1,3584]{2,0,1:T(8,128)S(1)}, s32[]{:T(128)}, /*index=5*/s32[]{:T(128)}) while((s32[]{:T(128)}, f32[48,3840]{1,0:T(8,128)}, s32[32,2]{0,1:T(2,128)S(1)}, f32[32,1,3584]{2,0,1:T(8,128)S(1)}, s32[]{:T(128)}, /*index=5*/s32[]{:T(128)}) %tuple.174), condition=%wide.while_cond.5, body=%wide.while_body.5.sunk | while | flops 2 | bytes 57469 | solution.py:64
  490.7 93.7 %while.10 = (s32[]{:T(128)}, f32[48,4096]{1,0:T(8,128)}, s32[32,2]{0,1:T(2,128)S(1)}, f32[32,1,3840]{2,1,0:T(1,128)S(1)}, s32[]{:T(128)}) while((s32[]{:T(128)}, f32[48,4096]{1,0:T(8,128)}, s32[32,2]{0,1:T(2,128)S(1)}, f32[32,1,3840]{2,1,0:T(1,128)S(1)}, s32[]{:T(128)}) %tuple.171), condition=%wide.while_cond.2, body=%wide.while_body.2.sunk | while | flops 2 | bytes 30837 | solution.py:61
  491.3 2.3 bitcast_dynamic-update-slice_fusion.9
  500.1 2.3 bitcast_dynamic-update-slice_fusion.9
  503.0 2.3 bitcast_dynamic-update-slice_fusion.9
  511.8 2.3 bitcast_dynamic-update-slice_fusion.9
  514.7 2.3 bitcast_dynamic-update-slice_fusion.9
  520.6 2.3 bitcast_dynamic-update-slice_fusion.9
  523.5 2.3 bitcast_dynamic-update-slice_fusion.9
  532.3 2.3 bitcast_dynamic-update-slice_fusion.9
  535.2 2.3 bitcast_dynamic-update-slice_fusion.9
  544.0 2.3 bitcast_dynamic-update-slice_fusion.9
  588.2 5.1 concatenate.44
  593.4 6.4 fusion.42
  602.0 101.6 %while.11 = (s32[]{:T(128)}, f32[48,3840]{1,0:T(8,128)}, s32[32,2]{0,1:T(2,128)S(1)}, f32[32,1,3584]{2,0,1:T(8,128)S(1)}, s32[]{:T(128)}, /*index=5*/s32[]{:T(128)}) while((s32[]{:T(128)}, f32[48,3840]{1,0:T(8,128)}, s32[32,2]{0,1:T(2,128)S(1)}, f32[32,1,3584]{2,0,1:T(8,128)S(1)}, s32[]{:T(128)}, /*index=5*/s32[]{:T(128)}) %tuple.175), condition=%wide.while_cond.3, body=%wide.while_body.3.sunk | while | flops 2 | bytes 57469 | solution.py:64
  704.6 90.6 %while.8 = (s32[]{:T(128)}, f32[48,4096]{1,0:T(8,128)}, s32[32,2]{0,1:T(2,128)S(1)}, f32[32,1,3840]{2,1,0:T(1,128)S(1)}, s32[]{:T(128)}) while((s32[]{:T(128)}, f32[48,4096]{1,0:T(8,128)}, s32[32,2]{0,1:T(2,128)S(1)}, f32[32,1,3840]{2,1,0:T(1,128)S(1)}, s32[]{:T(128)}) %tuple.172), condition=%wide.while_cond, body=%wide.while_body.sunk | while | flops 2 | bytes 30837 | solution.py:61
  796.8 2.3 fusion.36
  799.1 4.9 concatenate.40
  804.0 6.4 fusion.41
  810.4 2.3 reshape.509
  812.8 101.6 %while.9 = (s32[]{:T(128)}, f32[48,3840]{1,0:T(8,128)}, s32[32,2]{0,1:T(2,128)S(1)}, f32[32,1,3584]{2,0,1:T(8,128)S(1)}, s32[]{:T(128)}, /*index=5*/s32[]{:T(128)}) while((s32[]{:T(128)}, f32[48,3840]{1,0:T(8,128)}, s32[32,2]{0,1:T(2,128)S(1)}, f32[32,1,3584]{2,0,1:T(8,128)S(1)}, s32[]{:T(128)}, /*index=5*/s32[]{:T(128)}) %tuple.176), condition=%wide.while_cond.1, body=%wide.while_body.1.sunk | while | flops 2 | bytes 57469 | solution.py:64
  915.7 5.0 copy.19
  920.6 6.7 reshape.706
  927.4 10.6 %reduce-scatter.4.cloned.1.call-done = f32[1792,16]{1,0:T(8,128)} async-done(((f32[3584,16]{1,0:T(8,128)}), f32[1792,16]{1,0:T(8,128)}) %reduce-scatter.4.cloned.1.call-update) | async-done | bytes 114704
  938.0 3.9 reshape.707
  941.9 4.0 copy.20
  (1028 shorter events, 750.4 us)
Async XLA Ops:
  9.8 20.9 %all-to-all-start = ((s32[8,1,12]{2,1,0:T(1,128)}), s32[8,1,12]{2,1,0:T(1,128)S(1)}, u32[]{:S(2)}, u32[]{:S(2)}) async-start(s32[8,1,12]{2,1,0:T(1,128)} %bitcast), calls=%async_computation | async-start | bytes 8192 | tf_op jit(solution)/shard_map/all_to_all | solution.py:107
  17.1 25.7 %collective-permute-start = (s32[4,8]{1,0:T(4,128)}, s32[4,8]{1,0:T(4,128)S(1)}, u32[]{:S(2)}, u32[]{:S(2)}) collective-permute-start(s32[4,8]{1,0:T(4,128)} %param.12), channel_id=1, source_target_pairs={{0,2},{2,4},{4,6},{6,8},{8,10},{10,12},{12,14},{14,0},{1,3},{3,5},... | collective-permute-start | bytes 392 | tf_op jit(solution)/shard_map/ppermute | solution.py:18
  19.1 25.7 %collective-permute-start.1 = (s32[4,8]{1,0:T(4,128)}, s32[4,8]{1,0:T(4,128)S(1)}, u32[]{:S(2)}, u32[]{:S(2)}) collective-permute-start(s32[4,8]{1,0:T(4,128)} %param.13), channel_id=1, source_target_pairs={{0,2},{2,4},{4,6},{6,8},{8,10},{10,12},{12,14},{14,0},{1,3},{3,5},... | collective-permute-start | bytes 392 | tf_op jit(solution)/shard_map/ppermute | solution.py:18
  23.2 56.3 %collective-permute-start.2 = (f32[4,8,256]{2,1,0:T(8,128)S(1)}, f32[4,8,256]{2,1,0:T(8,128)S(1)}, u32[]{:S(2)}, u32[]{:S(2)}) collective-permute-start(f32[4,8,256]{2,1,0:T(8,128)S(1)} %subtract_divide_fusion), channel_id=1, source_target_pairs={{0,2},{2,4},{4,6},{6,8},{8,10},{10,12},{12,14},{14,0},{1,3},{3,5},... | collective-permute-start | bytes 98312 | tf_op jit(solution)/shard_map/ppermute | solution.py:18
  30.7 4.7 copy-start.16
  30.7 82.2 %all-to-all-start.1 = ((f32[8,12,4096]{2,1,0:T(8,128)}), f32[8,12,4096]{2,1,0:T(8,128)}, u32[]{:S(2)}, u32[]{:S(2)}) async-start(f32[8,12,4096]{2,1,0:T(8,128)} %reshape.503), calls=%async_computation.1 | async-start | bytes 4194304 | tf_op jit(solution)/shard_map/all_to_all | solution.py:106
  35.3 902.6 %reduce-scatter.4.cloned.1.call-start = ((), (), s32[]{:S(2)}) async-start(), calls=%async_computation.3 | async-start | bytes 2752512
  38.4 1.7 slice-start
  42.8 30.1 %collective-permute-start.3 = (s32[4,8]{1,0:T(4,128)S(1)}, s32[4,8]{1,0:T(4,128)S(1)}, u32[]{:S(2)}, u32[]{:S(2)}) collective-permute-start(s32[4,8]{1,0:T(4,128)S(1)} %collective-permute-done), channel_id=1, source_target_pairs={{0,2},{2,4},{4,6},{6,8},{8,10},{10,12},{12,14},{14,0},{1,3},{3,5},... | collective-permute-start | bytes 392 | tf_op jit(solution)/shard_map/ppermute | solution.py:18
  44.9 28.0 %collective-permute-start.4 = (s32[4,8]{1,0:T(4,128)S(1)}, s32[4,8]{1,0:T(4,128)S(1)}, u32[]{:S(2)}, u32[]{:S(2)}) collective-permute-start(s32[4,8]{1,0:T(4,128)S(1)} %collective-permute-done.1), channel_id=1, source_target_pairs={{0,2},{2,4},{4,6},{6,8},{8,10},{10,12},{12,14},{14,0},{1,3},{3,5},... | collective-permute-start | bytes 392 | tf_op jit(solution)/shard_map/ppermute | solution.py:18
  72.8 6.4 collective-permute-start.6
  73.0 6.3 collective-permute-start.7
  79.5 7.7 collective-permute-start.5
  87.2 18.3 %collective-permute-start.8 = (f32[4,8,256]{2,1,0:T(8,128)S(1)}, f32[4,8,256]{2,1,0:T(8,128)S(1)}, u32[]{:S(2)}, u32[]{:S(2)}) collective-permute-start(f32[4,8,256]{2,1,0:T(8,128)S(1)} %collective-permute-done.5), channel_id=1, source_target_pairs={{0,2},{2,4},{4,6},{6,8},{8,10},{10,12},{12,14},{14,0},{1,3},{3,5},... | collective-permute-start | bytes 98312 | tf_op jit(solution)/shard_map/ppermute | solution.py:18
  93.6 1.7 slice-start.1
  101.1 1.7 slice-start.2
  108.5 1.7 slice-start.3
  178.9 0.9 copy-start.4
  183.6 4.9 copy-start.3
  273.9 0.8 copy-start.5
  274.7 0.9 copy-start.15
  372.4 4.9 copy-start.2
  489.6 0.8 copy-start.7
  588.2 5.2 copy-start.1
  703.6 0.8 copy-start.9
  799.1 4.9 copy-start
  810.4 104.0 %copy-start.6 = (f32[32,1,3584]{2,0,1:T(8,128)S(1)}, f32[32,1,3584]{2,0,1:T(8,128)}, u32[]{:S(2)}) copy-start(f32[32,1,3584]{2,0,1:T(8,128)} %copy-done.5) | copy-start | bytes 1376260
  810.4 104.0 %copy-start.11 = (f32[4,8,3584]{2,1,0:T(8,128)S(1)}, f32[4,8,3584]{2,1,0:T(8,128)}, u32[]{:S(2)}) copy-start(f32[4,8,3584]{2,1,0:T(8,128)} %reshape.525) | copy-start | bytes 1376260
  810.4 104.2 %copy-start.8 = (f32[32,1,3584]{2,0,1:T(8,128)S(1)}, f32[32,1,3584]{2,0,1:T(8,128)}, u32[]{:S(2)}) copy-start(f32[32,1,3584]{2,0,1:T(8,128)} %copy-done.7) | copy-start | bytes 1376260
  810.4 104.2 %copy-start.12 = (f32[4,8,3584]{2,1,0:T(8,128)S(1)}, f32[4,8,3584]{2,1,0:T(8,128)}, u32[]{:S(2)}) copy-start(f32[4,8,3584]{2,1,0:T(8,128)} %reshape.520) | copy-start | bytes 1376260
  810.4 104.4 %copy-start.10 = (f32[32,1,3584]{2,0,1:T(8,128)S(1)}, f32[32,1,3584]{2,0,1:T(8,128)}, u32[]{:S(2)}) copy-start(f32[32,1,3584]{2,0,1:T(8,128)} %copy-done.9) | copy-start | bytes 1376260
  810.4 104.4 %copy-start.13 = (f32[4,8,3584]{2,1,0:T(8,128)S(1)}, f32[4,8,3584]{2,1,0:T(8,128)}, u32[]{:S(2)}) copy-start(f32[4,8,3584]{2,1,0:T(8,128)} %reshape.515) | copy-start | bytes 1376260
  914.4 1.0 copy-start.14
Sparse Core Ops, SparseCore 0:
  927.5 10.4 reduce-scatter.3
where the time goes:
time: 967 us; the launch traced here: 953 us
  local copies, waits for them, and re-layouts  817 us (84%)
  waiting for transfers between devices  43.4 us (4%)
  starting transfers between devices  30.4 us (3%)
  matrix products  27.3 us (3%)
  between operations  14.1 us (1%)
  other arithmetic  13.3 us (1%)
    gather x896, local copies, waits for them, and re-layouts  712 us
    ppermute x9, waiting for transfers between devices, shifted(): lax.ppermute(x, axis, [(i, (i + by) % devices) for i in range(devices)])  32.7 us
    unnamed x48, local copies, waits for them, and re-layouts  27.1 us
    dot_general x4, matrix products, correlate(): jnp.einsum('pbu,pru->pbr', windows, toeplitz, precision=highest)  25.4 us
    concatenate x4, local copies, waits for them, and re-layouts, correlate(): jnp.concatenate([pieces[:, shift:block_count + shift] for shift in range(...  19.9 us
  transfers between devices with their start and end apart: 12, of which 5 were waited for; matrix products, arithmetic and copies ran while one was open for 3% of the time, Pallas kernels for 0%

commit v1 on v0

v1 whole, which is shorter than its diff:
```python
import functools

import jax
import jax.numpy as jnp
from jax import lax
from jax.experimental import pallas as pl
from jax.experimental.pallas import tpu as pltpu
from jax.sharding import PartitionSpec as P

TCH = 16
MAXOFF = 256
STOPS = 4
LANES = 128
UNROLL = 4

FLOOR_SHARE = 0.25
TEMPLATE_EPS = 1e-06


def normalized(template_rows):
    centred = template_rows - jnp.mean(template_rows, axis=-1, keepdims=True)
    energy = jnp.sum(centred * centred, axis=-1, keepdims=True)
    return centred / jnp.sqrt(energy + template_rows.shape[-1] * TEMPLATE_EPS)


def pack_kernel(half, capacity, dest, chan, length, where, rec, out, count, source):
    slot_count = dest.shape[0]
    blocks = rec.shape[1]
    member = where[0]

    def clear_count(i, c):
        count[i] = 0
        return c

    lax.fori_loop(0, count.shape[0], clear_count, 0)

    def clear_source(i, c):
        source[i] = -1
        return c

    lax.fori_loop(0, slot_count, clear_source, 0, unroll=8)

    def place(r, c):
        d = dest[r]
        used = d >= 0
        d = jnp.where(used, d, 2 * half)
        step = jnp.bitwise_xor(lax.rem(d, half), member)
        side = lax.div(d, half)
        rank = count[d]
        count[d] = rank + 1
        pos = (step * 2 + side) * capacity + rank
        source[jnp.where(used, pos, slot_count)] = r
        return c

    lax.fori_loop(0, slot_count, place, 0, unroll=4)
    flat = lax.broadcasted_iota(jnp.int32, (blocks, LANES), 0) * LANES + lax.broadcasted_iota(
        jnp.int32, (blocks, LANES), 1
    )
    last = blocks * LANES - 1

    def emit(pos, c):
        r = source[pos]
        used = r >= 0
        row = jnp.maximum(r, 0)
        limit = jnp.where(used, length[row], 0)
        tag = jnp.where(used, chan[row], -1).astype(jnp.float32)
        tile = jnp.where(flat < limit, rec[row], 0.0)
        out[pos] = jnp.where(flat == last, tag, tile)
        return c

    lax.fori_loop(0, slot_count, emit, 0, unroll=2)


def pack_rows(records, row_dest, row_chan, row_len, where, half):
    slot_count, sample_count = records.shape
    capacity = slot_count // (2 * half)
    smem = pl.BlockSpec(memory_space=pltpu.SMEM)
    vmem = pl.BlockSpec(memory_space=pltpu.VMEM)
    return pl.pallas_call(
        functools.partial(pack_kernel, half, capacity),
        out_shape=jax.ShapeDtypeStruct((slot_count, sample_count // LANES, LANES), jnp.float32),
        in_specs=[smem, smem, smem, smem, vmem],
        out_specs=vmem,
        scratch_shapes=[
            pltpu.SMEM((2 * half + 1,), jnp.int32),
            pltpu.SMEM((slot_count + 1,), jnp.int32),
        ],
        name="pack_rows",
    )(row_dest, row_chan, row_len, where, records.reshape(slot_count, -1, LANES))


def split(x):
    high = x.astype(jnp.bfloat16)
    return high, (x - high.astype(jnp.float32)).astype(jnp.bfloat16)


def segment_kernel(shape, tags, chans, offs, where, *refs):
    parts, capacity, blocks, taps, per_block, half_taps, lags = shape
    rows_in = refs[:parts]
    templ_in = refs[parts : parts + STOPS]
    keep, send = refs[parts + STOPS : parts + STOPS + 2]
    x_sc, s_sc, q_sc, inv_sc, h_sc, u_sc, acc, table, pair_id, pair_slot = refs[parts + STOPS + 2 :]
    side = where[0]
    core = where[1]
    slot_count = parts * capacity
    rows = slot_count * blocks
    stack_count = STOPS * per_block
    pair_count = stack_count * half_taps
    channel_count = table.shape[0] - 1
    stack_gain = (taps * TCH) ** 0.5 / TCH

    def clear(i, c):
        table[i] = -1
        return c

    lax.fori_loop(0, channel_count, clear, 0, unroll=8)

    def mark(i, c):
        tag = tags[side, i]
        table[jnp.where(tag >= 0, tag, channel_count)] = i
        return c

    lax.fori_loop(0, slot_count, mark, 0, unroll=4)

    def gather_pairs(i, filled):
        slot = table[chans[i]]
        pair_id[filled] = i
        pair_slot[filled] = slot
        return filled + jnp.where(slot >= 0, 1, 0)

    found = lax.fori_loop(0, pair_count, gather_pairs, 0, unroll=4)
    groups = lax.div(found + UNROLL - 1, UNROLL)

    def fill(i, c):
        pair_id[found + i] = stack_count * half_taps
        pair_slot[found + i] = 0
        return c

    lax.fori_loop(0, UNROLL, fill, 0)

    for s in range(STOPS):
        u_sc[s * per_block * half_taps * 2 : (s + 1) * per_block * half_taps * 2, :] = templ_in[s][
            : per_block * half_taps * 2, :
        ]
    u_sc[pair_count * 2 :, :] = jnp.zeros((8, LANES), jnp.float32)
    acc[...] = jnp.zeros_like(acc)
    part_rows = capacity * blocks
    for k in range(parts):
        x_sc[k * part_rows : (k + 1) * part_rows, :] = rows_in[k][side].reshape(part_rows, LANES)
    x_sc[rows:, :] = jnp.zeros((8, LANES), jnp.float32)

    row_i = lax.broadcasted_iota(jnp.int32, (LANES, LANES), 0)
    lane_i = lax.broadcasted_iota(jnp.int32, (LANES, LANES), 1)
    lower = row_i >= lane_i
    tail = lower.astype(jnp.float32).astype(jnp.bfloat16)
    ones = jnp.ones((LANES, LANES), jnp.bfloat16)
    sums = jnp.concatenate([tail, ones], axis=1)
    sums = jnp.concatenate([sums, sums], axis=0)
    chunk_slots = 8 if slot_count % 8 == 0 else 1
    chunk = chunk_slots * blocks

    def prepare(g, c):
        base = pl.multiple_of(g * chunk, chunk)
        x0 = x_sc[pl.ds(base, chunk), :]
        high0, low0 = split(x0)
        s_sc[:chunk, :] = jnp.dot(
            jnp.concatenate([high0, low0], axis=1), sums, preferred_element_type=jnp.float32
        )
        square_high, square_low = split(x0 * x0)
        q_sc[:chunk, :] = jnp.dot(
            jnp.concatenate([square_high, square_low], axis=1),
            sums,
            preferred_element_type=jnp.float32,
        )

        def window(ref):
            return (
                ref[:chunk, :LANES]
                + ref[pl.ds(1, chunk), LANES:]
                + (ref[pl.ds(2, chunk), LANES:] - ref[pl.ds(2, chunk), :LANES])
            )

        win_sum = window(s_sc)
        variance = window(q_sc) - win_sum * win_sum / taps
        inv = stack_gain / jnp.sqrt(jnp.maximum(variance, FLOOR_SHARE * taps))
        inv_sc[pl.ds(base, chunk), :] = inv
        high1, low1 = split(x_sc[pl.ds(base + 1, chunk), :])
        high2, low2 = split(x_sc[pl.ds(base + 2, chunk), :])
        slot0 = g * chunk_slots
        for j, (high, low) in enumerate(((high0, low0), (high1, low1), (high2, low2))):
            lanes = slice(j * LANES, (j + 1) * LANES)
            h_sc[pl.ds(slot0, chunk_slots), :blocks, lanes] = high.reshape(
                chunk_slots, blocks, LANES
            )
            h_sc[pl.ds(slot0, chunk_slots), blocks:, lanes] = low.reshape(
                chunk_slots, blocks, LANES
            )
        return c

    s_sc[chunk:, :] = jnp.zeros((8, 2 * LANES), jnp.float32)
    q_sc[chunk:, :] = jnp.zeros((8, 2 * LANES), jnp.float32)
    lax.fori_loop(0, slot_count // chunk_slots, prepare, 0)

    lane_b = lax.broadcasted_iota(jnp.int32, (blocks, LANES), 1)

    def circulant(row):
        return pltpu.roll(
            jnp.broadcast_to(u_sc[pl.ds(row, 1), :], (LANES, LANES)), 0, 1, stride=1, stride_axis=0
        )

    def pairs(g, c):
        for j in range(UNROLL):
            pair = pair_id[g * UNROLL + j]
            slot = pair_slot[g * UNROLL + j]
            first = circulant(pair * 2)
            second = circulant(pair * 2 + 1)
            zero = jnp.zeros_like(first)
            bands = []
            for band in (
                jnp.where(lower, first, zero),
                jnp.where(lower, second, first),
                jnp.where(lower, zero, second),
            ):
                bands.append(jnp.concatenate(split(band), axis=1))
            weights = jnp.concatenate(bands, axis=0)
            terms = jnp.dot(h_sc[slot], weights, preferred_element_type=jnp.float32)
            corr = (terms[:blocks, :LANES] + terms[:blocks, LANES:]) + (
                terms[blocks:, :LANES] + terms[blocks:, LANES:]
            )
            ratio = corr * inv_sc[pl.ds(pl.multiple_of(slot * blocks, blocks), blocks), :]
            off = offs[pair]
            by_lane = lax.rem(off, LANES)
            whole = off >= LANES
            here = pltpu.roll(ratio, lax.rem(LANES - by_lane, LANES), 1)
            after = pltpu.roll(here, blocks - 1, 0)
            beyond = pltpu.roll(here, blocks - 2, 0)
            moved = jnp.where(
                lane_b < LANES - by_lane,
                jnp.where(whole, after, here),
                jnp.where(whole, beyond, after),
            )
            stack = lax.div(pair, half_taps)
            acc[stack] += moved
        return c

    lax.fori_loop(0, groups, pairs, 0)

    half_lags = lags // 2 // LANES
    for which, ref in ((core, keep), (1 - core, send)):
        for b in range(half_lags):
            ref[:, b * LANES : (b + 1) * LANES] = jnp.where(
                which == 0, acc[:stack_count, b, :], acc[:stack_count, half_lags + b, :]
            )


def segment_stack(rows, templates, tags, chans, offs, where, shape):
    parts, capacity, blocks, taps, per_block, half_taps, lags = shape
    slot_count = parts * capacity
    stack_count = STOPS * per_block
    pair_count = stack_count * half_taps
    chunk = (8 if slot_count % 8 == 0 else 1) * blocks
    smem = pl.BlockSpec(memory_space=pltpu.SMEM)
    vmem = pl.BlockSpec(memory_space=pltpu.VMEM)
    out = jax.ShapeDtypeStruct((stack_count, lags // 2), jnp.float32)
    return pl.pallas_call(
        functools.partial(segment_kernel, shape),
        out_shape=(out, out),
        in_specs=[smem] * 4 + [vmem] * (parts + STOPS),
        out_specs=(vmem, vmem),
        scratch_shapes=[
            pltpu.VMEM((slot_count * blocks + 8, LANES), jnp.float32),
            pltpu.VMEM((chunk + 8, 2 * LANES), jnp.float32),
            pltpu.VMEM((chunk + 8, 2 * LANES), jnp.float32),
            pltpu.VMEM((slot_count * blocks, LANES), jnp.float32),
            pltpu.VMEM((slot_count, 2 * blocks, 3 * LANES), jnp.bfloat16),
            pltpu.VMEM((pair_count * 2 + 8, LANES), jnp.float32),
            pltpu.VMEM((stack_count + 1, blocks, LANES), jnp.float32),
            pltpu.SMEM((slot_count + 1,), jnp.int32),
            pltpu.SMEM((pair_count + UNROLL,), jnp.int32),
            pltpu.SMEM((pair_count + UNROLL,), jnp.int32),
        ],
        name="segment_stack",
    )(tags, chans, offs, where, *rows, *templates)


def local(records, row_dest, row_chan, row_len, templates, tmpl_chan, tmpl_off):
    slot_count, sample_count = records.shape
    size = lax.axis_size("tm")
    half = size // 2
    capacity = slot_count // size
    blocks = sample_count // LANES
    per_block, half_taps, taps = templates.shape
    lags = sample_count - taps - MAXOFF
    me = lax.axis_index("tm")
    side = me // half
    core = lax.axis_index("chan")
    pair_rows = per_block * half_taps

    unit = normalized(templates).reshape(pair_rows * 2, LANES)
    turned = jnp.concatenate([unit[:, :1], jnp.flip(unit[:, 1:], axis=1)], axis=1)
    maps = jnp.concatenate([tmpl_chan.reshape(1, -1), tmpl_off.reshape(1, -1)], axis=1)
    maps = jnp.pad(maps.astype(jnp.float32), ((0, 7), (0, LANES - 2 * pair_rows)))
    block = jnp.concatenate([turned, maps], axis=0)
    shifts = [s for s in range(STOPS)] + [half + s for s in range(STOPS)]
    visiting = {0: block}
    for shift in shifts:
        if shift % size not in visiting:
            visiting[shift % size] = lax.ppermute(
                block, "tm", [(i, (i + shift) % size) for i in range(size)]
            )
    own = [visiting[s % size] for s in range(STOPS)]
    other = [visiting[(half + s) % size] for s in range(STOPS)]

    where = jnp.stack([side, core]).astype(jnp.int32)
    packed = pack_rows(
        records, row_dest, row_chan, row_len, (me % half).reshape(1).astype(jnp.int32), half
    ).reshape(half, 2, capacity, blocks, LANES)
    rows = [packed[0]]
    for step in range(1, half):
        rows.append(
            lax.ppermute(
                packed[step], "tm", [(i, (i // half) * half + ((i % half) ^ step)) for i in range(size)]
            )
        )
    tags = jnp.stack([r[:, :, blocks - 1, LANES - 1] for r in rows], axis=1)
    tags = tags.reshape(2, half * capacity).astype(jnp.int32)
    shape = (half, capacity, blocks, taps, per_block, half_taps, lags)

    def stack_of(group, at):
        maps = jnp.stack([b[2 * pair_rows, : 2 * pair_rows] for b in group]).astype(jnp.int32)
        chans = maps[:, :pair_rows].reshape(-1)
        offs = jnp.pad(maps[:, pair_rows:].reshape(-1), (0, 1))
        return segment_stack(
            rows, group, tags, chans, offs, jnp.stack([at, core]).astype(jnp.int32), shape
        )

    swap = [(0, 1), (1, 0)]
    keep, send = stack_of(other, 1 - side)
    far = keep + lax.ppermute(send, "chan", swap)
    far = lax.ppermute(far, "tm", [(i, (i + half) % size) for i in range(size)])
    keep, send = stack_of(own, side)
    total = keep + lax.ppermute(send, "chan", swap) + far
    return total.reshape(1, STOPS, per_block, lags // 2)


def solution(mesh):
    in_specs = (
        P(("fam", "tm", "chan"), None),
        P(("fam", "tm", "chan")),
        P(("fam", "tm", "chan")),
        P(("fam", "tm", "chan")),
        P(("fam", "tm"), "chan", None),
        P(("fam", "tm"), "chan"),
        P(("fam", "tm"), "chan"),
    )
    out_specs = P(("fam", "tm"), None, None, "chan")
    return jax.shard_map(local, mesh=mesh, in_specs=in_specs, out_specs=out_specs, check_vma=False)
```

time: 967 us -> 88.5 us (0.09); the launches traced: 953 us -> 88.7 us
  local copies, waits for them, and re-layouts: 817 us -> 11.2 us
  Pallas kernels: 0 us -> 32.3 us
  matrix products: 27.3 us -> 0 us
  waiting for transfers between devices: 43.4 us -> 19.8 us
  between operations: 14.1 us -> 0.18 us
  starting transfers between devices: 30.4 us -> 20.4 us
    gather x896 -> x0, local copies, waits for them, and re-layouts: 712 us -> none
    pallas_call x0 -> x3, Pallas kernels: none -> 32.3 us  [the longest x2 28 us: segment_stack(): pl.pallas_call(functools.partial(segment_kernel, shape), out_shape=(out,...]
    dot_general x6 -> x0, matrix products: 27.3 us -> none  [the longest x4 25.4 us: correlate(): jnp.einsum('pbu,pru->pbr', windows, toeplitz, precision=highest)]
    unnamed x48 -> x27, local copies, waits for them, and re-layouts: 27.1 us -> 2.89 us
    reshape x19 -> x6, local copies, waits for them, and re-layouts: 24.9 us -> 2.04 us  [the longest x2 1.18 us: stack_of(): chans = maps[:, :pair_rows].reshape(-1)]
    concatenate x5 -> x2, local copies, waits for them, and re-layouts: 20.3 us -> 1.54 us  [local(): jnp.concatenate([tmpl_chan.reshape(1, -1), tmpl_off.reshape(1, -1)], axis=1)]
    slice x13 -> x15, local copies, waits for them, and re-layouts: 16 us -> 2.78 us  [the longest x1 1.47 us: local(): rows = [packed[0]]]
    ppermute x9 -> x13, waiting for transfers between devices: 32.7 us -> 19.8 us  [the longest x3 13.8 us: local(): lax.ppermute(packed[step], 'tm', [(i, i // half * half + (i % half ^ step...]
  transfers between devices with their start and end apart: 12 -> 13, of which waited for: 5 -> 5; matrix products, arithmetic and copies ran while one was open for 3% -> 10% of each run, Pallas kernels for 0% -> 19%
where the time goes in v1:
time: 88.5 us; the launch traced here: 88.7 us
  Pallas kernels  32.3 us (36%)
  starting transfers between devices  20.4 us (23%)
  waiting for transfers between devices  19.8 us (22%)
  local copies, waits for them, and re-layouts  11.2 us (13%)
  other arithmetic  4.96 us (6%)
    pallas_call x2, Pallas kernels, segment_stack(): pl.pallas_call(functools.partial(segment_kernel, shape), out_shape=(out,...  28 us
    ppermute x3, waiting for transfers between devices, local(): lax.ppermute(packed[step], 'tm', [(i, i // half * half + (i % half ^ step...  13.8 us
    ppermute x7, starting transfers between devices, local(): lax.ppermute(block, 'tm', [(i, (i + shift) % size) for i in range(size)])  12.9 us
    ppermute x1, waiting for transfers between devices, local(): far = lax.ppermute(far, 'tm', [(i, (i + half) % size) for i in range(size)])  4.88 us
    pallas_call x1, Pallas kernels, pack_rows(): pl.pallas_call(functools.partial(pack_kernel, half, capacity), out_shape=...  4.21 us
    ppermute x1, starting transfers between devices, local(): total = keep + lax.ppermute(send, 'chan', swap) + far  3.79 us
    ppermute x3, starting transfers between devices, local(): lax.ppermute(packed[step], 'tm', [(i, i // half * half + (i % half ^ step...  3.55 us
    unnamed x27, local copies, waits for them, and re-layouts  2.89 us
  transfers between devices with their start and end apart: 13, of which 5 were waited for; matrix products, arithmetic and copies ran while one was open for 10% of the time, Pallas kernels for 19%

profile of v1, /device:TPU:0, one launch (start us, length us, event | category | flops | bytes accessed | tf_op | source)
XLA Modules:
  0.0 88.7 jit_solution(13191093157394638026)
XLA Ops:
  0.0 0.8 reduce_sum.18
  0.9 0.9 %multiply_reduce_fusion = f32[4,8]{1,0:T(4,128)S(1)} fusion(f32[4,8,256]{2,1,0:T(8,128)} %param.11, f32[4,8]{1,0:T(4,128)S(1)} %broadcast_multiply_fusion), kind=kLoop, calls=%fused_computation.3 | loop fusion | flops 24544 | bytes 33024 | tf_op jit(solution)/shard_map/reduce_sum | solution.py:22
  1.8 0.8 subtract_divide_fusion
  2.6 0.1 slice.98
  2.7 0.1 rev.4
  2.8 0.8 concatenate.21
  3.5 0.8 concatenate.22
  4.3 0.1 add_convert_fusion
  4.4 0.1 select_maximum_fusion.refs_4_
  4.5 3.1 %collective-permute-start.4 = (f32[72,128]{1,0:T(8,128)S(1)}, f32[72,128]{1,0:T(8,128)S(1)}, u32[]{:S(2)}, u32[]{:S(2)}) collective-permute-start(f32[72,128]{1,0:T(8,128)S(1)} %select_maximum_fusion.refs_4_), channel_id=1, source_target_pairs={{0,4},{2,6},{4,8},{6,10},{8,12},{10,14},{12,0},{14,2},{1,5},{3,7},... | collective-permute-start | bytes 110600 | tf_op jit(solution)/shard_map/ppermute | solution.py:308
  7.6 2.6 %collective-permute-start.7 = (f32[72,128]{1,0:T(8,128)S(1)}, f32[72,128]{1,0:T(8,128)S(1)}, u32[]{:S(2)}, u32[]{:S(2)}) collective-permute-start(f32[72,128]{1,0:T(8,128)S(1)} %select_maximum_fusion.refs_4_), channel_id=1, source_target_pairs={{0,8},{2,10},{4,12},{6,14},{8,0},{10,2},{12,4},{14,6},{1,9},{3,11}... | collective-permute-start | bytes 110600 | tf_op jit(solution)/shard_map/ppermute | solution.py:308
  10.1 1.3 %collective-permute-start.8 = (f32[72,128]{1,0:T(8,128)S(1)}, f32[72,128]{1,0:T(8,128)S(1)}, u32[]{:S(2)}, u32[]{:S(2)}) collective-permute-start(f32[72,128]{1,0:T(8,128)S(1)} %select_maximum_fusion.refs_4_), channel_id=1, source_target_pairs={{0,10},{2,12},{4,14},{6,0},{8,2},{10,4},{12,6},{14,8},{1,11},{3,13... | collective-permute-start | bytes 110600 | tf_op jit(solution)/shard_map/ppermute | solution.py:308
  11.4 2.2 %collective-permute-start.9 = (f32[72,128]{1,0:T(8,128)S(1)}, f32[72,128]{1,0:T(8,128)S(1)}, u32[]{:S(2)}, u32[]{:S(2)}) collective-permute-start(f32[72,128]{1,0:T(8,128)S(1)} %select_maximum_fusion.refs_4_), channel_id=1, source_target_pairs={{0,12},{2,14},{4,0},{6,2},{8,4},{10,6},{12,8},{14,10},{1,13},{3,15... | collective-permute-start | bytes 110600 | tf_op jit(solution)/shard_map/ppermute | solution.py:308
  13.7 0.4 collective-permute-start.10
  14.0 2.8 %copy.14 = f32[12,8,32,128]{3,2,1,0:T(8,128)} copy(f32[12,8,32,128]{3,1,2,0:T(8,128)} %bitcast.27) | data formatting | bytes 3145728
  16.9 4.2 %pack_rows.1 = f32[96,32,128]{2,1,0:T(8,128)} custom-call(s32[96]{0:T(128)} %dest.1, s32[96]{0:T(128)} %chan.1, s32[96]{0:T(128)} %length.1, s32[1]{0:T(128)} %bitcast.where, f32[96,32,128]{2,1,0:T(8,128)} %bitcast.23), custom_call_target="tpu_custom_call" | custom-call | tf_op jit(solution)/shard_map/pack_rows/pallas_call | solution.py:79
  21.1 1.5 %fusion = (f32[24,32,128]{2,1,0:T(8,128)S(1)}, f32[24,32,128]{2,1,0:T(8,128)S(1)}, f32[24,32,128]{2,1,0:T(8,128)S(1)}, f32[24,32,128]{2,1,0:T(8,128)S(1)}) fusion(f32[96,32,128]{2,1,0:T(8,128)} %pack_rows.1), kind=kLoop, calls=%fused_computation.17 | loop fusion | bytes 3145728 | tf_op jit(solution)/shard_map/slice | solution.py:318
  22.6 0.3 slice_reduce_fusion.3
  22.9 0.6 pad_add_fusion.where
  23.5 0.6 pad_add_fusion.1.where
  24.1 0.9 collective-permute-start.5
  25.0 2.5 %collective-permute-start.3 = (f32[72,128]{1,0:T(8,128)S(1)}, f32[72,128]{1,0:T(8,128)S(1)}, u32[]{:S(2)}, u32[]{:S(2)}) collective-permute-start(f32[72,128]{1,0:T(8,128)S(1)} %select_maximum_fusion.refs_4_), channel_id=1, source_target_pairs={{0,2},{2,4},{4,6},{6,8},{8,10},{10,12},{12,14},{14,0},{1,3},{3,5},... | collective-permute-start | bytes 110600 | tf_op jit(solution)/shard_map/ppermute | solution.py:308
  27.4 0.6 collective-permute-start
  28.1 1.6 %collective-permute-start.1 = (f32[2,12,32,128]{3,2,1,0:T(8,128)S(1)}, f32[2,12,32,128]{3,2,1,0:T(8,128)S(1)}, u32[]{:S(2)}, u32[]{:S(2)}) collective-permute-start(f32[2,12,32,128]{3,2,1,0:T(8,128)S(1)} %bitcast.29), channel_id=1, source_target_pairs={{0,4},{2,6},{4,0},{6,2},{8,12},{10,14},{12,8},{14,10},{1,5},{3,7},... | collective-permute-start | bytes 1179656 | tf_op jit(solution)/shard_map/ppermute | solution.py:321
  29.7 1.4 %collective-permute-start.2 = (f32[2,12,32,128]{3,2,1,0:T(8,128)S(1)}, f32[2,12,32,128]{3,2,1,0:T(8,128)S(1)}, u32[]{:S(2)}, u32[]{:S(2)}) collective-permute-start(f32[2,12,32,128]{3,2,1,0:T(8,128)S(1)} %bitcast.28), channel_id=1, source_target_pairs={{0,6},{2,4},{4,2},{6,0},{8,14},{10,12},{12,10},{14,8},{1,7},{3,5},... | collective-permute-start | bytes 1179656 | tf_op jit(solution)/shard_map/ppermute | solution.py:321
  31.0 0.1 fusion.2
  31.1 0.1 reshape.89
  31.2 0.6 pad.13.offs
  31.8 0.6 reshape.88.chans
  32.4 7.0 %collective-permute-done.refs_1_ = f32[2,12,32,128]{3,2,1,0:T(8,128)S(1)} collective-permute-done((f32[2,12,32,128]{3,2,1,0:T(8,128)S(1)}, f32[2,12,32,128]{3,2,1,0:T(8,128)S(1)}, u32[]{:S(2)}, u32[]{:S(2)}) %collective-permute-start) | collective-permute-done | bytes 393248 | tf_op jit(solution)/shard_map/ppermute | solution.py:321
  39.4 0.3 slice_reduce_fusion.2
  39.7 0.4 collective-permute-done.1.refs_2_
  40.1 0.3 slice_reduce_fusion.1
  40.3 6.4 %collective-permute-done.2.refs_3_ = f32[2,12,32,128]{3,2,1,0:T(8,128)S(1)} collective-permute-done((f32[2,12,32,128]{3,2,1,0:T(8,128)S(1)}, f32[2,12,32,128]{3,2,1,0:T(8,128)S(1)}, u32[]{:S(2)}, u32[]{:S(2)}) %collective-permute-start.2) | collective-permute-done | bytes 393248 | tf_op jit(solution)/shard_map/ppermute | solution.py:321
  46.8 0.3 slice_reduce_fusion
  47.0 0.7 convert_element_type.25.tags
  47.8 15.7 %segment_stack.3 = (f32[16,1792]{1,0:T(8,128)}, f32[16,1792]{1,0:T(8,128)}) custom-call(s32[2,48]{1,0:T(2,128)} %convert_element_type.25.tags, s32[128]{0:T(128)} %reshape.88.chans, s32[129]{0:T(256)} %pad.13.offs, s32[2]{0:T(128)} %pad_add_fusion.1.where, f32[2,12,32,128]{3,2,1,0:T(8,128)} %bitcast.25, f32[2,12,32,128]{3,2,1,0:T(8,128)} %copy-done.1, ...), custom_call_target="tpu_custom_call" | custom-call | tf_op jit(solution)/shard_map/segment_stack/pallas_call | solution.py:265
  63.5 0.1 fusion.1
  63.6 0.1 reshape.87
  63.7 0.6 pad.12.offs
  64.3 0.6 reshape.86.chans
  64.9 12.4 %segment_stack.2 = (f32[16,1792]{1,0:T(8,128)}, f32[16,1792]{1,0:T(8,128)}) custom-call(s32[2,48]{1,0:T(2,128)} %convert_element_type.25.tags, s32[128]{0:T(128)} %reshape.86.chans, s32[129]{0:T(256)} %pad.12.offs, s32[2]{0:T(128)} %pad_add_fusion.where, f32[2,12,32,128]{3,2,1,0:T(8,128)} %bitcast.26, f32[2,12,32,128]{3,2,1,0:T(8,128)} %copy-done.1, ...), custom_call_target="tpu_custom_call" | custom-call | tf_op jit(solution)/shard_map/segment_stack/pallas_call | solution.py:265
  77.2 3.8 %collective-permute-start.6 = (f32[16,1792]{1,0:T(8,128)}, f32[16,1792]{1,0:T(8,128)S(1)}, u32[]{:S(2)}, u32[]{:S(2)}) collective-permute-start(f32[16,1792]{1,0:T(8,128)} %get-tuple-element.10), channel_id=1, source_target_pairs={{0,1},{1,0},{2,3},{3,2},{4,5},{5,4},{6,7},{7,6},{8,9},{9,8},{10,11... | collective-permute-start | bytes 344072 | tf_op jit(solution)/shard_map/ppermute | solution.py:342
  81.1 0.1 collective-permute-start.12
  81.1 1.1 %collective-permute-done.6 = f32[16,1792]{1,0:T(8,128)S(1)} collective-permute-done((f32[16,1792]{1,0:T(8,128)}, f32[16,1792]{1,0:T(8,128)S(1)}, u32[]{:S(2)}, u32[]{:S(2)}) %collective-permute-start.6) | collective-permute-done | bytes 114720 | tf_op jit(solution)/shard_map/ppermute | solution.py:342
  82.2 4.9 %collective-permute-done.12 = f32[16,1792]{1,0:T(8,128)S(1)} collective-permute-done((f32[16,1792]{1,0:T(8,128)S(1)}, f32[16,1792]{1,0:T(8,128)S(1)}, u32[]{:S(2)}, u32[]{:S(2)}) %collective-permute-start.12) | collective-permute-done | bytes 114720 | tf_op jit(solution)/shard_map/ppermute | solution.py:340
  87.1 0.9 %add_add_fusion = f32[16,1792]{1,0:T(8,128)S(1)} fusion(f32[16,1792]{1,0:T(8,128)S(1)} %collective-permute-done.12, f32[16,1792]{1,0:T(8,128)} %get-tuple-element.9, f32[16,1792]{1,0:T(8,128)S(1)} %collective-permute-done.6), kind=kLoop, calls=%fused_computation | loop fusion | flops 57344 | bytes 458752 | tf_op jit(solution)/shard_map/add | solution.py:342
  88.0 0.7 reshape.90
  (49 shorter events, 0.2 us)
Async XLA Ops:
  4.5 20.5 %copy-start.4 = (f32[72,128]{1,0:T(8,128)}, f32[72,128]{1,0:T(8,128)S(1)}, u32[]{:S(2)}) copy-start(f32[72,128]{1,0:T(8,128)S(1)} %select_maximum_fusion.refs_4_) | copy-start | bytes 110596
  4.5 25.2 %collective-permute-start.4 = (f32[72,128]{1,0:T(8,128)S(1)}, f32[72,128]{1,0:T(8,128)S(1)}, u32[]{:S(2)}, u32[]{:S(2)}) collective-permute-start(f32[72,128]{1,0:T(8,128)S(1)} %select_maximum_fusion.refs_4_), channel_id=1, source_target_pairs={{0,4},{2,6},{4,8},{6,10},{8,12},{10,14},{12,0},{14,2},{1,5},{3,7},... | collective-permute-start | bytes 110600 | tf_op jit(solution)/shard_map/ppermute | solution.py:308
  7.6 16.5 %collective-permute-start.7 = (f32[72,128]{1,0:T(8,128)S(1)}, f32[72,128]{1,0:T(8,128)S(1)}, u32[]{:S(2)}, u32[]{:S(2)}) collective-permute-start(f32[72,128]{1,0:T(8,128)S(1)} %select_maximum_fusion.refs_4_), channel_id=1, source_target_pairs={{0,8},{2,10},{4,12},{6,14},{8,0},{10,2},{12,4},{14,6},{1,9},{3,11}... | collective-permute-start | bytes 110600 | tf_op jit(solution)/shard_map/ppermute | solution.py:308
  10.1 14.8 %collective-permute-start.8 = (f32[72,128]{1,0:T(8,128)S(1)}, f32[72,128]{1,0:T(8,128)S(1)}, u32[]{:S(2)}, u32[]{:S(2)}) collective-permute-start(f32[72,128]{1,0:T(8,128)S(1)} %select_maximum_fusion.refs_4_), channel_id=1, source_target_pairs={{0,10},{2,12},{4,14},{6,0},{8,2},{10,4},{12,6},{14,8},{1,11},{3,13... | collective-permute-start | bytes 110600 | tf_op jit(solution)/shard_map/ppermute | solution.py:308
  11.4 16.0 %collective-permute-start.9 = (f32[72,128]{1,0:T(8,128)S(1)}, f32[72,128]{1,0:T(8,128)S(1)}, u32[]{:S(2)}, u32[]{:S(2)}) collective-permute-start(f32[72,128]{1,0:T(8,128)S(1)} %select_maximum_fusion.refs_4_), channel_id=1, source_target_pairs={{0,12},{2,14},{4,0},{6,2},{8,4},{10,6},{12,8},{14,10},{1,13},{3,15... | collective-permute-start | bytes 110600 | tf_op jit(solution)/shard_map/ppermute | solution.py:308
  13.7 14.4 %collective-permute-start.10 = (f32[72,128]{1,0:T(8,128)S(1)}, f32[72,128]{1,0:T(8,128)S(1)}, u32[]{:S(2)}, u32[]{:S(2)}) collective-permute-start(f32[72,128]{1,0:T(8,128)S(1)} %select_maximum_fusion.refs_4_), channel_id=1, source_target_pairs={{0,14},{2,0},{4,2},{6,4},{8,6},{10,8},{12,10},{14,12},{1,15},{3,1}... | collective-permute-start | bytes 110600 | tf_op jit(solution)/shard_map/ppermute | solution.py:308
  22.6 25.1 %copy-start = (f32[24,32,128]{2,1,0:T(8,128)}, f32[24,32,128]{2,1,0:T(8,128)S(1)}, u32[]{:S(2)}) copy-start(f32[24,32,128]{2,1,0:T(8,128)S(1)} %get-tuple-element.13) | copy-start | bytes 1179652
  24.1 23.6 %copy-start.7 = (f32[72,128]{1,0:T(8,128)}, f32[72,128]{1,0:T(8,128)S(1)}, u32[]{:S(2)}) copy-start(f32[72,128]{1,0:T(8,128)S(1)} %collective-permute-done.7.refs_4_) | copy-start | bytes 110596
  24.1 8.3 %collective-permute-start.5 = (f32[72,128]{1,0:T(8,128)S(1)}, f32[72,128]{1,0:T(8,128)S(1)}, u32[]{:S(2)}, u32[]{:S(2)}) collective-permute-start(f32[72,128]{1,0:T(8,128)S(1)} %select_maximum_fusion.refs_4_), channel_id=1, source_target_pairs={{0,6},{2,8},{4,10},{6,12},{8,14},{10,0},{12,2},{14,4},{1,7},{3,9},... | collective-permute-start | bytes 110600 | tf_op jit(solution)/shard_map/ppermute | solution.py:308
  25.0 22.8 %copy-start.8 = (f32[72,128]{1,0:T(8,128)}, f32[72,128]{1,0:T(8,128)S(1)}, u32[]{:S(2)}) copy-start(f32[72,128]{1,0:T(8,128)S(1)} %collective-permute-done.8.refs_5_) | copy-start | bytes 110596
  25.0 7.4 %collective-permute-start.3 = (f32[72,128]{1,0:T(8,128)S(1)}, f32[72,128]{1,0:T(8,128)S(1)}, u32[]{:S(2)}, u32[]{:S(2)}) collective-permute-start(f32[72,128]{1,0:T(8,128)S(1)} %select_maximum_fusion.refs_4_), channel_id=1, source_target_pairs={{0,2},{2,4},{4,6},{6,8},{8,10},{10,12},{12,14},{14,0},{1,3},{3,5},... | collective-permute-start | bytes 110600 | tf_op jit(solution)/shard_map/ppermute | solution.py:308
  27.4 20.3 %copy-start.9 = (f32[72,128]{1,0:T(8,128)}, f32[72,128]{1,0:T(8,128)S(1)}, u32[]{:S(2)}) copy-start(f32[72,128]{1,0:T(8,128)S(1)} %collective-permute-done.9.refs_6_) | copy-start | bytes 110596
  27.4 11.9 %collective-permute-start = (f32[2,12,32,128]{3,2,1,0:T(8,128)S(1)}, f32[2,12,32,128]{3,2,1,0:T(8,128)S(1)}, u32[]{:S(2)}, u32[]{:S(2)}) collective-permute-start(f32[2,12,32,128]{3,2,1,0:T(8,128)S(1)} %bitcast.30), channel_id=1, source_target_pairs={{0,2},{2,0},{4,6},{6,4},{8,10},{10,8},{12,14},{14,12},{1,3},{3,1},... | collective-permute-start | bytes 1179656 | tf_op jit(solution)/shard_map/ppermute | solution.py:321
  28.1 19.7 %copy-start.10 = (f32[72,128]{1,0:T(8,128)}, f32[72,128]{1,0:T(8,128)S(1)}, u32[]{:S(2)}) copy-start(f32[72,128]{1,0:T(8,128)S(1)} %collective-permute-done.10.refs_7_) | copy-start | bytes 110596
  28.1 12.0 %collective-permute-start.1 = (f32[2,12,32,128]{3,2,1,0:T(8,128)S(1)}, f32[2,12,32,128]{3,2,1,0:T(8,128)S(1)}, u32[]{:S(2)}, u32[]{:S(2)}) collective-permute-start(f32[2,12,32,128]{3,2,1,0:T(8,128)S(1)} %bitcast.29), channel_id=1, source_target_pairs={{0,4},{2,6},{4,0},{6,2},{8,12},{10,14},{12,8},{14,10},{1,5},{3,7},... | collective-permute-start | bytes 1179656 | tf_op jit(solution)/shard_map/ppermute | solution.py:321
  29.7 35.2 %copy-start.6 = (f32[72,128]{1,0:T(8,128)}, f32[72,128]{1,0:T(8,128)S(1)}, u32[]{:S(2)}) copy-start(f32[72,128]{1,0:T(8,128)S(1)} %collective-permute-done.4.refs_6_) | copy-start | bytes 110596
  29.7 17.1 %collective-permute-start.2 = (f32[2,12,32,128]{3,2,1,0:T(8,128)S(1)}, f32[2,12,32,128]{3,2,1,0:T(8,128)S(1)}, u32[]{:S(2)}, u32[]{:S(2)}) collective-permute-start(f32[2,12,32,128]{3,2,1,0:T(8,128)S(1)} %bitcast.28), channel_id=1, source_target_pairs={{0,6},{2,4},{4,2},{6,0},{8,14},{10,12},{12,10},{14,8},{1,7},{3,5},... | collective-permute-start | bytes 1179656 | tf_op jit(solution)/shard_map/ppermute | solution.py:321
  32.4 32.5 %copy-start.11 = (f32[72,128]{1,0:T(8,128)}, f32[72,128]{1,0:T(8,128)S(1)}, u32[]{:S(2)}) copy-start(f32[72,128]{1,0:T(8,128)S(1)} %collective-permute-done.5.refs_7_) | copy-start | bytes 110596
  32.4 32.5 %copy-start.12 = (f32[72,128]{1,0:T(8,128)}, f32[72,128]{1,0:T(8,128)S(1)}, u32[]{:S(2)}) copy-start(f32[72,128]{1,0:T(8,128)S(1)} %collective-permute-done.3.refs_5_) | copy-start | bytes 110596
  39.4 8.4 %copy-start.1 = (f32[2,12,32,128]{3,2,1,0:T(8,128)}, f32[2,12,32,128]{3,2,1,0:T(8,128)S(1)}, u32[]{:S(2)}) copy-start(f32[2,12,32,128]{3,2,1,0:T(8,128)S(1)} %collective-permute-done.refs_1_) | copy-start | bytes 1179652
  40.1 7.7 %copy-start.2 = (f32[2,12,32,128]{3,2,1,0:T(8,128)}, f32[2,12,32,128]{3,2,1,0:T(8,128)S(1)}, u32[]{:S(2)}) copy-start(f32[2,12,32,128]{3,2,1,0:T(8,128)S(1)} %collective-permute-done.1.refs_2_) | copy-start | bytes 1179652
  46.7 1.0 %copy-start.3 = (f32[2,12,32,128]{3,2,1,0:T(8,128)}, f32[2,12,32,128]{3,2,1,0:T(8,128)S(1)}, u32[]{:S(2)}) copy-start(f32[2,12,32,128]{3,2,1,0:T(8,128)S(1)} %collective-permute-done.2.refs_3_) | copy-start | bytes 1179652
  63.4 17.6 %copy-start.5 = (f32[16,1792]{1,0:T(8,128)S(1)}, f32[16,1792]{1,0:T(8,128)}, u32[]{:S(2)}) copy-start(f32[16,1792]{1,0:T(8,128)} %get-tuple-element.11) | copy-start | bytes 344068
  63.4 17.6 %collective-permute-start.11 = (f32[16,1792]{1,0:T(8,128)}, f32[16,1792]{1,0:T(8,128)S(1)}, u32[]{:S(2)}, u32[]{:S(2)}) collective-permute-start(f32[16,1792]{1,0:T(8,128)} %get-tuple-element.12), channel_id=1, source_target_pairs={{0,1},{1,0},{2,3},{3,2},{4,5},{5,4},{6,7},{7,6},{8,9},{9,8},{10,11... | collective-permute-start | bytes 344072 | tf_op jit(solution)/shard_map/ppermute | solution.py:339
  77.2 5.0 %collective-permute-start.6 = (f32[16,1792]{1,0:T(8,128)}, f32[16,1792]{1,0:T(8,128)S(1)}, u32[]{:S(2)}, u32[]{:S(2)}) collective-permute-start(f32[16,1792]{1,0:T(8,128)} %get-tuple-element.10), channel_id=1, source_target_pairs={{0,1},{1,0},{2,3},{3,2},{4,5},{5,4},{6,7},{7,6},{8,9},{9,8},{10,11... | collective-permute-start | bytes 344072 | tf_op jit(solution)/shard_map/ppermute | solution.py:342
  81.1 6.0 %collective-permute-start.12 = (f32[16,1792]{1,0:T(8,128)S(1)}, f32[16,1792]{1,0:T(8,128)S(1)}, u32[]{:S(2)}, u32[]{:S(2)}) collective-permute-start(f32[16,1792]{1,0:T(8,128)S(1)} %add.35), channel_id=1, source_target_pairs={{0,8},{2,10},{4,12},{6,14},{8,0},{10,2},{12,4},{14,6},{1,9},{3,11}... | collective-permute-start | bytes 344072 | tf_op jit(solution)/shard_map/ppermute | solution.py:340

commit v2 on v1

v2 whole, which is shorter than its diff:
```python
import functools

import jax
import jax.numpy as jnp
from jax import lax
from jax.experimental import pallas as pl
from jax.experimental.pallas import tpu as pltpu
from jax.sharding import PartitionSpec as P


TCH = 16
MAXOFF = 256
STOPS = 4
LANES = 128
SUB = 8
UNROLL = 16
PAIR_BITS = 8
SLOT_BITS = 6
PAIR_STEP = 1 << PAIR_BITS
SLOT_STEP = 1 << SLOT_BITS

FLOOR_SHARE = 0.25
TEMPLATE_EPS = 1e-06

SMEM = pl.BlockSpec(memory_space=pltpu.SMEM)
VMEM = pl.BlockSpec(memory_space=pltpu.VMEM)


def split(x):
    high = x.astype(jnp.bfloat16)
    return high, (x - high.astype(jnp.float32)).astype(jnp.bfloat16)


def pack_kernel(half, capacity, dest, chan, length, where, rec, *refs):
    outs = refs[: 2 * half]
    count, source, rows = refs[2 * half :]
    slot_count = dest.shape[0]
    blocks = rec.shape[1] // LANES
    member, home = where[0], where[1]

    def clear_count(i, c):
        count[i] = 0
        return c

    lax.fori_loop(0, count.shape[0], clear_count, 0)

    def clear_source(i, c):
        source[i] = -1
        return c

    lax.fori_loop(0, slot_count, clear_source, 0, unroll=8)

    def place(r, c):
        d = dest[r]
        used = d >= 0
        d = jnp.where(used, d, 2 * half)
        side = jnp.where(d >= half, 1, 0)
        step = jnp.bitwise_xor(d - side * half, member)
        rank = count[d]
        count[d] = rank + 1
        pos = (jnp.where(side == home, half, 0) + step) * capacity + rank
        source[jnp.where(used, pos, slot_count)] = r
        return c

    lax.fori_loop(0, slot_count, place, 0, unroll=8)

    def reform(g, c):
        first = pl.multiple_of(g * SUB, SUB)
        for b in range(blocks):
            rows[pl.ds(first * blocks + b, SUB, stride=blocks), :] = rec[
                pl.ds(first, SUB), b * LANES : (b + 1) * LANES
            ]
        return c

    lax.fori_loop(0, slot_count // SUB, reform, 0)
    flat = lax.broadcasted_iota(jnp.int32, (blocks, LANES), 0) * LANES + lax.broadcasted_iota(
        jnp.int32, (blocks, LANES), 1
    )
    last = blocks * LANES - 1
    for group, out in enumerate(outs):

        def emit(i, c, group=group, out=out):
            r = source[group * capacity + i]
            used = r >= 0
            row = jnp.maximum(r, 0)
            limit = jnp.where(used, length[row], 0)
            tag = jnp.where(used, chan[row], -1).astype(jnp.float32)
            tile = rows[pl.ds(pl.multiple_of(row * blocks, blocks), blocks), :]
            tile = jnp.where(flat < limit, tile, 0.0)
            out[i] = jnp.where(flat == last, tag, tile)
            return c

        lax.fori_loop(0, capacity, emit, 0, unroll=4 if capacity % 4 == 0 else True)


def pack_rows(records, row_dest, row_chan, row_len, where, half):
    slot_count, sample_count = records.shape
    capacity = slot_count // (2 * half)
    blocks = sample_count // LANES
    out = jax.ShapeDtypeStruct((capacity, blocks, LANES), jnp.float32)
    outs = pl.pallas_call(
        functools.partial(pack_kernel, half, capacity),
        out_shape=[out] * (2 * half),
        in_specs=[SMEM] * 4 + [VMEM],
        out_specs=[VMEM] * (2 * half),
        scratch_shapes=[
            pltpu.SMEM((2 * half + 1,), jnp.int32),
            pltpu.SMEM((slot_count + 1,), jnp.int32),
            pltpu.VMEM((slot_count * blocks, LANES), jnp.float32),
        ],
        name="pack_rows",
    )(row_dest, row_chan, row_len, where, records)
    return outs[:half], outs[half:]


def unit_kernel(templ, chan, off, out):
    per_block, half_taps, taps = templ.shape
    pair_rows = per_block * half_taps
    x = templ[...].reshape(pair_rows, taps)
    centred = x - jnp.mean(x, axis=-1, keepdims=True)
    energy = jnp.sum(centred * centred, axis=-1, keepdims=True)
    unit = centred / jnp.sqrt(energy + taps * TEMPLATE_EPS)
    high, rest = split(unit)
    middle, low = split(unit - high.astype(jnp.float32))
    del rest
    row_i = lax.broadcasted_iota(jnp.int32, (LANES, LANES), 0)
    lane_i = lax.broadcasted_iota(jnp.int32, (LANES, LANES), 1)
    turn = jnp.where(row_i == lax.rem(LANES - lane_i, LANES), 1.0, 0.0).astype(jnp.bfloat16)
    for j in range(taps // LANES):
        lanes = slice(j * LANES, (j + 1) * LANES)
        pieces = [
            jnp.dot(part[:, lanes], turn, preferred_element_type=jnp.float32)
            for part in (high, middle, low)
        ]
        out[j * pair_rows : (j + 1) * pair_rows, :] = pieces[0] + (pieces[1] + pieces[2])
    base = (taps // LANES) * pair_rows
    out[base:, :] = jnp.zeros((out.shape[0] - base, LANES), jnp.float32)
    row = jnp.zeros((1, LANES), jnp.float32)
    for which, ref in enumerate((chan, off)):
        for k in range(per_block):
            piece = ref[k : k + 1, :].astype(jnp.float32)
            first = which * pair_rows + k * half_taps
            row += jnp.pad(piece, ((0, 0), (first, LANES - first - half_taps)))
    out[base : base + 1, :] = row


def unit_block(templates, tmpl_chan, tmpl_off):
    per_block, half_taps, taps = templates.shape
    rows = (taps // LANES) * per_block * half_taps + SUB
    return pl.pallas_call(
        unit_kernel,
        out_shape=jax.ShapeDtypeStruct((rows, LANES), jnp.float32),
        in_specs=[VMEM] * 3,
        out_specs=VMEM,
        name="unit_block",
    )(templates, tmpl_chan, tmpl_off)


def segment_kernel(shape, where, *refs):
    parts, capacity, blocks, taps, per_block, half_taps, lags = shape
    rows_in = refs[:parts]
    templ_in = refs[parts : 2 * parts]
    keep, send = refs[2 * parts : 2 * parts + 2]
    (
        x_sc, s_sc, q_sc, inv_sc, h_sc, u_sc, acc, code_v, code_s, listed, sem,
    ) = refs[2 * parts + 2 :]
    segment, member, home, core = where[0], where[1], where[2], where[3]
    size = 2 * parts
    slot_count = parts * capacity
    rows = slot_count * blocks
    pair_rows = per_block * half_taps
    pair_count = STOPS * pair_rows
    block_rows = u_sc.shape[1]
    stack_gain = (taps * TCH) ** 0.5 / TCH

    part_rows = capacity * blocks
    for k in range(parts):
        x_sc[k * part_rows : (k + 1) * part_rows, :] = rows_in[k][...].reshape(part_rows, LANES)
        index = jnp.bitwise_xor(member, k)
        u_sc[home * parts + index] = templ_in[k][:block_rows, :]
        u_sc[(1 - home) * parts + index] = templ_in[k][block_rows:, :]
    x_sc[rows:, :] = jnp.zeros((SUB, LANES), jnp.float32)
    lane_p = lax.broadcasted_iota(jnp.int32, (1, LANES), 1)
    chan_of = jnp.zeros((1, LANES), jnp.float32)
    off_of = jnp.zeros((1, LANES), jnp.float32)
    for s in range(STOPS):
        block = lax.rem(segment - s + size, size)
        maps = u_sc[block, block_rows - SUB : block_rows, :][:1]
        here = lax.div(lane_p, pair_rows) == s
        chan_of = jnp.where(here, pltpu.roll(maps, (s * pair_rows) % LANES, 1), chan_of)
        off_of = jnp.where(here, pltpu.roll(maps, ((s - 1) * pair_rows) % LANES, 1), off_of)
    tags = x_sc[pl.ds(blocks - 1, slot_count, stride=blocks), :][:, LANES - 1 :]
    match = (tags == chan_of).astype(jnp.float32)
    slots = lax.broadcasted_iota(jnp.int32, (slot_count, LANES), 0).astype(jnp.float32)
    slot_of = jnp.sum(match * slots, axis=0, keepdims=True)
    held = jnp.sum(match, axis=0, keepdims=True)
    code = lane_p.astype(jnp.float32) + slot_of * PAIR_STEP + off_of * (PAIR_STEP * SLOT_STEP)
    code = jnp.where(held > 0, code, -1.0).astype(jnp.int32)
    code_v[...] = jnp.broadcast_to(code, (SUB, LANES))
    copy = pltpu.make_async_copy(code_v, code_s, sem)
    copy.start()
    acc[...] = jnp.zeros_like(acc)

    row_i = lax.broadcasted_iota(jnp.int32, (LANES, LANES), 0)
    lane_i = lax.broadcasted_iota(jnp.int32, (LANES, LANES), 1)
    lower = row_i >= lane_i
    tail = lower.astype(jnp.float32).astype(jnp.bfloat16)
    ones = jnp.ones((LANES, LANES), jnp.bfloat16)
    sums = jnp.concatenate([tail, ones], axis=1)
    sums = jnp.concatenate([sums, sums], axis=0)
    chunk_slots = SUB if slot_count % SUB == 0 else 1
    chunk = chunk_slots * blocks

    def prepare(g, c):
        base = pl.multiple_of(g * chunk, chunk)
        x0 = x_sc[pl.ds(base, chunk), :]
        high0, low0 = split(x0)
        s_sc[:chunk, :] = jnp.dot(
            jnp.concatenate([high0, low0], axis=1), sums, preferred_element_type=jnp.float32
        )
        square_high, square_low = split(x0 * x0)
        q_sc[:chunk, :] = jnp.dot(
            jnp.concatenate([square_high, square_low], axis=1),
            sums,
            preferred_element_type=jnp.float32,
        )

        def window(ref):
            return (
                ref[:chunk, :LANES]
                + ref[pl.ds(1, chunk), LANES:]
                + (ref[pl.ds(2, chunk), LANES:] - ref[pl.ds(2, chunk), :LANES])
            )

        win_sum = window(s_sc)
        variance = window(q_sc) - win_sum * win_sum / taps
        inv = stack_gain / jnp.sqrt(jnp.maximum(variance, FLOOR_SHARE * taps))
        inv_sc[pl.ds(base, chunk), :] = inv
        high1, low1 = split(x_sc[pl.ds(base + 1, chunk), :])
        high2, low2 = split(x_sc[pl.ds(base + 2, chunk), :])
        slot0 = g * chunk_slots
        for j, (high, low) in enumerate(((high0, low0), (high1, low1), (high2, low2))):
            lanes = slice(j * LANES, (j + 1) * LANES)
            h_sc[pl.ds(slot0, chunk_slots), :blocks, lanes] = high.reshape(
                chunk_slots, blocks, LANES
            )
            h_sc[pl.ds(slot0, chunk_slots), blocks:, lanes] = low.reshape(
                chunk_slots, blocks, LANES
            )
        return c

    s_sc[chunk:, :] = jnp.zeros((SUB, 2 * LANES), jnp.float32)
    q_sc[chunk:, :] = jnp.zeros((SUB, 2 * LANES), jnp.float32)
    lax.fori_loop(0, slot_count // chunk_slots, prepare, 0)

    copy.wait()

    def gather_pairs(i, filled):
        value = code_s[0, i]
        listed[filled] = value
        return filled + jnp.where(value >= 0, 1, 0)

    filled = lax.fori_loop(0, pair_count, gather_pairs, 0, unroll=16)
    groups = lax.div(filled + UNROLL - 1, UNROLL)
    for i in range(UNROLL):
        listed[filled + i] = pair_count

    lane_b = lax.broadcasted_iota(jnp.int32, (blocks, LANES), 1)
    low_mask = tail > 0
    zero = jnp.zeros((LANES, LANES), jnp.bfloat16)

    def pairs(g, c):
        for j in range(UNROLL):
            value = listed[g * UNROLL + j]
            pair = jnp.bitwise_and(value, PAIR_STEP - 1)
            slot = jnp.bitwise_and(lax.shift_right_logical(value, PAIR_BITS), SLOT_STEP - 1)
            off = lax.shift_right_logical(value, PAIR_BITS + SLOT_BITS)
            stop = lax.div(pair, pair_rows)
            block = lax.rem(segment - stop + size, size)
            inner = pair - stop * pair_rows

            def circulant(row):
                return pltpu.roll(
                    jnp.broadcast_to(u_sc[block, pl.ds(row, 1), :], (LANES, LANES)),
                    0,
                    1,
                    stride=1,
                    stride_axis=0,
                )

            first = split(circulant(inner))
            second = split(circulant(inner + pair_rows))
            bands = [
                jnp.concatenate([jnp.where(low_mask, x, zero) for x in first], axis=1),
                jnp.concatenate(
                    [jnp.where(low_mask, y, x) for x, y in zip(first, second)], axis=1
                ),
                jnp.concatenate([jnp.where(low_mask, zero, y) for y in second], axis=1),
            ]
            weights = jnp.concatenate(bands, axis=0)
            terms = jnp.dot(h_sc[slot], weights, preferred_element_type=jnp.float32)
            corr = (terms[:blocks, :LANES] + terms[:blocks, LANES:]) + (
                terms[blocks:, :LANES] + terms[blocks:, LANES:]
            )
            ratio = corr * inv_sc[pl.ds(pl.multiple_of(slot * blocks, blocks), blocks), :]
            by_lane = jnp.bitwise_and(off, LANES - 1)
            whole = off >= LANES
            here = pltpu.roll(ratio, lax.rem(LANES - by_lane, LANES), 1)
            after = pltpu.roll(here, blocks - 1, 0)
            beyond = pltpu.roll(here, blocks - 2, 0)
            moved = jnp.where(
                lane_b < LANES - by_lane,
                jnp.where(whole, after, here),
                jnp.where(whole, beyond, after),
            )
            acc[lax.div(pair, half_taps)] += moved
        return c

    lax.fori_loop(0, groups, pairs, 0)

    half_lags = lags // 2 // LANES
    for which, ref in ((core, keep), (1 - core, send)):
        for s in range(STOPS):
            stacks = slice(s * per_block, (s + 1) * per_block)
            for b in range(half_lags):
                ref[s, :, b * LANES : (b + 1) * LANES] = jnp.where(
                    which == 0, acc[stacks, b, :], acc[stacks, half_lags + b, :]
                )


def segment_stack(rows, templates, where, shape):
    parts, capacity, blocks, _, per_block, half_taps, lags = shape
    slot_count = parts * capacity
    stack_count = STOPS * per_block
    pair_count = stack_count * half_taps
    chunk = (SUB if slot_count % SUB == 0 else 1) * blocks
    block_rows = templates[0].shape[0] // 2
    out = jax.ShapeDtypeStruct((STOPS, per_block, lags // 2), jnp.float32)
    return pl.pallas_call(
        functools.partial(segment_kernel, shape),
        out_shape=(out, out),
        in_specs=[SMEM] + [VMEM] * (2 * parts),
        out_specs=(VMEM, VMEM),
        scratch_shapes=[
            pltpu.VMEM((slot_count * blocks + SUB, LANES), jnp.float32),
            pltpu.VMEM((chunk + SUB, 2 * LANES), jnp.float32),
            pltpu.VMEM((chunk + SUB, 2 * LANES), jnp.float32),
            pltpu.VMEM((slot_count * blocks, LANES), jnp.float32),
            pltpu.VMEM((slot_count, 2 * blocks, 3 * LANES), jnp.bfloat16),
            pltpu.VMEM((2 * parts, block_rows, LANES), jnp.float32),
            pltpu.VMEM((stack_count + 1, blocks, LANES), jnp.float32),
            pltpu.VMEM((SUB, LANES), jnp.int32),
            pltpu.SMEM((SUB, LANES), jnp.int32),
            pltpu.SMEM((pair_count + UNROLL,), jnp.int32),
            pltpu.SemaphoreType.DMA,
        ],
        name="segment_stack",
    )(where, *rows, *templates)


def local(records, row_dest, row_chan, row_len, templates, tmpl_chan, tmpl_off):
    slot_count, sample_count = records.shape
    size = lax.axis_size("tm")
    half = size // 2
    capacity = slot_count // size
    per_block, half_taps, taps = templates.shape
    lags = sample_count - taps - MAXOFF
    me = lax.axis_index("tm")
    core = lax.axis_index("chan")
    home, member = me // half, me % half
    across = [(i, (i + half) % size) for i in range(size)]
    swap = [(0, 1), (1, 0)]
    shape = (half, capacity, sample_count // LANES, taps, per_block, half_taps, lags)

    def within(x, step):
        return lax.ppermute(
            x, "tm", [(i, (i // half) * half + ((i % half) ^ step)) for i in range(size)]
        )

    far_out, own_out = pack_rows(
        records, row_dest, row_chan, row_len, jnp.stack([member, home]).astype(jnp.int32), half
    )
    far_rows = [far_out[0]] + [within(far_out[k], k) for k in range(1, half)]
    templates, own_out = lax.optimization_barrier((templates, own_out))
    block = unit_block(templates, tmpl_chan, tmpl_off)
    pair = jnp.concatenate([block, lax.ppermute(block, "tm", across)], axis=0)
    pair, own_out = lax.optimization_barrier((pair, own_out))
    blocks = [pair] + [within(pair, k) for k in range(1, half)]
    own_rows = [own_out[0]] + [within(own_out[k], k) for k in range(1, half)]

    def stack_of(rows, segment):
        where = jnp.stack([segment, member, home, core]).astype(jnp.int32)
        return segment_stack(rows, blocks, where, shape)

    keep, send = stack_of(far_rows, (me + half) % size)
    far = keep + lax.ppermute(send, "chan", swap)
    far, *own_rows = lax.optimization_barrier((far, *own_rows))
    far = lax.ppermute(far, "tm", across)
    keep, send = stack_of(own_rows, me)
    total = keep + lax.ppermute(send, "chan", swap) + far
    return total[None]


def solution(mesh):
    in_specs = (
        P(("fam", "tm", "chan"), None),
        P(("fam", "tm", "chan")),
        P(("fam", "tm", "chan")),
        P(("fam", "tm", "chan")),
        P(("fam", "tm"), "chan", None),
        P(("fam", "tm"), "chan"),
        P(("fam", "tm"), "chan"),
    )
    out_specs = P(("fam", "tm"), None, None, "chan")
    return jax.shard_map(local, mesh=mesh, in_specs=in_specs, out_specs=out_specs, check_vma=False)
```

time: 88.5 us -> 68.1 us (0.77)
  local copies, waits for them, and re-layouts: 11.2 us -> 2.09 us
  Pallas kernels: 32.3 us -> 26.3 us
  waiting for transfers between devices: 19.8 us -> 15.2 us
  starting transfers between devices: 20.4 us -> 18.9 us
    pallas_call x2, Pallas kernels: 28 us -> 19.7 us  [segment_stack(): pl.pallas_call(functools.partial(segment_kernel, shape), out_shape=(out,...]
    ppermute x11, waiting for transfers between devices: 18.7 us -> 14.3 us  [the longest x9 7.84 us: within(): lax.ppermute(x, 'tm', [(i, i // half * half + (i % half ^ step)) for i in...]
    ppermute x1, starting transfers between devices: 3.79 us -> 0.22 us  [local(): total = keep + lax.ppermute(send, 'chan', swap) + far]
    slice x15 -> x0, local copies, waits for them, and re-layouts: 2.78 us -> none  [the longest x1 1.47 us: local(): rows = [packed[0]]]
    ppermute x11, starting transfers between devices: 16.5 us -> 18.6 us  [the longest x9 11.7 us: within(): lax.ppermute(x, 'tm', [(i, i // half * half + (i % half ^ step)) for i in...]
    reshape x6 -> x0, local copies, waits for them, and re-layouts: 2.04 us -> none  [the longest x2 1.18 us: stack_of(): chans = maps[:, :pair_rows].reshape(-1)]
    reduce_sum x2 -> x0, other arithmetic: 1.76 us -> none  [the longest x1 0.92 us: normalized(): energy = jnp.sum(centred * centred, axis=-1, keepdims=True)]
    pallas_call x0 -> x1, Pallas kernels: none -> 1.72 us  [unit_block(): pl.pallas_call(unit_kernel, out_shape=jax.ShapeDtypeStruct((rows, LANES),...]
  transfers between devices with their start and end apart: 13 -> 13, of which waited for: 5 -> 5; matrix products, arithmetic and copies ran while one was open for 10% -> 4% of each run, Pallas kernels for 19% -> 16%
where the time goes in v2:
time: 68.1 us; the launch traced here: 67.7 us
  Pallas kernels  26.3 us (39%)
  starting transfers between devices  18.9 us (28%)
  waiting for transfers between devices  15.2 us (22%)
  other arithmetic  5.15 us (8%)
  local copies, waits for them, and re-layouts  2.09 us (3%)
    pallas_call x2, Pallas kernels, segment_stack(): pl.pallas_call(functools.partial(segment_kernel, shape), out_shape=(out,...  19.7 us
    ppermute x9, starting transfers between devices, within(): lax.ppermute(x, 'tm', [(i, i // half * half + (i % half ^ step)) for i in...  11.7 us
    ppermute x9, waiting for transfers between devices, within(): lax.ppermute(x, 'tm', [(i, i // half * half + (i % half ^ step)) for i in...  7.84 us
    ppermute x1, waiting for transfers between devices, local(): far = lax.ppermute(far, 'tm', across)  5.4 us
    pallas_call x1, Pallas kernels, pack_rows(): pl.pallas_call(functools.partial(pack_kernel, half, capacity), out_shape=...  4.89 us
    ppermute x1, starting transfers between devices, local(): pair = jnp.concatenate([block, lax.ppermute(block, 'tm', across)], axis=0)  4.06 us
    ppermute x1, starting transfers between devices, local(): far = lax.ppermute(far, 'tm', across)  2.86 us
    unnamed x20, local copies, waits for them, and re-layouts  2.09 us
  transfers between devices with their start and end apart: 13, of which 5 were waited for; matrix products, arithmetic and copies ran while one was open for 4% of the time, Pallas kernels for 16%

profile of v2, /device:TPU:0, one launch (start us, length us, event | category | flops | bytes accessed | tf_op | source)
XLA Modules:
  0.0 67.7 jit_solution(16642272465945983415)
XLA Ops:
  0.0 0.6 pad_add_fusion.where
  0.6 4.9 %pack_rows.1 = (f32[12,32,128]{2,1,0:T(8,128)}, f32[12,32,128]{2,1,0:T(8,128)}, f32[12,32,128]{2,1,0:T(8,128)}, f32[12,32,128]{2,1,0:T(8,128)}, f32[12,32,128]{2...) custom-call(s32[96]{0:T(128)} %dest.1, s32[96]{0:T(128)} %chan.2, ...), custom_call_target="tpu_custom_call" | custom-call | tf_op jit(solution)/shard_map/pack_rows/pallas_call | solution.py:101
  5.5 1.7 %unit_block.1 = f32[72,128]{1,0:T(8,128)} custom-call(f32[4,8,256]{2,1,0:T(8,128)} %templ, s32[4,8]{1,0:T(4,128)} %chan.3, s32[4,8]{1,0:T(4,128)} %off.1), custom_call_target="tpu_custom_call" | custom-call | tf_op jit(solution)/shard_map/unit_block/pallas_call | solution.py:150
  7.2 4.1 %collective-permute-start.3 = (f32[72,128]{1,0:T(8,128)}, f32[72,128]{1,0:T(8,128)S(1)}, u32[]{:S(2)}, u32[]{:S(2)}) collective-permute-start(f32[72,128]{1,0:T(8,128)} %unit_block.1), channel_id=1, source_target_pairs={{0,8},{2,10},{4,12},{6,14},{8,0},{10,2},{12,4},{14,6},{1,9},{3,11}... | collective-permute-start | bytes 110600 | tf_op jit(solution)/shard_map/ppermute | solution.py:386
  11.3 1.5 %collective-permute-start = (f32[12,32,128]{2,1,0:T(8,128)}, f32[12,32,128]{2,1,0:T(8,128)S(1)}, u32[]{:S(2)}, u32[]{:S(2)}) collective-permute-start(f32[12,32,128]{2,1,0:T(8,128)} %get-tuple-element.33), channel_id=1, source_target_pairs={{0,2},{2,0},{4,6},{6,4},{8,10},{10,8},{12,14},{14,12},{1,3},{3,1},... | collective-permute-start | bytes 589832 | tf_op jit(solution)/shard_map/ppermute | solution.py:376
  12.8 1.0 %collective-permute-done.3 = f32[72,128]{1,0:T(8,128)S(1)} collective-permute-done((f32[72,128]{1,0:T(8,128)}, f32[72,128]{1,0:T(8,128)S(1)}, u32[]{:S(2)}, u32[]{:S(2)}) %collective-permute-start.3) | collective-permute-done | bytes 36896 | tf_op jit(solution)/shard_map/ppermute | solution.py:386
  13.8 0.8 %pad_maximum_fusion.refs_4_ = f32[144,128]{1,0:T(8,128)S(1)} fusion(f32[72,128]{1,0:T(8,128)S(1)} %collective-permute-done.3, f32[72,128]{1,0:T(8,128)} %unit_block.1), kind=kLoop, calls=%fused_computation.1 | loop fusion | flops 18432 | bytes 147456 | tf_op jit(solution)/shard_map/concatenate | solution.py:386
  14.6 2.5 %collective-permute-start.6 = (f32[144,128]{1,0:T(8,128)S(1)}, f32[144,128]{1,0:T(8,128)S(1)}, u32[]{:S(2)}, u32[]{:S(2)}) collective-permute-start(f32[144,128]{1,0:T(8,128)S(1)} %pad_maximum_fusion.refs_4_), channel_id=1, source_target_pairs={{0,6},{2,4},{4,2},{6,0},{8,14},{10,12},{12,10},{14,8},{1,7},{3,5},... | collective-permute-start | bytes 221192 | tf_op jit(solution)/shard_map/ppermute | solution.py:376
  17.0 0.7 %collective-permute-start.1 = (f32[12,32,128]{2,1,0:T(8,128)}, f32[12,32,128]{2,1,0:T(8,128)S(1)}, u32[]{:S(2)}, u32[]{:S(2)}) collective-permute-start(f32[12,32,128]{2,1,0:T(8,128)} %get-tuple-element.34), channel_id=1, source_target_pairs={{0,4},{2,6},{4,0},{6,2},{8,12},{10,14},{12,8},{14,10},{1,5},{3,7},... | collective-permute-start | bytes 589832 | tf_op jit(solution)/shard_map/ppermute | solution.py:376
  17.8 1.2 %collective-permute-start.2 = (f32[12,32,128]{2,1,0:T(8,128)}, f32[12,32,128]{2,1,0:T(8,128)S(1)}, u32[]{:S(2)}, u32[]{:S(2)}) collective-permute-start(f32[12,32,128]{2,1,0:T(8,128)} %get-tuple-element.35), channel_id=1, source_target_pairs={{0,6},{2,4},{4,2},{6,0},{8,14},{10,12},{12,10},{14,8},{1,7},{3,5},... | collective-permute-start | bytes 589832 | tf_op jit(solution)/shard_map/ppermute | solution.py:376
  19.0 0.5 collective-permute-start.5
  19.5 1.1 %collective-permute-done.6.refs_7_ = f32[144,128]{1,0:T(8,128)S(1)} collective-permute-done((f32[144,128]{1,0:T(8,128)S(1)}, f32[144,128]{1,0:T(8,128)S(1)}, u32[]{:S(2)}, u32[]{:S(2)}) %collective-permute-start.6) | collective-permute-done | bytes 73760 | tf_op jit(solution)/shard_map/ppermute | solution.py:376
  20.6 1.7 %collective-permute-start.4 = (f32[144,128]{1,0:T(8,128)S(1)}, f32[144,128]{1,0:T(8,128)S(1)}, u32[]{:S(2)}, u32[]{:S(2)}) collective-permute-start(f32[144,128]{1,0:T(8,128)S(1)} %pad_maximum_fusion.refs_4_), channel_id=1, source_target_pairs={{0,2},{2,0},{4,6},{6,4},{8,10},{10,8},{12,14},{14,12},{1,3},{3,1},... | collective-permute-start | bytes 221192 | tf_op jit(solution)/shard_map/ppermute | solution.py:376
  22.4 6.7 %collective-permute-done.5.refs_6_ = f32[144,128]{1,0:T(8,128)S(1)} collective-permute-done((f32[144,128]{1,0:T(8,128)S(1)}, f32[144,128]{1,0:T(8,128)S(1)}, u32[]{:S(2)}, u32[]{:S(2)}) %collective-permute-start.5) | collective-permute-done | bytes 73760 | tf_op jit(solution)/shard_map/ppermute | solution.py:376
  29.1 0.6 collective-permute-start.8
  29.7 0.0 collective-permute-done.4.refs_5_
  29.7 0.9 %collective-permute-start.9 = (f32[12,32,128]{2,1,0:T(8,128)}, f32[12,32,128]{2,1,0:T(8,128)S(1)}, u32[]{:S(2)}, u32[]{:S(2)}) collective-permute-start(f32[12,32,128]{2,1,0:T(8,128)} %get-tuple-element.50), channel_id=1, source_target_pairs={{0,4},{2,6},{4,0},{6,2},{8,12},{10,14},{12,8},{14,10},{1,5},{3,7},... | collective-permute-start | bytes 589832 | tf_op jit(solution)/shard_map/ppermute | solution.py:376
  30.5 0.0 collective-permute-done.refs_1_
  30.5 2.0 %collective-permute-start.10 = (f32[12,32,128]{2,1,0:T(8,128)}, f32[12,32,128]{2,1,0:T(8,128)S(1)}, u32[]{:S(2)}, u32[]{:S(2)}) collective-permute-start(f32[12,32,128]{2,1,0:T(8,128)} %get-tuple-element.51), channel_id=1, source_target_pairs={{0,6},{2,4},{4,2},{6,0},{8,14},{10,12},{12,10},{14,8},{1,7},{3,5},... | collective-permute-start | bytes 589832 | tf_op jit(solution)/shard_map/ppermute | solution.py:376
  32.6 0.7 add_add_fusion.1.where
  33.3 0.0 collective-permute-done.1.refs_2_
  33.3 0.0 collective-permute-done.2.refs_3_
  33.3 0.0 copy-start.6
  33.3 0.0 copy-done
  33.3 0.0 copy-done.1
  33.3 0.0 copy-done.2
  33.3 0.0 copy-done.3
  33.3 0.0 copy-done.4
  33.3 0.6 copy-done.5
  33.9 0.1 copy-done.6
  34.0 10.8 %segment_stack.2 = (f32[4,4,1792]{2,1,0:T(4,128)}, f32[4,4,1792]{2,1,0:T(4,128)}) custom-call(s32[4]{0:T(128)} %add_add_fusion.1.where, f32[12,32,128]{2,1,0:T(8,128)} %get-tuple-element.32.refs_0_, f32[12,32,128]{2,1,0:T(8,128)} %copy-done.4, f32[12,32,128]{2,1,0:T(8,128)} %copy-done.5, f32[12,32,128]{2,1,0:T(8,128)} %copy-done.6, f32[144,128]{1,0:T(8,128)} %copy-done, ...), custom_call_target="tpu_custom_call" | custom-call | tf_op jit(solution)/shard_map/segment_stack/pallas_call | solution.py:339
  44.9 0.1 collective-permute-start.7
  44.9 0.6 add_add_fusion.where
  45.5 0.9 %collective-permute-done.7 = f32[4,4,1792]{2,1,0:T(4,128)S(1)} collective-permute-done((f32[4,4,1792]{2,1,0:T(4,128)}, f32[4,4,1792]{2,1,0:T(4,128)S(1)}, u32[]{:S(2)}, u32[]{:S(2)}) %collective-permute-start.7) | collective-permute-done | bytes 114720 | tf_op jit(solution)/shard_map/ppermute | solution.py:396
  46.5 0.9 %add.23 = f32[4,4,1792]{2,1,0:T(4,128)S(1)} add(f32[4,4,1792]{2,1,0:T(4,128)} %get-tuple-element.46, f32[4,4,1792]{2,1,0:T(4,128)S(1)} %collective-permute-done.7) | non-fusion elementwise | flops 28672 | bytes 344064 | tf_op jit(solution)/shard_map/add | solution.py:396
  47.4 0.0 collective-permute-done.8.refs_1_
  47.4 0.0 copy-start.7
  47.4 0.0 collective-permute-done.9.refs_2_
  47.4 0.0 collective-permute-done.10.refs_3_
  47.4 0.6 copy-done.7
  48.1 0.1 copy-done.8
  48.1 0.7 copy-done.9
  48.8 8.8 %segment_stack.3 = (f32[4,4,1792]{2,1,0:T(4,128)}, f32[4,4,1792]{2,1,0:T(4,128)}) custom-call(s32[4]{0:T(128)} %add_add_fusion.where, f32[12,32,128]{2,1,0:T(8,128)} %get-tuple-element.52.refs_0_, f32[12,32,128]{2,1,0:T(8,128)} %copy-done.7, f32[12,32,128]{2,1,0:T(8,128)} %copy-done.8, f32[12,32,128]{2,1,0:T(8,128)} %copy-done.9, f32[144,128]{1,0:T(8,128)} %copy-done, ...), custom_call_target="tpu_custom_call" | custom-call | tf_op jit(solution)/shard_map/segment_stack/pallas_call | solution.py:339
  57.7 0.2 collective-permute-start.11
  57.9 2.9 %collective-permute-start.12 = (f32[4,4,1792]{2,1,0:T(4,128)S(1)}, f32[4,4,1792]{2,1,0:T(4,128)S(1)}, u32[]{:S(2)}, u32[]{:S(2)}) collective-permute-start(f32[4,4,1792]{2,1,0:T(4,128)S(1)} %add.23), channel_id=1, source_target_pairs={{0,8},{2,10},{4,12},{6,14},{8,0},{10,2},{12,4},{14,6},{1,9},{3,11}... | collective-permute-start | bytes 344072 | tf_op jit(solution)/shard_map/ppermute | solution.py:398
  60.7 0.0 collective-permute-done.11
  60.7 5.4 %collective-permute-done.12 = f32[4,4,1792]{2,1,0:T(4,128)S(1)} collective-permute-done((f32[4,4,1792]{2,1,0:T(4,128)S(1)}, f32[4,4,1792]{2,1,0:T(4,128)S(1)}, u32[]{:S(2)}, u32[]{:S(2)}) %collective-permute-start.12) | collective-permute-done | bytes 114720 | tf_op jit(solution)/shard_map/ppermute | solution.py:398
  66.1 1.6 %add_bitcast_fusion = f32[1,4,4,1792]{3,2,1,0:T(4,128)} fusion(f32[4,4,1792]{2,1,0:T(4,128)S(1)} %collective-permute-done.12, f32[4,4,1792]{2,1,0:T(4,128)} %get-tuple-element.56, f32[4,4,1792]{2,1,0:T(4,128)S(1)} %collective-permute-done.11), kind=kLoop, calls=%fused_computation | loop fusion | flops 57344 | bytes 458752 | tf_op jit(solution)/shard_map/broadcast_in_dim | solution.py:401
  (8 shorter events, 0.0 us)
Async XLA Ops:
  7.2 6.6 %collective-permute-start.3 = (f32[72,128]{1,0:T(8,128)}, f32[72,128]{1,0:T(8,128)S(1)}, u32[]{:S(2)}, u32[]{:S(2)}) collective-permute-start(f32[72,128]{1,0:T(8,128)} %unit_block.1), channel_id=1, source_target_pairs={{0,8},{2,10},{4,12},{6,14},{8,0},{10,2},{12,4},{14,6},{1,9},{3,11}... | collective-permute-start | bytes 110600 | tf_op jit(solution)/shard_map/ppermute | solution.py:386
  11.3 19.3 %collective-permute-start = (f32[12,32,128]{2,1,0:T(8,128)}, f32[12,32,128]{2,1,0:T(8,128)S(1)}, u32[]{:S(2)}, u32[]{:S(2)}) collective-permute-start(f32[12,32,128]{2,1,0:T(8,128)} %get-tuple-element.33), channel_id=1, source_target_pairs={{0,2},{2,0},{4,6},{6,4},{8,10},{10,8},{12,14},{14,12},{1,3},{3,1},... | collective-permute-start | bytes 589832 | tf_op jit(solution)/shard_map/ppermute | solution.py:376
  14.6 18.7 %copy-start = (f32[144,128]{1,0:T(8,128)}, f32[144,128]{1,0:T(8,128)S(1)}, u32[]{:S(2)}) copy-start(f32[144,128]{1,0:T(8,128)S(1)} %pad_maximum_fusion.refs_4_) | copy-start | bytes 221188
  14.6 6.0 %collective-permute-start.6 = (f32[144,128]{1,0:T(8,128)S(1)}, f32[144,128]{1,0:T(8,128)S(1)}, u32[]{:S(2)}, u32[]{:S(2)}) collective-permute-start(f32[144,128]{1,0:T(8,128)S(1)} %pad_maximum_fusion.refs_4_), channel_id=1, source_target_pairs={{0,6},{2,4},{4,2},{6,0},{8,14},{10,12},{12,10},{14,8},{1,7},{3,5},... | collective-permute-start | bytes 221192 | tf_op jit(solution)/shard_map/ppermute | solution.py:376
  17.0 16.2 %collective-permute-start.1 = (f32[12,32,128]{2,1,0:T(8,128)}, f32[12,32,128]{2,1,0:T(8,128)S(1)}, u32[]{:S(2)}, u32[]{:S(2)}) collective-permute-start(f32[12,32,128]{2,1,0:T(8,128)} %get-tuple-element.34), channel_id=1, source_target_pairs={{0,4},{2,6},{4,0},{6,2},{8,12},{10,14},{12,8},{14,10},{1,5},{3,7},... | collective-permute-start | bytes 589832 | tf_op jit(solution)/shard_map/ppermute | solution.py:376
  17.8 15.5 %collective-permute-start.2 = (f32[12,32,128]{2,1,0:T(8,128)}, f32[12,32,128]{2,1,0:T(8,128)S(1)}, u32[]{:S(2)}, u32[]{:S(2)}) collective-permute-start(f32[12,32,128]{2,1,0:T(8,128)} %get-tuple-element.35), channel_id=1, source_target_pairs={{0,6},{2,4},{4,2},{6,0},{8,14},{10,12},{12,10},{14,8},{1,7},{3,5},... | collective-permute-start | bytes 589832 | tf_op jit(solution)/shard_map/ppermute | solution.py:376
  19.0 10.1 %collective-permute-start.5 = (f32[144,128]{1,0:T(8,128)S(1)}, f32[144,128]{1,0:T(8,128)S(1)}, u32[]{:S(2)}, u32[]{:S(2)}) collective-permute-start(f32[144,128]{1,0:T(8,128)S(1)} %pad_maximum_fusion.refs_4_), channel_id=1, source_target_pairs={{0,4},{2,6},{4,0},{6,2},{8,12},{10,14},{12,8},{14,10},{1,5},{3,7},... | collective-permute-start | bytes 221192 | tf_op jit(solution)/shard_map/ppermute | solution.py:376
  20.6 12.7 %copy-start.1 = (f32[144,128]{1,0:T(8,128)}, f32[144,128]{1,0:T(8,128)S(1)}, u32[]{:S(2)}) copy-start(f32[144,128]{1,0:T(8,128)S(1)} %collective-permute-done.6.refs_7_) | copy-start | bytes 221188
  20.6 9.0 %collective-permute-start.4 = (f32[144,128]{1,0:T(8,128)S(1)}, f32[144,128]{1,0:T(8,128)S(1)}, u32[]{:S(2)}, u32[]{:S(2)}) collective-permute-start(f32[144,128]{1,0:T(8,128)S(1)} %pad_maximum_fusion.refs_4_), channel_id=1, source_target_pairs={{0,2},{2,0},{4,6},{6,4},{8,10},{10,8},{12,14},{14,12},{1,3},{3,1},... | collective-permute-start | bytes 221192 | tf_op jit(solution)/shard_map/ppermute | solution.py:376
  29.1 4.2 %copy-start.2 = (f32[144,128]{1,0:T(8,128)}, f32[144,128]{1,0:T(8,128)S(1)}, u32[]{:S(2)}) copy-start(f32[144,128]{1,0:T(8,128)S(1)} %collective-permute-done.5.refs_6_) | copy-start | bytes 221188
  29.1 18.3 %collective-permute-start.8 = (f32[12,32,128]{2,1,0:T(8,128)}, f32[12,32,128]{2,1,0:T(8,128)S(1)}, u32[]{:S(2)}, u32[]{:S(2)}) collective-permute-start(f32[12,32,128]{2,1,0:T(8,128)} %get-tuple-element.49), channel_id=1, source_target_pairs={{0,2},{2,0},{4,6},{6,4},{8,10},{10,8},{12,14},{14,12},{1,3},{3,1},... | collective-permute-start | bytes 589832 | tf_op jit(solution)/shard_map/ppermute | solution.py:376
  29.7 3.6 %copy-start.3 = (f32[144,128]{1,0:T(8,128)}, f32[144,128]{1,0:T(8,128)S(1)}, u32[]{:S(2)}) copy-start(f32[144,128]{1,0:T(8,128)S(1)} %collective-permute-done.4.refs_5_) | copy-start | bytes 221188
  29.7 17.7 %collective-permute-start.9 = (f32[12,32,128]{2,1,0:T(8,128)}, f32[12,32,128]{2,1,0:T(8,128)S(1)}, u32[]{:S(2)}, u32[]{:S(2)}) collective-permute-start(f32[12,32,128]{2,1,0:T(8,128)} %get-tuple-element.50), channel_id=1, source_target_pairs={{0,4},{2,6},{4,0},{6,2},{8,12},{10,14},{12,8},{14,10},{1,5},{3,7},... | collective-permute-start | bytes 589832 | tf_op jit(solution)/shard_map/ppermute | solution.py:376
  30.5 2.8 %copy-start.4 = (f32[12,32,128]{2,1,0:T(8,128)}, f32[12,32,128]{2,1,0:T(8,128)S(1)}, u32[]{:S(2)}) copy-start(f32[12,32,128]{2,1,0:T(8,128)S(1)} %collective-permute-done.refs_1_) | copy-start | bytes 589828
  30.5 16.9 %collective-permute-start.10 = (f32[12,32,128]{2,1,0:T(8,128)}, f32[12,32,128]{2,1,0:T(8,128)S(1)}, u32[]{:S(2)}, u32[]{:S(2)}) collective-permute-start(f32[12,32,128]{2,1,0:T(8,128)} %get-tuple-element.51), channel_id=1, source_target_pairs={{0,6},{2,4},{4,2},{6,0},{8,14},{10,12},{12,10},{14,8},{1,7},{3,5},... | collective-permute-start | bytes 589832 | tf_op jit(solution)/shard_map/ppermute | solution.py:376
  33.3 0.7 copy-start.5
  33.3 0.8 %copy-start.6 = (f32[12,32,128]{2,1,0:T(8,128)}, f32[12,32,128]{2,1,0:T(8,128)S(1)}, u32[]{:S(2)}) copy-start(f32[12,32,128]{2,1,0:T(8,128)S(1)} %collective-permute-done.2.refs_3_) | copy-start | bytes 589828
  44.9 1.6 %collective-permute-start.7 = (f32[4,4,1792]{2,1,0:T(4,128)}, f32[4,4,1792]{2,1,0:T(4,128)S(1)}, u32[]{:S(2)}, u32[]{:S(2)}) collective-permute-start(f32[4,4,1792]{2,1,0:T(4,128)} %get-tuple-element.47), channel_id=1, source_target_pairs={{0,1},{1,0},{2,3},{3,2},{4,5},{5,4},{6,7},{7,6},{8,9},{9,8},{10,11... | collective-permute-start | bytes 344072 | tf_op jit(solution)/shard_map/ppermute | solution.py:396
  47.4 0.7 copy-start.7
  47.4 0.7 %copy-start.8 = (f32[12,32,128]{2,1,0:T(8,128)}, f32[12,32,128]{2,1,0:T(8,128)S(1)}, u32[]{:S(2)}) copy-start(f32[12,32,128]{2,1,0:T(8,128)S(1)} %collective-permute-done.9.refs_2_) | copy-start | bytes 589828
  48.1 0.7 copy-start.9
  57.7 3.1 %collective-permute-start.11 = (f32[4,4,1792]{2,1,0:T(4,128)}, f32[4,4,1792]{2,1,0:T(4,128)S(1)}, u32[]{:S(2)}, u32[]{:S(2)}) collective-permute-start(f32[4,4,1792]{2,1,0:T(4,128)} %get-tuple-element.57), channel_id=1, source_target_pairs={{0,1},{1,0},{2,3},{3,2},{4,5},{5,4},{6,7},{7,6},{8,9},{9,8},{10,11... | collective-permute-start | bytes 344072 | tf_op jit(solution)/shard_map/ppermute | solution.py:400
  57.9 8.3 %collective-permute-start.12 = (f32[4,4,1792]{2,1,0:T(4,128)S(1)}, f32[4,4,1792]{2,1,0:T(4,128)S(1)}, u32[]{:S(2)}, u32[]{:S(2)}) collective-permute-start(f32[4,4,1792]{2,1,0:T(4,128)S(1)} %add.23), channel_id=1, source_target_pairs={{0,8},{2,10},{4,12},{6,14},{8,0},{10,2},{12,4},{14,6},{1,9},{3,11}... | collective-permute-start | bytes 344072 | tf_op jit(solution)/shard_map/ppermute | solution.py:398

commit v3 on v2

--- a/solution.py
+++ b/solution.py
@@ -12,6 +12,7 @@
 MAXOFF = 256
 STOPS = 4
 LANES = 128
+HALF = LANES // 2
 SUB = 8
 UNROLL = 16
 PAIR_BITS = 8
@@ -22,6 +23,7 @@
 FLOOR_SHARE = 0.25
 TEMPLATE_EPS = 1e-06
 
+
 SMEM = pl.BlockSpec(memory_space=pltpu.SMEM)
 VMEM = pl.BlockSpec(memory_space=pltpu.VMEM)
 
@@ -31,12 +33,22 @@
     return high, (x - high.astype(jnp.float32)).astype(jnp.bfloat16)
 
 
-def pack_kernel(half, capacity, dest, chan, length, where, rec, *refs):
-    outs = refs[: 2 * half]
-    count, source, rows = refs[2 * half :]
+def pack_kernel(half, capacity, dest, chan, length, rec, templ, templ_chan, templ_off, *refs):
+    block_out = refs[0]
+    outs = refs[1 : 2 * half + 1]
+    count, source, raw, rows, stage, in_sems, out_sems = refs[2 * half + 1 :]
     slot_count = dest.shape[0]
     blocks = rec.shape[1] // LANES
-    member, home = where[0], where[1]
+    me = lax.axis_index("tm")
+    member, home = lax.rem(me, half), lax.div(me, half)
+    pieces = in_sems.shape[0]
+    piece_rows = slot_count // pieces
+    arriving = []
+    for p in range(pieces):
+        part = pl.ds(p * piece_rows, piece_rows)
+        arriving.append(pltpu.make_async_copy(rec.at[part], raw.at[part], in_sems.at[p]))
+        arriving[-1].start()
+    write_unit(templ, templ_chan, templ_off, block_out)
 
     def clear_count(i, c):
         count[i] = 0
@@ -67,19 +79,22 @@
     def reform(g, c):
         first = pl.multiple_of(g * SUB, SUB)
         for b in range(blocks):
-            rows[pl.ds(first * blocks + b, SUB, stride=blocks), :] = rec[
+            rows[pl.ds(first * blocks + b, SUB, stride=blocks), :] = raw[
                 pl.ds(first, SUB), b * LANES : (b + 1) * LANES
             ]
         return c
 
-    lax.fori_loop(0, slot_count // SUB, reform, 0)
+    for p in range(pieces):
+        arriving[p].wait()
+        lax.fori_loop(p * piece_rows // SUB, (p + 1) * piece_rows // SUB, reform, 0)
     flat = lax.broadcasted_iota(jnp.int32, (blocks, LANES), 0) * LANES + lax.broadcasted_iota(
         jnp.int32, (blocks, LANES), 1
     )
     last = blocks * LANES - 1
+    leaving = []
     for group, out in enumerate(outs):
 
-        def emit(i, c, group=group, out=out):
+        def emit(i, c, group=group):
             r = source[group * capacity + i]
             used = r >= 0
             row = jnp.maximum(r, 0)
@@ -87,33 +102,21 @@
             tag = jnp.where(used, chan[row], -1).astype(jnp.float32)
             tile = rows[pl.ds(pl.multiple_of(row * blocks, blocks), blocks), :]
             tile = jnp.where(flat < limit, tile, 0.0)
-            out[i] = jnp.where(flat == last, tag, tile)
+            stage[group, i * blocks : (i + 1) * blocks, :] = jnp.where(flat == last, tag, tile)
             return c
 
-        lax.fori_loop(0, capacity, emit, 0, unroll=4 if capacity % 4 == 0 else True)
-
-
-def pack_rows(records, row_dest, row_chan, row_len, where, half):
-    slot_count, sample_count = records.shape
-    capacity = slot_count // (2 * half)
-    blocks = sample_count // LANES
-    out = jax.ShapeDtypeStruct((capacity, blocks, LANES), jnp.float32)
-    outs = pl.pallas_call(
-        functools.partial(pack_kernel, half, capacity),
-        out_shape=[out] * (2 * half),
-        in_specs=[SMEM] * 4 + [VMEM],
-        out_specs=[VMEM] * (2 * half),
-        scratch_shapes=[
-            pltpu.SMEM((2 * half + 1,), jnp.int32),
-            pltpu.SMEM((slot_count + 1,), jnp.int32),
-            pltpu.VMEM((slot_count * blocks, LANES), jnp.float32),
-        ],
-        name="pack_rows",
-    )(row_dest, row_chan, row_len, where, records)
-    return outs[:half], outs[half:]
-
-
-def unit_kernel(templ, chan, off, out):
+        for i in range(capacity):
+            emit(i, 0)
+        if group < half:
+            stage[group, capacity * blocks :, :] = block_out[...]
+        part = stage.at[group, pl.ds(0, out.shape[0])]
+        leaving.append(pltpu.make_async_copy(part, out, out_sems.at[group]))
+        leaving[-1].start()
+    for copy in leaving:
+        copy.wait()
+
+
+def write_unit(templ, chan, off, out):
     per_block, half_taps, taps = templ.shape
     pair_rows = per_block * half_taps
     x = templ[...].reshape(pair_rows, taps)
@@ -144,28 +147,52 @@
     out[base : base + 1, :] = row
 
 
-def unit_block(templates, tmpl_chan, tmpl_off):
+def pack(records, row_dest, row_chan, row_len, templates, tmpl_chan, tmpl_off, half):
+    slot_count, sample_count = records.shape
+    capacity = slot_count // (2 * half)
+    blocks = sample_count // LANES
     per_block, half_taps, taps = templates.shape
-    rows = (taps // LANES) * per_block * half_taps + SUB
-    return pl.pallas_call(
-        unit_kernel,
-        out_shape=jax.ShapeDtypeStruct((rows, LANES), jnp.float32),
-        in_specs=[VMEM] * 3,
-        out_specs=VMEM,
-        name="unit_block",
-    )(templates, tmpl_chan, tmpl_off)
-
-
-def segment_kernel(shape, where, *refs):
+    block_rows = (taps // LANES) * per_block * half_taps + SUB
+    pieces = 4 if slot_count % (4 * SUB) == 0 else 1
+    far = jax.ShapeDtypeStruct((capacity * blocks + block_rows, LANES), jnp.float32)
+    own = jax.ShapeDtypeStruct((capacity * blocks, LANES), jnp.float32)
+    whole = pl.BlockSpec(memory_space=pl.ANY)
+    block, *outs = pl.pallas_call(
+        functools.partial(pack_kernel, half, capacity),
+        out_shape=[jax.ShapeDtypeStruct((block_rows, LANES), jnp.float32)]
+        + [far] * half
+        + [own] * half,
+        in_specs=[SMEM] * 3 + [whole] + [VMEM] * 3,
+        out_specs=[VMEM] + [whole] * (2 * half),
+        scratch_shapes=[
+            pltpu.SMEM((2 * half + 1,), jnp.int32),
+            pltpu.SMEM((slot_count + 1,), jnp.int32),
+            pltpu.VMEM((slot_count, sample_count), jnp.float32),
+            pltpu.VMEM((slot_count * blocks, LANES), jnp.float32),
+            pltpu.VMEM((2 * half, capacity * blocks + block_rows, LANES), jnp.float32),
+            pltpu.SemaphoreType.DMA((pieces,)),
+            pltpu.SemaphoreType.DMA((2 * half,)),
+        ],
+        name="pack",
+    )(row_dest, row_chan, row_len, records, templates, tmpl_chan, tmpl_off)
+    return block, outs[:half], outs[half:]
+
+
+def segment_kernel(shape, ahead, *refs):
     parts, capacity, blocks, taps, per_block, half_taps, lags = shape
+    count = len(refs) - 14
     rows_in = refs[:parts]
-    templ_in = refs[parts : 2 * parts]
-    keep, send = refs[2 * parts : 2 * parts + 2]
+    near_in = refs[:parts] if count == 2 * parts else refs[parts : 2 * parts]
+    other_in = refs[count - parts : count]
+    keep, send = refs[count : count + 2]
     (
-        x_sc, s_sc, q_sc, inv_sc, h_sc, u_sc, acc, code_v, code_s, listed, sem,
-    ) = refs[2 * parts + 2 :]
-    segment, member, home, core = where[0], where[1], where[2], where[3]
+        x_sc, y_sc, s_sc, q_sc, inv_sc, h_sc, u_sc, acc, code_v, code_s, listed, sems,
+    ) = refs[count + 2 :]
     size = 2 * parts
+    me = lax.axis_index("tm")
+    core = lax.axis_index("chan")
+    segment = lax.rem(me + ahead, size)
+    member, home = lax.rem(me, parts), lax.div(me, parts)
     slot_count = parts * capacity
     rows = slot_count * blocks
     pair_rows = per_block * half_taps
@@ -174,18 +201,27 @@
     stack_gain = (taps * TCH) ** 0.5 / TCH
 
     part_rows = capacity * blocks
+    copies = []
     for k in range(parts):
-        x_sc[k * part_rows : (k + 1) * part_rows, :] = rows_in[k][...].reshape(part_rows, LANES)
         index = jnp.bitwise_xor(member, k)
-        u_sc[home * parts + index] = templ_in[k][:block_rows, :]
-        u_sc[(1 - home) * parts + index] = templ_in[k][block_rows:, :]
+        moves = (
+            (rows_in[k].at[pl.ds(0, part_rows)], x_sc.at[pl.ds(k * part_rows, part_rows)]),
+            (near_in[k].at[pl.ds(part_rows, block_rows)], u_sc.at[home * parts + index]),
+            (other_in[k], u_sc.at[(1 - home) * parts + index]),
+        )
+        for source, target in moves:
+            copies.append(pltpu.make_async_copy(source, target, sems.at[1 + len(copies)]))
+            copies[-1].start()
     x_sc[rows:, :] = jnp.zeros((SUB, LANES), jnp.float32)
+    acc[...] = jnp.zeros_like(acc)
+    for copy in copies:
+        copy.wait()
+
     lane_p = lax.broadcasted_iota(jnp.int32, (1, LANES), 1)
     chan_of = jnp.zeros((1, LANES), jnp.float32)
     off_of = jnp.zeros((1, LANES), jnp.float32)
     for s in range(STOPS):
-        block = lax.rem(segment - s + size, size)
-        maps = u_sc[block, block_rows - SUB : block_rows, :][:1]
+        maps = u_sc[lax.rem(segment - s + size, size), block_rows - SUB : block_rows, :][:1]
         here = lax.div(lane_p, pair_rows) == s
         chan_of = jnp.where(here, pltpu.roll(maps, (s * pair_rows) % LANES, 1), chan_of)
         off_of = jnp.where(here, pltpu.roll(maps, ((s - 1) * pair_rows) % LANES, 1), off_of)
@@ -197,9 +233,8 @@
     code = lane_p.astype(jnp.float32) + slot_of * PAIR_STEP + off_of * (PAIR_STEP * SLOT_STEP)
     code = jnp.where(held > 0, code, -1.0).astype(jnp.int32)
     code_v[...] = jnp.broadcast_to(code, (SUB, LANES))
-    copy = pltpu.make_async_copy(code_v, code_s, sem)
+    copy = pltpu.make_async_copy(code_v, code_s, sems.at[0])
     copy.start()
-    acc[...] = jnp.zeros_like(acc)
 
     row_i = lax.broadcasted_iota(jnp.int32, (LANES, LANES), 0)
     lane_i = lax.broadcasted_iota(jnp.int32, (LANES, LANES), 1)
@@ -236,21 +271,35 @@
         variance = window(q_sc) - win_sum * win_sum / taps
         inv = stack_gain / jnp.sqrt(jnp.maximum(variance, FLOOR_SHARE * taps))
         inv_sc[pl.ds(base, chunk), :] = inv
-        high1, low1 = split(x_sc[pl.ds(base + 1, chunk), :])
-        high2, low2 = split(x_sc[pl.ds(base + 2, chunk), :])
+        before = y_sc[pl.ds(base + SUB - 1, chunk), :]
+        after = y_sc[pl.ds(base + SUB + 1, chunk), :]
+        windows = (
+            (jnp.where(left, x0, after), x_sc[pl.ds(base + 2, chunk), :]),
+            (jnp.where(left, before, x0), after),
+        )
         slot0 = g * chunk_slots
-        for j, (high, low) in enumerate(((high0, low0), (high1, low1), (high2, low2))):
-            lanes = slice(j * LANES, (j + 1) * LANES)
-            h_sc[pl.ds(slot0, chunk_slots), :blocks, lanes] = high.reshape(
-                chunk_slots, blocks, LANES
-            )
-            h_sc[pl.ds(slot0, chunk_slots), blocks:, lanes] = low.reshape(
-                chunk_slots, blocks, LANES
-            )
+        for i, window_pair in enumerate(windows):
+            for j, part in enumerate(window_pair):
+                lanes = slice(j * LANES, (j + 1) * LANES)
+                for k, piece in enumerate(split(part)):
+                    first = (2 * i + k) * blocks
+                    h_sc[pl.ds(slot0, chunk_slots), first : first + blocks, lanes] = piece.reshape(
+                        chunk_slots, blocks, LANES
+                    )
         return c
 
     s_sc[chunk:, :] = jnp.zeros((SUB, 2 * LANES), jnp.float32)
     q_sc[chunk:, :] = jnp.zeros((SUB, 2 * LANES), jnp.float32)
+    left = lax.broadcasted_iota(jnp.int32, (chunk, LANES), 1) < HALF
+
+    def turn(g, c):
+        base = pl.multiple_of(g * chunk, chunk)
+        y_sc[pl.ds(base + SUB, chunk), :] = pltpu.roll(x_sc[pl.ds(base, chunk), :], HALF, 1)
+        return c
+
+    y_sc[:SUB, :] = jnp.zeros((SUB, LANES), jnp.float32)
+    y_sc[rows + SUB :, :] = jnp.zeros((SUB, LANES), jnp.float32)
+    lax.fori_loop(0, slot_count // chunk_slots, turn, 0)
     lax.fori_loop(0, slot_count // chunk_slots, prepare, 0)
 
     copy.wait()
@@ -266,8 +315,11 @@
         listed[filled + i] = pair_count
 
     lane_b = lax.broadcasted_iota(jnp.int32, (blocks, LANES), 1)
-    low_mask = tail > 0
-    zero = jnp.zeros((LANES, LANES), jnp.bfloat16)
+    row_h = lax.broadcasted_iota(jnp.int32, (HALF, LANES), 0)
+    lane_h = lax.broadcasted_iota(jnp.int32, (HALF, LANES), 1)
+    mask = (row_h >= lane_h).astype(jnp.float32).astype(jnp.bfloat16) > 0
+    zero = jnp.zeros((HALF, LANES), jnp.bfloat16)
+    left_b = lane_b < HALF
 
     def pairs(g, c):
         for j in range(UNROLL):
@@ -281,7 +333,7 @@
 
             def circulant(row):
                 return pltpu.roll(
-                    jnp.broadcast_to(u_sc[block, pl.ds(row, 1), :], (LANES, LANES)),
+                    jnp.broadcast_to(u_sc[block, pl.ds(row, 1), :], (HALF, LANES)),
                     0,
                     1,
                     stride=1,
@@ -291,17 +343,22 @@
             first = split(circulant(inner))
             second = split(circulant(inner + pair_rows))
             bands = [
-                jnp.concatenate([jnp.where(low_mask, x, zero) for x in first], axis=1),
-                jnp.concatenate(
-                    [jnp.where(low_mask, y, x) for x, y in zip(first, second)], axis=1
-                ),
-                jnp.concatenate([jnp.where(low_mask, zero, y) for y in second], axis=1),
+                jnp.concatenate([jnp.where(mask, x, zero) for x in first], axis=1),
+                jnp.concatenate([jnp.where(mask, y, x) for x, y in zip(first, second)], axis=1),
+                jnp.concatenate([jnp.where(mask, zero, y) for y in second], axis=1),
             ]
-            weights = jnp.concatenate(bands, axis=0)
-            terms = jnp.dot(h_sc[slot], weights, preferred_element_type=jnp.float32)
-            corr = (terms[:blocks, :LANES] + terms[:blocks, LANES:]) + (
-                terms[blocks:, :LANES] + terms[blocks:, LANES:]
+            terms = jnp.dot(
+                h_sc[slot, :, : 3 * HALF],
+                jnp.concatenate(bands, axis=0),
+                preferred_element_type=jnp.float32,
             )
+            front, back = (
+                (part[:blocks, :LANES] + part[:blocks, LANES:])
+                + (part[blocks:, :LANES] + part[blocks:, LANES:])
+                for part in (terms[: 2 * blocks], terms[2 * blocks :])
+            )
+            back = jnp.where(left_b, pltpu.roll(back, blocks - 1, 0), back)
+            corr = front + pltpu.roll(back, HALF, 1)
             ratio = corr * inv_sc[pl.ds(pl.multiple_of(slot * blocks, blocks), blocks), :]
             by_lane = jnp.bitwise_and(off, LANES - 1)
             whole = off >= LANES
@@ -328,34 +385,36 @@
                 )
 
 
-def segment_stack(rows, templates, where, shape):
+def segment_stack(rows, near, other, ahead, shape):
     parts, capacity, blocks, _, per_block, half_taps, lags = shape
     slot_count = parts * capacity
     stack_count = STOPS * per_block
     pair_count = stack_count * half_taps
     chunk = (SUB if slot_count % SUB == 0 else 1) * blocks
-    block_rows = templates[0].shape[0] // 2
+    block_rows = other[0].shape[0]
     out = jax.ShapeDtypeStruct((STOPS, per_block, lags // 2), jnp.float32)
+    operands = list(rows) + ([] if near is rows else list(near)) + list(other)
     return pl.pallas_call(
-        functools.partial(segment_kernel, shape),
+        functools.partial(segment_kernel, shape, ahead),
         out_shape=(out, out),
-        in_specs=[SMEM] + [VMEM] * (2 * parts),
+        in_specs=[pl.BlockSpec(memory_space=pltpu.HBM)] * len(operands),
         out_specs=(VMEM, VMEM),
         scratch_shapes=[
             pltpu.VMEM((slot_count * blocks + SUB, LANES), jnp.float32),
+            pltpu.VMEM((slot_count * blocks + 2 * SUB, LANES), jnp.float32),
             pltpu.VMEM((chunk + SUB, 2 * LANES), jnp.float32),
             pltpu.VMEM((chunk + SUB, 2 * LANES), jnp.float32),
             pltpu.VMEM((slot_count * blocks, LANES), jnp.float32),
-            pltpu.VMEM((slot_count, 2 * blocks, 3 * LANES), jnp.bfloat16),
+            pltpu.VMEM((slot_count, 4 * blocks, 2 * LANES), jnp.bfloat16),
             pltpu.VMEM((2 * parts, block_rows, LANES), jnp.float32),
             pltpu.VMEM((stack_count + 1, blocks, LANES), jnp.float32),
             pltpu.VMEM((SUB, LANES), jnp.int32),
             pltpu.SMEM((SUB, LANES), jnp.int32),
             pltpu.SMEM((pair_count + UNROLL,), jnp.int32),
-            pltpu.SemaphoreType.DMA,
+            pltpu.SemaphoreType.DMA((3 * parts + 1,)),
         ],
         name="segment_stack",
-    )(where, *rows, *templates)
+    )(*operands)
 
 
 def local(records, row_dest, row_chan, row_len, templates, tmpl_chan, tmpl_off):
@@ -365,9 +424,6 @@
     capacity = slot_count // size
     per_block, half_taps, taps = templates.shape
     lags = sample_count - taps - MAXOFF
-    me = lax.axis_index("tm")
-    core = lax.axis_index("chan")
-    home, member = me // half, me % half
     across = [(i, (i + half) % size) for i in range(size)]
     swap = [(0, 1), (1, 0)]
     shape = (half, capacity, sample_count // LANES, taps, per_block, half_taps, lags)
@@ -377,26 +433,21 @@
             x, "tm", [(i, (i // half) * half + ((i % half) ^ step)) for i in range(size)]
         )
 
-    far_out, own_out = pack_rows(
-        records, row_dest, row_chan, row_len, jnp.stack([member, home]).astype(jnp.int32), half
+    block, far_out, own_out = pack(
+        records, row_dest, row_chan, row_len, templates, tmpl_chan, tmpl_off, half
     )
+
     far_rows = [far_out[0]] + [within(far_out[k], k) for k in range(1, half)]
-    templates, own_out = lax.optimization_barrier((templates, own_out))
-    block = unit_block(templates, tmpl_chan, tmpl_off)
-    pair = jnp.concatenate([block, lax.ppermute(block, "tm", across)], axis=0)
-    pair, own_out = lax.optimization_barrier((pair, own_out))
-    blocks = [pair] + [within(pair, k) for k in range(1, half)]
+    other = [
+        lax.ppermute(block, "tm", [(i, (i ^ k) ^ half) for i in range(size)])
+        for k in range(half)
+    ]
     own_rows = [own_out[0]] + [within(own_out[k], k) for k in range(1, half)]
-
-    def stack_of(rows, segment):
-        where = jnp.stack([segment, member, home, core]).astype(jnp.int32)
-        return segment_stack(rows, blocks, where, shape)
-
-    keep, send = stack_of(far_rows, (me + half) % size)
+    keep, send = segment_stack(far_rows, far_rows, other, half, shape)
     far = keep + lax.ppermute(send, "chan", swap)
     far, *own_rows = lax.optimization_barrier((far, *own_rows))
     far = lax.ppermute(far, "tm", across)
-    keep, send = stack_of(own_rows, me)
+    keep, send = segment_stack(own_rows, far_rows, other, 0, shape)
     total = keep + lax.ppermute(send, "chan", swap) + far
     return total[None]
 

time: 68.1 us -> 64.7 us (0.950)
  Pallas kernels: 26.3 us -> 22.4 us
  waiting for transfers between devices: 15.2 us -> 19.1 us
  other arithmetic: 5.15 us -> 2.51 us
    ppermute x1 -> x4, waiting for transfers between devices: 1.02 us -> 11.4 us  [local(): lax.ppermute(block, 'tm', [(i, i ^ k ^ half) for i in range(size)])]
    ppermute x9 -> x6, waiting for transfers between devices: 7.84 us -> 0.02 us  [within(): lax.ppermute(x, 'tm', [(i, i // half * half + (i % half ^ step)) for i in...]
    ppermute x1 -> x4, starting transfers between devices: 4.06 us -> 8.58 us  [local(): lax.ppermute(block, 'tm', [(i, i ^ k ^ half) for i in range(size)])]
    pallas_call x4 -> x3, Pallas kernels: 26.3 us -> 22.4 us  [the longest x2 17.6 us: segment_stack(): pl.pallas_call(functools.partial(segment_kernel, shape, ahead), out_shape...]
    ppermute x9 -> x6, starting transfers between devices: 11.7 us -> 8.13 us  [within(): lax.ppermute(x, 'tm', [(i, i // half * half + (i % half ^ step)) for i in...]
    another operation x3 -> x0, other arithmetic: 1.86 us -> none  [the longest x2 1.27 us: stack_of(): where = jnp.stack([segment, member, home, core]).astype(jnp.int32)]
    ppermute x1, starting transfers between devices: 2.86 us -> 1.81 us  [local(): far = lax.ppermute(far, 'tm', across)]
    ppermute x1, waiting for transfers between devices: 5.4 us -> 6.2 us  [local(): far = lax.ppermute(far, 'tm', across)]
  transfers between devices with their start and end apart: 13 -> 13, of which waited for: 5 -> 5; matrix products, arithmetic and copies ran while one was open for 4% -> 1% of each run, Pallas kernels for 16% -> 15%
where the time goes in v3:
time: 64.7 us; the launch traced here: 64.5 us
  Pallas kernels  22.4 us (35%)
  waiting for transfers between devices  19.1 us (30%)
  starting transfers between devices  18.8 us (29%)
  other arithmetic  2.51 us (4%)
  local copies, waits for them, and re-layouts  1.51 us (2%)
    pallas_call x2, Pallas kernels, segment_stack(): pl.pallas_call(functools.partial(segment_kernel, shape, ahead), out_shape...  17.6 us
    ppermute x4, waiting for transfers between devices, local(): lax.ppermute(block, 'tm', [(i, i ^ k ^ half) for i in range(size)])  11.4 us
    ppermute x4, starting transfers between devices, local(): lax.ppermute(block, 'tm', [(i, i ^ k ^ half) for i in range(size)])  8.58 us
    ppermute x6, starting transfers between devices, within(): lax.ppermute(x, 'tm', [(i, i // half * half + (i % half ^ step)) for i in...  8.13 us
    ppermute x1, waiting for transfers between devices, local(): far = lax.ppermute(far, 'tm', across)  6.2 us
    pallas_call x1, Pallas kernels, pack(): pl.pallas_call(functools.partial(pack_kernel, half, capacity), out_shape=...  4.83 us
    ppermute x1, starting transfers between devices, local(): far = lax.ppermute(far, 'tm', across)  1.81 us
    broadcast_in_dim x1, other arithmetic, local(): return total[None]  1.58 us
  transfers between devices with their start and end apart: 13, of which 5 were waited for; matrix products, arithmetic and copies ran while one was open for 1% of the time, Pallas kernels for 15%

profile of v3, /device:TPU:0, one launch (start us, length us, event | category | flops | bytes accessed | tf_op | source)
XLA Modules:
  0.0 64.5 jit_solution(1426033503631993244)
XLA Ops:
  0.0 4.8 %pack.1 = (f32[72,128]{1,0:T(8,128)}, f32[456,128]{1,0:T(8,128)}, f32[456,128]{1,0:T(8,128)}, f32[456,128]{1,0:T(8,128)}, f32[456,128]{1,0:T(8,128)}, /*index=5*...) custom-call(s32[96]{0:T(128)} %dest.1, s32[96]{0:T(128)} %chan.1, s32[96]{0:T(128)} %length.1, ...), custom_call_target="tpu_custom_call" | custom-call | tf_op jit(solution)/shard_map/pack/pallas_call | solution.py:160
  4.8 3.1 %collective-permute-start = (f32[456,128]{1,0:T(8,128)}, f32[456,128]{1,0:T(8,128)S(1)}, u32[]{:S(2)}, u32[]{:S(2)}) collective-permute-start(f32[456,128]{1,0:T(8,128)} %get-tuple-element.24), channel_id=1, source_target_pairs={{0,2},{2,0},{4,6},{6,4},{8,10},{10,8},{12,14},{14,12},{1,3},{3,1},... | collective-permute-start | bytes 700424 | tf_op jit(solution)/shard_map/ppermute | solution.py:432
  7.9 1.6 %collective-permute-start.1 = (f32[456,128]{1,0:T(8,128)}, f32[456,128]{1,0:T(8,128)S(1)}, u32[]{:S(2)}, u32[]{:S(2)}) collective-permute-start(f32[456,128]{1,0:T(8,128)} %get-tuple-element.25), channel_id=1, source_target_pairs={{0,4},{2,6},{4,0},{6,2},{8,12},{10,14},{12,8},{14,10},{1,5},{3,7},... | collective-permute-start | bytes 700424 | tf_op jit(solution)/shard_map/ppermute | solution.py:432
  9.5 0.0 collective-permute-start.2
  9.5 4.9 %collective-permute-start.6 = (f32[72,128]{1,0:T(8,128)}, f32[72,128]{1,0:T(8,128)S(1)}, u32[]{:S(2)}, u32[]{:S(2)}) collective-permute-start(f32[72,128]{1,0:T(8,128)} %get-tuple-element.27), channel_id=1, source_target_pairs={{0,14},{2,12},{4,10},{6,8},{8,6},{10,4},{12,2},{14,0},{1,15},{3,13... | collective-permute-start | bytes 110600 | tf_op jit(solution)/shard_map/ppermute | solution.py:442
  14.4 0.2 collective-permute-start.5
  14.6 8.8 %collective-permute-done.6.refs_7_.refs_11_ = f32[72,128]{1,0:T(8,128)S(1)} collective-permute-done((f32[72,128]{1,0:T(8,128)}, f32[72,128]{1,0:T(8,128)S(1)}, u32[]{:S(2)}, u32[]{:S(2)}) %collective-permute-start.6) | collective-permute-done | bytes 36896 | tf_op jit(solution)/shard_map/ppermute | solution.py:442
  23.4 0.0 copy-start.6
  23.4 0.0 collective-permute-start.4
  23.4 0.5 collective-permute-done.5.refs_6_.refs_10_
  23.9 0.0 copy-start.7
  23.9 3.4 %collective-permute-start.3 = (f32[72,128]{1,0:T(8,128)}, f32[72,128]{1,0:T(8,128)S(1)}, u32[]{:S(2)}, u32[]{:S(2)}) collective-permute-start(f32[72,128]{1,0:T(8,128)} %get-tuple-element.27), channel_id=1, source_target_pairs={{0,8},{2,10},{4,12},{6,14},{8,0},{10,2},{12,4},{14,6},{1,9},{3,11}... | collective-permute-start | bytes 110600 | tf_op jit(solution)/shard_map/ppermute | solution.py:442
  27.3 2.1 %collective-permute-done.4.refs_5_.refs_9_ = f32[72,128]{1,0:T(8,128)S(1)} collective-permute-done((f32[72,128]{1,0:T(8,128)}, f32[72,128]{1,0:T(8,128)S(1)}, u32[]{:S(2)}, u32[]{:S(2)}) %collective-permute-start.4) | collective-permute-done | bytes 36896 | tf_op jit(solution)/shard_map/ppermute | solution.py:442
  29.4 0.0 copy-start.8
  29.4 1.5 %collective-permute-start.8 = (f32[384,128]{1,0:T(8,128)}, f32[384,128]{1,0:T(8,128)S(1)}, u32[]{:S(2)}, u32[]{:S(2)}) collective-permute-start(f32[384,128]{1,0:T(8,128)} %get-tuple-element.31), channel_id=1, source_target_pairs={{0,2},{2,0},{4,6},{6,4},{8,10},{10,8},{12,14},{14,12},{1,3},{3,1},... | collective-permute-start | bytes 589832 | tf_op jit(solution)/shard_map/ppermute | solution.py:432
  30.9 0.0 collective-permute-done.3.refs_4_.refs_8_
  30.9 0.5 collective-permute-start.9
  31.5 0.0 collective-permute-done.refs_1_.refs_5_
  31.5 1.4 %collective-permute-start.10 = (f32[384,128]{1,0:T(8,128)}, f32[384,128]{1,0:T(8,128)S(1)}, u32[]{:S(2)}, u32[]{:S(2)}) collective-permute-start(f32[384,128]{1,0:T(8,128)} %get-tuple-element.33), channel_id=1, source_target_pairs={{0,6},{2,4},{4,2},{6,0},{8,14},{10,12},{12,10},{14,8},{1,7},{3,5},... | collective-permute-start | bytes 589832 | tf_op jit(solution)/shard_map/ppermute | solution.py:432
  32.9 0.0 collective-permute-done.1.refs_2_.refs_6_
  32.9 0.0 collective-permute-done.2.refs_3_.refs_7_
  32.9 0.0 copy-start.2
  32.9 0.0 copy-done.6
  33.0 0.0 copy-done.7
  33.0 0.0 copy-done.8
  33.0 0.0 copy-done.9
  33.0 0.0 copy-done
  33.0 0.6 copy-done.1
  33.6 0.1 copy-done.2
  33.7 9.5 %segment_stack.2 = (f32[4,4,1792]{2,1,0:T(4,128)}, f32[4,4,1792]{2,1,0:T(4,128)}) custom-call(f32[456,128]{1,0:T(8,128)} %get-tuple-element.23.refs_0_.refs_4_, f32[456,128]{1,0:T(8,128)} %copy-done, f32[456,128]{1,0:T(8,128)} %copy-done.1, f32[456,128]{1,0:T(8,128)} %copy-done.2, f32[72,128]{1,0:T(8,128)} %copy-done.9, f32[72,128]{1,0:T(8,128)} %copy-done.8, ...), custom_call_target="tpu_custom_call" | custom-call | tf_op jit(solution)/shard_map/segment_stack/pallas_call | solution.py:397
  43.2 0.1 collective-permute-start.7
  43.3 1.5 %collective-permute-done.7 = f32[4,4,1792]{2,1,0:T(4,128)S(1)} collective-permute-done((f32[4,4,1792]{2,1,0:T(4,128)}, f32[4,4,1792]{2,1,0:T(4,128)S(1)}, u32[]{:S(2)}, u32[]{:S(2)}) %collective-permute-start.7) | collective-permute-done | bytes 114720 | tf_op jit(solution)/shard_map/ppermute | solution.py:447
  44.8 0.9 %add.9 = f32[4,4,1792]{2,1,0:T(4,128)S(1)} add(f32[4,4,1792]{2,1,0:T(4,128)} %get-tuple-element.28, f32[4,4,1792]{2,1,0:T(4,128)S(1)} %collective-permute-done.7) | non-fusion elementwise | flops 28672 | bytes 344064 | tf_op jit(solution)/shard_map/add | solution.py:447
  45.7 0.0 collective-permute-done.8.refs_1_
  45.7 0.0 copy-start.3
  45.8 0.0 collective-permute-done.9.refs_2_
  45.8 0.0 copy-start.4
  45.8 0.0 collective-permute-done.10.refs_3_
  45.8 0.0 copy-start.5
  45.8 0.6 copy-done.3
  46.4 0.1 copy-done.4
  46.5 0.1 copy-done.5
  46.6 8.1 %segment_stack.3 = (f32[4,4,1792]{2,1,0:T(4,128)}, f32[4,4,1792]{2,1,0:T(4,128)}) custom-call(f32[384,128]{1,0:T(8,128)} %get-tuple-element.34.refs_0_, f32[384,128]{1,0:T(8,128)} %copy-done.3, f32[384,128]{1,0:T(8,128)} %copy-done.4, f32[384,128]{1,0:T(8,128)} %copy-done.5, f32[456,128]{1,0:T(8,128)} %get-tuple-element.23.refs_0_.refs_4_, ...), custom_call_target="tpu_custom_call" | custom-call | tf_op jit(solution)/shard_map/segment_stack/pallas_call | solution.py:397
  54.7 0.2 collective-permute-start.11
  54.9 1.8 %collective-permute-start.12 = (f32[4,4,1792]{2,1,0:T(4,128)S(1)}, f32[4,4,1792]{2,1,0:T(4,128)S(1)}, u32[]{:S(2)}, u32[]{:S(2)}) collective-permute-start(f32[4,4,1792]{2,1,0:T(4,128)S(1)} %add.9), channel_id=1, source_target_pairs={{0,8},{2,10},{4,12},{6,14},{8,0},{10,2},{12,4},{14,6},{1,9},{3,11}... | collective-permute-start | bytes 344072 | tf_op jit(solution)/shard_map/ppermute | solution.py:449
  56.7 0.0 collective-permute-done.11
  56.7 6.2 %collective-permute-done.12 = f32[4,4,1792]{2,1,0:T(4,128)S(1)} collective-permute-done((f32[4,4,1792]{2,1,0:T(4,128)S(1)}, f32[4,4,1792]{2,1,0:T(4,128)S(1)}, u32[]{:S(2)}, u32[]{:S(2)}) %collective-permute-start.12) | collective-permute-done | bytes 114720 | tf_op jit(solution)/shard_map/ppermute | solution.py:449
  62.9 1.6 %add_bitcast_fusion = f32[1,4,4,1792]{3,2,1,0:T(4,128)} fusion(f32[4,4,1792]{2,1,0:T(4,128)S(1)} %collective-permute-done.12, f32[4,4,1792]{2,1,0:T(4,128)} %get-tuple-element.38, f32[4,4,1792]{2,1,0:T(4,128)S(1)} %collective-permute-done.11), kind=kLoop, calls=%fused_computation | loop fusion | flops 57344 | bytes 458752 | tf_op jit(solution)/shard_map/broadcast_in_dim | solution.py:452
  (3 shorter events, 0.0 us)
Async XLA Ops:
  4.8 26.6 %collective-permute-start = (f32[456,128]{1,0:T(8,128)}, f32[456,128]{1,0:T(8,128)S(1)}, u32[]{:S(2)}, u32[]{:S(2)}) collective-permute-start(f32[456,128]{1,0:T(8,128)} %get-tuple-element.24), channel_id=1, source_target_pairs={{0,2},{2,0},{4,6},{6,4},{8,10},{10,8},{12,14},{14,12},{1,3},{3,1},... | collective-permute-start | bytes 700424 | tf_op jit(solution)/shard_map/ppermute | solution.py:432
  7.9 25.0 %collective-permute-start.1 = (f32[456,128]{1,0:T(8,128)}, f32[456,128]{1,0:T(8,128)S(1)}, u32[]{:S(2)}, u32[]{:S(2)}) collective-permute-start(f32[456,128]{1,0:T(8,128)} %get-tuple-element.25), channel_id=1, source_target_pairs={{0,4},{2,6},{4,0},{6,2},{8,12},{10,14},{12,8},{14,10},{1,5},{3,7},... | collective-permute-start | bytes 700424 | tf_op jit(solution)/shard_map/ppermute | solution.py:432
  9.5 23.5 %collective-permute-start.2 = (f32[456,128]{1,0:T(8,128)}, f32[456,128]{1,0:T(8,128)S(1)}, u32[]{:S(2)}, u32[]{:S(2)}) collective-permute-start(f32[456,128]{1,0:T(8,128)} %get-tuple-element.26), channel_id=1, source_target_pairs={{0,6},{2,4},{4,2},{6,0},{8,14},{10,12},{12,10},{14,8},{1,7},{3,5},... | collective-permute-start | bytes 700424 | tf_op jit(solution)/shard_map/ppermute | solution.py:432
  9.5 13.9 %collective-permute-start.6 = (f32[72,128]{1,0:T(8,128)}, f32[72,128]{1,0:T(8,128)S(1)}, u32[]{:S(2)}, u32[]{:S(2)}) collective-permute-start(f32[72,128]{1,0:T(8,128)} %get-tuple-element.27), channel_id=1, source_target_pairs={{0,14},{2,12},{4,10},{6,8},{8,6},{10,4},{12,2},{14,0},{1,15},{3,13... | collective-permute-start | bytes 110600 | tf_op jit(solution)/shard_map/ppermute | solution.py:442
  14.4 9.5 %collective-permute-start.5 = (f32[72,128]{1,0:T(8,128)}, f32[72,128]{1,0:T(8,128)S(1)}, u32[]{:S(2)}, u32[]{:S(2)}) collective-permute-start(f32[72,128]{1,0:T(8,128)} %get-tuple-element.27), channel_id=1, source_target_pairs={{0,12},{2,14},{4,8},{6,10},{8,4},{10,6},{12,0},{14,2},{1,13},{3,15... | collective-permute-start | bytes 110600 | tf_op jit(solution)/shard_map/ppermute | solution.py:442
  23.4 9.5 %copy-start.6 = (f32[72,128]{1,0:T(8,128)}, f32[72,128]{1,0:T(8,128)S(1)}, u32[]{:S(2)}) copy-start(f32[72,128]{1,0:T(8,128)S(1)} %collective-permute-done.6.refs_7_.refs_11_) | copy-start | bytes 110596
  23.4 6.0 %collective-permute-start.4 = (f32[72,128]{1,0:T(8,128)}, f32[72,128]{1,0:T(8,128)S(1)}, u32[]{:S(2)}, u32[]{:S(2)}) collective-permute-start(f32[72,128]{1,0:T(8,128)} %get-tuple-element.27), channel_id=1, source_target_pairs={{0,10},{2,8},{4,14},{6,12},{8,2},{10,0},{12,6},{14,4},{1,11},{3,9}... | collective-permute-start | bytes 110600 | tf_op jit(solution)/shard_map/ppermute | solution.py:442
  23.9 9.1 %copy-start.7 = (f32[72,128]{1,0:T(8,128)}, f32[72,128]{1,0:T(8,128)S(1)}, u32[]{:S(2)}) copy-start(f32[72,128]{1,0:T(8,128)S(1)} %collective-permute-done.5.refs_6_.refs_10_) | copy-start | bytes 110596
  23.9 7.1 %collective-permute-start.3 = (f32[72,128]{1,0:T(8,128)}, f32[72,128]{1,0:T(8,128)S(1)}, u32[]{:S(2)}, u32[]{:S(2)}) collective-permute-start(f32[72,128]{1,0:T(8,128)} %get-tuple-element.27), channel_id=1, source_target_pairs={{0,8},{2,10},{4,12},{6,14},{8,0},{10,2},{12,4},{14,6},{1,9},{3,11}... | collective-permute-start | bytes 110600 | tf_op jit(solution)/shard_map/ppermute | solution.py:442
  29.4 3.5 %copy-start.8 = (f32[72,128]{1,0:T(8,128)}, f32[72,128]{1,0:T(8,128)S(1)}, u32[]{:S(2)}) copy-start(f32[72,128]{1,0:T(8,128)S(1)} %collective-permute-done.4.refs_5_.refs_9_) | copy-start | bytes 110596
  29.4 16.3 %collective-permute-start.8 = (f32[384,128]{1,0:T(8,128)}, f32[384,128]{1,0:T(8,128)S(1)}, u32[]{:S(2)}, u32[]{:S(2)}) collective-permute-start(f32[384,128]{1,0:T(8,128)} %get-tuple-element.31), channel_id=1, source_target_pairs={{0,2},{2,0},{4,6},{6,4},{8,10},{10,8},{12,14},{14,12},{1,3},{3,1},... | collective-permute-start | bytes 589832 | tf_op jit(solution)/shard_map/ppermute | solution.py:432
  30.9 2.0 %copy-start.9 = (f32[72,128]{1,0:T(8,128)}, f32[72,128]{1,0:T(8,128)S(1)}, u32[]{:S(2)}) copy-start(f32[72,128]{1,0:T(8,128)S(1)} %collective-permute-done.3.refs_4_.refs_8_) | copy-start | bytes 110596
  30.9 14.8 %collective-permute-start.9 = (f32[384,128]{1,0:T(8,128)}, f32[384,128]{1,0:T(8,128)S(1)}, u32[]{:S(2)}, u32[]{:S(2)}) collective-permute-start(f32[384,128]{1,0:T(8,128)} %get-tuple-element.32), channel_id=1, source_target_pairs={{0,4},{2,6},{4,0},{6,2},{8,12},{10,14},{12,8},{14,10},{1,5},{3,7},... | collective-permute-start | bytes 589832 | tf_op jit(solution)/shard_map/ppermute | solution.py:432
  31.5 1.5 %copy-start = (f32[456,128]{1,0:T(8,128)}, f32[456,128]{1,0:T(8,128)S(1)}, u32[]{:S(2)}) copy-start(f32[456,128]{1,0:T(8,128)S(1)} %collective-permute-done.refs_1_.refs_5_) | copy-start | bytes 700420
  31.5 14.3 %collective-permute-start.10 = (f32[384,128]{1,0:T(8,128)}, f32[384,128]{1,0:T(8,128)S(1)}, u32[]{:S(2)}, u32[]{:S(2)}) collective-permute-start(f32[384,128]{1,0:T(8,128)} %get-tuple-element.33), channel_id=1, source_target_pairs={{0,6},{2,4},{4,2},{6,0},{8,14},{10,12},{12,10},{14,8},{1,7},{3,5},... | collective-permute-start | bytes 589832 | tf_op jit(solution)/shard_map/ppermute | solution.py:432
  32.9 0.7 %copy-start.1 = (f32[456,128]{1,0:T(8,128)}, f32[456,128]{1,0:T(8,128)S(1)}, u32[]{:S(2)}) copy-start(f32[456,128]{1,0:T(8,128)S(1)} %collective-permute-done.1.refs_2_.refs_6_) | copy-start | bytes 700420
  32.9 0.8 %copy-start.2 = (f32[456,128]{1,0:T(8,128)}, f32[456,128]{1,0:T(8,128)S(1)}, u32[]{:S(2)}) copy-start(f32[456,128]{1,0:T(8,128)S(1)} %collective-permute-done.2.refs_3_.refs_7_) | copy-start | bytes 700420
  43.2 1.6 %collective-permute-start.7 = (f32[4,4,1792]{2,1,0:T(4,128)}, f32[4,4,1792]{2,1,0:T(4,128)S(1)}, u32[]{:S(2)}, u32[]{:S(2)}) collective-permute-start(f32[4,4,1792]{2,1,0:T(4,128)} %get-tuple-element.29), channel_id=1, source_target_pairs={{0,1},{1,0},{2,3},{3,2},{4,5},{5,4},{6,7},{7,6},{8,9},{9,8},{10,11... | collective-permute-start | bytes 344072 | tf_op jit(solution)/shard_map/ppermute | solution.py:447
  45.7 0.7 %copy-start.3 = (f32[384,128]{1,0:T(8,128)}, f32[384,128]{1,0:T(8,128)S(1)}, u32[]{:S(2)}) copy-start(f32[384,128]{1,0:T(8,128)S(1)} %collective-permute-done.8.refs_1_) | copy-start | bytes 589828
  45.8 0.7 %copy-start.4 = (f32[384,128]{1,0:T(8,128)}, f32[384,128]{1,0:T(8,128)S(1)}, u32[]{:S(2)}) copy-start(f32[384,128]{1,0:T(8,128)S(1)} %collective-permute-done.9.refs_2_) | copy-start | bytes 589828
  45.8 0.8 %copy-start.5 = (f32[384,128]{1,0:T(8,128)}, f32[384,128]{1,0:T(8,128)S(1)}, u32[]{:S(2)}) copy-start(f32[384,128]{1,0:T(8,128)S(1)} %collective-permute-done.10.refs_3_) | copy-start | bytes 589828
  54.7 2.0 %collective-permute-start.11 = (f32[4,4,1792]{2,1,0:T(4,128)}, f32[4,4,1792]{2,1,0:T(4,128)S(1)}, u32[]{:S(2)}, u32[]{:S(2)}) collective-permute-start(f32[4,4,1792]{2,1,0:T(4,128)} %get-tuple-element.39), channel_id=1, source_target_pairs={{0,1},{1,0},{2,3},{3,2},{4,5},{5,4},{6,7},{7,6},{8,9},{9,8},{10,11... | collective-permute-start | bytes 344072 | tf_op jit(solution)/shard_map/ppermute | solution.py:451
  54.9 8.0 %collective-permute-start.12 = (f32[4,4,1792]{2,1,0:T(4,128)S(1)}, f32[4,4,1792]{2,1,0:T(4,128)S(1)}, u32[]{:S(2)}, u32[]{:S(2)}) collective-permute-start(f32[4,4,1792]{2,1,0:T(4,128)S(1)} %add.9), channel_id=1, source_target_pairs={{0,8},{2,10},{4,12},{6,14},{8,0},{10,2},{12,4},{14,6},{1,9},{3,11}... | collective-permute-start | bytes 344072 | tf_op jit(solution)/shard_map/ppermute | solution.py:449

commit v4 on v3

--- a/solution.py
+++ b/solution.py
@@ -26,6 +26,15 @@
 
 SMEM = pl.BlockSpec(memory_space=pltpu.SMEM)
 VMEM = pl.BlockSpec(memory_space=pltpu.VMEM)
+KERNEL_BYTES = 24 << 20
+
+
+def in_main(arrays):
+    return [pltpu.with_memory_space_constraint(x, pltpu.HBM) for x in arrays]
+
+
+def on_chip(arrays):
+    return [pltpu.with_memory_space_constraint(x, pltpu.VMEM) for x in arrays]
 
 
 def split(x):
@@ -36,7 +45,7 @@
 def pack_kernel(half, capacity, dest, chan, length, rec, templ, templ_chan, templ_off, *refs):
     block_out = refs[0]
     outs = refs[1 : 2 * half + 1]
-    count, source, raw, rows, stage, in_sems, out_sems = refs[2 * half + 1 :]
+    count, source, raw, rows, in_sems = refs[2 * half + 1 :]
     slot_count = dest.shape[0]
     blocks = rec.shape[1] // LANES
     me = lax.axis_index("tm")
@@ -91,10 +100,9 @@
         jnp.int32, (blocks, LANES), 1
     )
     last = blocks * LANES - 1
-    leaving = []
     for group, out in enumerate(outs):
 
-        def emit(i, c, group=group):
+        def emit(i, c, group=group, out=out):
             r = source[group * capacity + i]
             used = r >= 0
             row = jnp.maximum(r, 0)
@@ -102,18 +110,13 @@
             tag = jnp.where(used, chan[row], -1).astype(jnp.float32)
             tile = rows[pl.ds(pl.multiple_of(row * blocks, blocks), blocks), :]
             tile = jnp.where(flat < limit, tile, 0.0)
-            stage[group, i * blocks : (i + 1) * blocks, :] = jnp.where(flat == last, tag, tile)
+            out[i * blocks : (i + 1) * blocks, :] = jnp.where(flat == last, tag, tile)
             return c
 
         for i in range(capacity):
             emit(i, 0)
         if group < half:
-            stage[group, capacity * blocks :, :] = block_out[...]
-        part = stage.at[group, pl.ds(0, out.shape[0])]
-        leaving.append(pltpu.make_async_copy(part, out, out_sems.at[group]))
-        leaving[-1].start()
-    for copy in leaving:
-        copy.wait()
+            out[capacity * blocks :, :] = block_out[...]
 
 
 def write_unit(templ, chan, off, out):
@@ -154,27 +157,26 @@
     per_block, half_taps, taps = templates.shape
     block_rows = (taps // LANES) * per_block * half_taps + SUB
     pieces = 4 if slot_count % (4 * SUB) == 0 else 1
-    far = jax.ShapeDtypeStruct((capacity * blocks + block_rows, LANES), jnp.float32)
-    own = jax.ShapeDtypeStruct((capacity * blocks, LANES), jnp.float32)
+    far = pltpu.VMEM((capacity * blocks + block_rows, LANES), jnp.float32)
+    own = pltpu.VMEM((capacity * blocks, LANES), jnp.float32)
     whole = pl.BlockSpec(memory_space=pl.ANY)
     block, *outs = pl.pallas_call(
         functools.partial(pack_kernel, half, capacity),
-        out_shape=[jax.ShapeDtypeStruct((block_rows, LANES), jnp.float32)]
+        out_shape=[pltpu.VMEM((block_rows, LANES), jnp.float32)]
         + [far] * half
         + [own] * half,
         in_specs=[SMEM] * 3 + [whole] + [VMEM] * 3,
-        out_specs=[VMEM] + [whole] * (2 * half),
+        out_specs=[VMEM] * (2 * half + 1),
         scratch_shapes=[
             pltpu.SMEM((2 * half + 1,), jnp.int32),
             pltpu.SMEM((slot_count + 1,), jnp.int32),
             pltpu.VMEM((slot_count, sample_count), jnp.float32),
             pltpu.VMEM((slot_count * blocks, LANES), jnp.float32),
-            pltpu.VMEM((2 * half, capacity * blocks + block_rows, LANES), jnp.float32),
             pltpu.SemaphoreType.DMA((pieces,)),
-            pltpu.SemaphoreType.DMA((2 * half,)),
         ],
+        compiler_params=pltpu.CompilerParams(vmem_limit_bytes=KERNEL_BYTES),
         name="pack",
-    )(row_dest, row_chan, row_len, records, templates, tmpl_chan, tmpl_off)
+    )(*in_main((row_dest, row_chan, row_len, records, templates, tmpl_chan, tmpl_off)))
     return block, outs[:half], outs[half:]
 
 
@@ -201,21 +203,13 @@
     stack_gain = (taps * TCH) ** 0.5 / TCH
 
     part_rows = capacity * blocks
-    copies = []
     for k in range(parts):
         index = jnp.bitwise_xor(member, k)
-        moves = (
-            (rows_in[k].at[pl.ds(0, part_rows)], x_sc.at[pl.ds(k * part_rows, part_rows)]),
-            (near_in[k].at[pl.ds(part_rows, block_rows)], u_sc.at[home * parts + index]),
-            (other_in[k], u_sc.at[(1 - home) * parts + index]),
-        )
-        for source, target in moves:
-            copies.append(pltpu.make_async_copy(source, target, sems.at[1 + len(copies)]))
-            copies[-1].start()
+        x_sc[k * part_rows : (k + 1) * part_rows, :] = rows_in[k][:part_rows, :]
+        u_sc[home * parts + index] = near_in[k][part_rows:, :]
+        u_sc[(1 - home) * parts + index] = other_in[k][...]
     x_sc[rows:, :] = jnp.zeros((SUB, LANES), jnp.float32)
     acc[...] = jnp.zeros_like(acc)
-    for copy in copies:
-        copy.wait()
 
     lane_p = lax.broadcasted_iota(jnp.int32, (1, LANES), 1)
     chan_of = jnp.zeros((1, LANES), jnp.float32)
@@ -392,12 +386,12 @@
     pair_count = stack_count * half_taps
     chunk = (SUB if slot_count % SUB == 0 else 1) * blocks
     block_rows = other[0].shape[0]
-    out = jax.ShapeDtypeStruct((STOPS, per_block, lags // 2), jnp.float32)
+    out = pltpu.VMEM((STOPS, per_block, lags // 2), jnp.float32)
     operands = list(rows) + ([] if near is rows else list(near)) + list(other)
     return pl.pallas_call(
         functools.partial(segment_kernel, shape, ahead),
         out_shape=(out, out),
-        in_specs=[pl.BlockSpec(memory_space=pltpu.HBM)] * len(operands),
+        in_specs=[VMEM] * len(operands),
         out_specs=(VMEM, VMEM),
         scratch_shapes=[
             pltpu.VMEM((slot_count * blocks + SUB, LANES), jnp.float32),
@@ -411,10 +405,11 @@
             pltpu.VMEM((SUB, LANES), jnp.int32),
             pltpu.SMEM((SUB, LANES), jnp.int32),
             pltpu.SMEM((pair_count + UNROLL,), jnp.int32),
-            pltpu.SemaphoreType.DMA((3 * parts + 1,)),
+            pltpu.SemaphoreType.DMA((1,)),
         ],
+        compiler_params=pltpu.CompilerParams(vmem_limit_bytes=KERNEL_BYTES),
         name="segment_stack",
-    )(*operands)
+    )(*on_chip(operands))
 
 
 def local(records, row_dest, row_chan, row_len, templates, tmpl_chan, tmpl_off):

time: 64.7 us -> 55 us (0.85)
  Pallas kernels: 22.4 us -> 16.8 us
  other arithmetic: 2.51 us -> 0.72 us
  local copies, waits for them, and re-layouts: 1.51 us -> 0 us
    pallas_call x2, Pallas kernels: 17.6 us -> 13.6 us  [segment_stack(): pl.pallas_call(functools.partial(segment_kernel, shape, ahead), out_shape...]
    pallas_call x1, Pallas kernels: 4.83 us -> 3.19 us  [pack(): pl.pallas_call(functools.partial(pack_kernel, half, capacity), out_shape=...]
    unnamed x20 -> x0, local copies, waits for them, and re-layouts: 1.51 us -> none
    add x1, other arithmetic: 0.93 us -> 0.03 us  [local(): far = keep + lax.ppermute(send, 'chan', swap)]
    broadcast_in_dim x1, other arithmetic: 1.58 us -> 0.69 us  [local(): return total[None]]
  transfers between devices with their start and end apart: 13 -> 13, of which waited for: 5 -> 5; matrix products, arithmetic and copies ran while one was open for 1% -> 0% of each run, Pallas kernels for 15% -> 14%
where the time goes in v4:
time: 55 us; the launch traced here: 54.8 us
  waiting for transfers between devices  18.7 us (34%)
  starting transfers between devices  18.5 us (34%)
  Pallas kernels  16.8 us (31%)
  other arithmetic  0.72 us (1%)
    pallas_call x2, Pallas kernels, segment_stack(): pl.pallas_call(functools.partial(segment_kernel, shape, ahead), out_shape...  13.6 us
    ppermute x4, waiting for transfers between devices, local(): lax.ppermute(block, 'tm', [(i, i ^ k ^ half) for i in range(size)])  11.2 us
    ppermute x4, starting transfers between devices, local(): lax.ppermute(block, 'tm', [(i, i ^ k ^ half) for i in range(size)])  8.37 us
    ppermute x6, starting transfers between devices, within(): lax.ppermute(x, 'tm', [(i, i // half * half + (i % half ^ step)) for i in...  8.13 us
    ppermute x1, waiting for transfers between devices, local(): far = lax.ppermute(far, 'tm', across)  6.2 us
    pallas_call x1, Pallas kernels, pack(): pl.pallas_call(functools.partial(pack_kernel, half, capacity), out_shape=...  3.19 us
    ppermute x1, starting transfers between devices, local(): far = lax.ppermute(far, 'tm', across)  1.76 us
    ppermute x1, waiting for transfers between devices, local(): far = keep + lax.ppermute(send, 'chan', swap)  1.31 us
  transfers between devices with their start and end apart: 13, of which 5 were waited for; matrix products, arithmetic and copies ran while one was open for 0% of the time, Pallas kernels for 14%

profile of v4, /device:TPU:0, one launch (start us, length us, event | category | flops | bytes accessed | tf_op | source)
XLA Modules:
  0.0 54.8 jit_solution(4567049445051912405)
XLA Ops:
  0.0 3.2 %pack.1 = (f32[72,128]{1,0:T(8,128)S(1)}, f32[456,128]{1,0:T(8,128)S(1)}, f32[456,128]{1,0:T(8,128)S(1)}, f32[456,128]{1,0:T(8,128)S(1)}, f32[456,128]{1,0:T(8,1...) custom-call(s32[96]{0:T(128)} %dest.1, s32[96]{0:T(128)} %chan.1, ...), custom_call_target="tpu_custom_call" | custom-call | tf_op jit(solution)/shard_map/pack/pallas_call | solution.py:163
  3.2 3.1 %collective-permute-start = (f32[456,128]{1,0:T(8,128)S(1)}, f32[456,128]{1,0:T(8,128)S(1)}, u32[]{:S(2)}, u32[]{:S(2)}) collective-permute-start(f32[456,128]{1,0:T(8,128)S(1)} %get-tuple-element.24), channel_id=1, source_target_pairs={{0,2},{2,0},{4,6},{6,4},{8,10},{10,8},{12,14},{14,12},{1,3},{3,1},... | collective-permute-start | bytes 700424 | tf_op jit(solution)/shard_map/ppermute | solution.py:427
  6.3 1.6 %collective-permute-start.1 = (f32[456,128]{1,0:T(8,128)S(1)}, f32[456,128]{1,0:T(8,128)S(1)}, u32[]{:S(2)}, u32[]{:S(2)}) collective-permute-start(f32[456,128]{1,0:T(8,128)S(1)} %get-tuple-element.25), channel_id=1, source_target_pairs={{0,4},{2,6},{4,0},{6,2},{8,12},{10,14},{12,8},{14,10},{1,5},{3,7},... | collective-permute-start | bytes 700424 | tf_op jit(solution)/shard_map/ppermute | solution.py:427
  7.8 0.0 collective-permute-start.2
  7.8 4.9 %collective-permute-start.6 = (f32[72,128]{1,0:T(8,128)S(1)}, f32[72,128]{1,0:T(8,128)S(1)}, u32[]{:S(2)}, u32[]{:S(2)}) collective-permute-start(f32[72,128]{1,0:T(8,128)S(1)} %get-tuple-element.27), channel_id=1, source_target_pairs={{0,14},{2,12},{4,10},{6,8},{8,6},{10,4},{12,2},{14,0},{1,15},{3,13... | collective-permute-start | bytes 110600 | tf_op jit(solution)/shard_map/ppermute | solution.py:437
  12.8 0.2 collective-permute-start.5
  13.0 8.6 %collective-permute-done.6.refs_7_.refs_11_ = f32[72,128]{1,0:T(8,128)S(1)} collective-permute-done((f32[72,128]{1,0:T(8,128)S(1)}, f32[72,128]{1,0:T(8,128)S(1)}, u32[]{:S(2)}, u32[]{:S(2)}) %collective-permute-start.6) | collective-permute-done | bytes 36896 | tf_op jit(solution)/shard_map/ppermute | solution.py:437
  21.6 0.0 collective-permute-start.4
  21.6 0.7 %collective-permute-done.5.refs_6_.refs_10_ = f32[72,128]{1,0:T(8,128)S(1)} collective-permute-done((f32[72,128]{1,0:T(8,128)S(1)}, f32[72,128]{1,0:T(8,128)S(1)}, u32[]{:S(2)}, u32[]{:S(2)}) %collective-permute-start.5) | collective-permute-done | bytes 36896 | tf_op jit(solution)/shard_map/ppermute | solution.py:437
  22.3 3.2 %collective-permute-start.3 = (f32[72,128]{1,0:T(8,128)S(1)}, f32[72,128]{1,0:T(8,128)S(1)}, u32[]{:S(2)}, u32[]{:S(2)}) collective-permute-start(f32[72,128]{1,0:T(8,128)S(1)} %get-tuple-element.27), channel_id=1, source_target_pairs={{0,8},{2,10},{4,12},{6,14},{8,0},{10,2},{12,4},{14,6},{1,9},{3,11}... | collective-permute-start | bytes 110600 | tf_op jit(solution)/shard_map/ppermute | solution.py:437
  25.5 2.0 %collective-permute-done.4.refs_5_.refs_9_ = f32[72,128]{1,0:T(8,128)S(1)} collective-permute-done((f32[72,128]{1,0:T(8,128)S(1)}, f32[72,128]{1,0:T(8,128)S(1)}, u32[]{:S(2)}, u32[]{:S(2)}) %collective-permute-start.4) | collective-permute-done | bytes 36896 | tf_op jit(solution)/shard_map/ppermute | solution.py:437
  27.4 1.5 %collective-permute-start.8 = (f32[384,128]{1,0:T(8,128)S(1)}, f32[384,128]{1,0:T(8,128)S(1)}, u32[]{:S(2)}, u32[]{:S(2)}) collective-permute-start(f32[384,128]{1,0:T(8,128)S(1)} %get-tuple-element.31), channel_id=1, source_target_pairs={{0,2},{2,0},{4,6},{6,4},{8,10},{10,8},{12,14},{14,12},{1,3},{3,1},... | collective-permute-start | bytes 589832 | tf_op jit(solution)/shard_map/ppermute | solution.py:427
  28.9 0.0 collective-permute-done.3.refs_4_.refs_8_
  29.0 0.4 collective-permute-start.9
  29.4 0.0 collective-permute-done.refs_1_.refs_5_
  29.4 1.5 %collective-permute-start.10 = (f32[384,128]{1,0:T(8,128)S(1)}, f32[384,128]{1,0:T(8,128)S(1)}, u32[]{:S(2)}, u32[]{:S(2)}) collective-permute-start(f32[384,128]{1,0:T(8,128)S(1)} %get-tuple-element.33), channel_id=1, source_target_pairs={{0,6},{2,4},{4,2},{6,0},{8,14},{10,12},{12,10},{14,8},{1,7},{3,5},... | collective-permute-start | bytes 589832 | tf_op jit(solution)/shard_map/ppermute | solution.py:427
  30.9 0.0 collective-permute-done.1.refs_2_.refs_6_
  30.9 0.0 collective-permute-done.2.refs_3_.refs_7_
  30.9 7.5 %segment_stack.2 = (f32[4,4,1792]{2,1,0:T(4,128)S(1)}, f32[4,4,1792]{2,1,0:T(4,128)S(1)}) custom-call(f32[456,128]{1,0:T(8,128)S(1)} %get-tuple-element.23.refs_0_.refs_4_, f32[456,128]{1,0:T(8,128)S(1)} %collective-permute-done.refs_1_.refs_5_, f32[456,128]{1,0:T(8,128)S(1)} %collective-permute-done.1.refs_2_.refs_6_, ...), custom_call_target="tpu_custom_call" | custom-call | tf_op jit(solution)/shard_map/segment_stack/pallas_call | solution.py:391
  38.4 0.1 collective-permute-start.7
  38.5 1.3 %collective-permute-done.7 = f32[4,4,1792]{2,1,0:T(4,128)S(1)} collective-permute-done((f32[4,4,1792]{2,1,0:T(4,128)S(1)}, f32[4,4,1792]{2,1,0:T(4,128)S(1)}, u32[]{:S(2)}, u32[]{:S(2)}) %collective-permute-start.7) | collective-permute-done | bytes 114720 | tf_op jit(solution)/shard_map/ppermute | solution.py:442
  39.8 0.0 collective-permute-done.8.refs_1_
  39.9 0.0 collective-permute-done.9.refs_2_
  39.9 0.0 collective-permute-done.10.refs_3_
  39.9 6.1 %segment_stack.3 = (f32[4,4,1792]{2,1,0:T(4,128)S(1)}, f32[4,4,1792]{2,1,0:T(4,128)S(1)}) custom-call(f32[384,128]{1,0:T(8,128)S(1)} %get-tuple-element.34.refs_0_, f32[384,128]{1,0:T(8,128)S(1)} %collective-permute-done.8.refs_1_, f32[384,128]{1,0:T(8,128)S(1)} %collective-permute-done.9.refs_2_, f32[384,128]{1,0:T(8,128)S(1)} %collective-permute-done.10.refs_3_, ...), custom_call_target="tpu_custom_call" | custom-call | tf_op jit(solution)/shard_map/segment_stack/pallas_call | solution.py:391
  46.0 0.2 collective-permute-start.11
  46.2 1.8 %collective-permute-start.12 = (f32[4,4,1792]{2,1,0:T(4,128)S(1)}, f32[4,4,1792]{2,1,0:T(4,128)S(1)}, u32[]{:S(2)}, u32[]{:S(2)}) collective-permute-start(f32[4,4,1792]{2,1,0:T(4,128)S(1)} %add.9), channel_id=1, source_target_pairs={{0,8},{2,10},{4,12},{6,14},{8,0},{10,2},{12,4},{14,6},{1,9},{3,11}... | collective-permute-start | bytes 344072 | tf_op jit(solution)/shard_map/ppermute | solution.py:444
  48.0 0.0 collective-permute-done.11
  48.0 6.2 %collective-permute-done.12 = f32[4,4,1792]{2,1,0:T(4,128)S(1)} collective-permute-done((f32[4,4,1792]{2,1,0:T(4,128)S(1)}, f32[4,4,1792]{2,1,0:T(4,128)S(1)}, u32[]{:S(2)}, u32[]{:S(2)}) %collective-permute-start.12) | collective-permute-done | bytes 114720 | tf_op jit(solution)/shard_map/ppermute | solution.py:444
  54.2 0.7 %add_bitcast_fusion = f32[1,4,4,1792]{3,2,1,0:T(4,128)} fusion(f32[4,4,1792]{2,1,0:T(4,128)S(1)} %collective-permute-done.12, f32[4,4,1792]{2,1,0:T(4,128)S(1)} %get-tuple-element.38, f32[4,4,1792]{2,1,0:T(4,128)S(1)} %collective-permute-done.11), kind=kLoop, calls=%fused_computation | loop fusion | flops 57344 | bytes 458752 | tf_op jit(solution)/shard_map/broadcast_in_dim | solution.py:447
  (1 shorter events, 0.0 us)
Async XLA Ops:
  3.2 26.2 %collective-permute-start = (f32[456,128]{1,0:T(8,128)S(1)}, f32[456,128]{1,0:T(8,128)S(1)}, u32[]{:S(2)}, u32[]{:S(2)}) collective-permute-start(f32[456,128]{1,0:T(8,128)S(1)} %get-tuple-element.24), channel_id=1, source_target_pairs={{0,2},{2,0},{4,6},{6,4},{8,10},{10,8},{12,14},{14,12},{1,3},{3,1},... | collective-permute-start | bytes 700424 | tf_op jit(solution)/shard_map/ppermute | solution.py:427
  6.3 24.7 %collective-permute-start.1 = (f32[456,128]{1,0:T(8,128)S(1)}, f32[456,128]{1,0:T(8,128)S(1)}, u32[]{:S(2)}, u32[]{:S(2)}) collective-permute-start(f32[456,128]{1,0:T(8,128)S(1)} %get-tuple-element.25), channel_id=1, source_target_pairs={{0,4},{2,6},{4,0},{6,2},{8,12},{10,14},{12,8},{14,10},{1,5},{3,7},... | collective-permute-start | bytes 700424 | tf_op jit(solution)/shard_map/ppermute | solution.py:427
  7.8 23.1 %collective-permute-start.2 = (f32[456,128]{1,0:T(8,128)S(1)}, f32[456,128]{1,0:T(8,128)S(1)}, u32[]{:S(2)}, u32[]{:S(2)}) collective-permute-start(f32[456,128]{1,0:T(8,128)S(1)} %get-tuple-element.26), channel_id=1, source_target_pairs={{0,6},{2,4},{4,2},{6,0},{8,14},{10,12},{12,10},{14,8},{1,7},{3,5},... | collective-permute-start | bytes 700424 | tf_op jit(solution)/shard_map/ppermute | solution.py:427
  7.8 13.7 %collective-permute-start.6 = (f32[72,128]{1,0:T(8,128)S(1)}, f32[72,128]{1,0:T(8,128)S(1)}, u32[]{:S(2)}, u32[]{:S(2)}) collective-permute-start(f32[72,128]{1,0:T(8,128)S(1)} %get-tuple-element.27), channel_id=1, source_target_pairs={{0,14},{2,12},{4,10},{6,8},{8,6},{10,4},{12,2},{14,0},{1,15},{3,13... | collective-permute-start | bytes 110600 | tf_op jit(solution)/shard_map/ppermute | solution.py:437
  12.8 9.5 %collective-permute-start.5 = (f32[72,128]{1,0:T(8,128)S(1)}, f32[72,128]{1,0:T(8,128)S(1)}, u32[]{:S(2)}, u32[]{:S(2)}) collective-permute-start(f32[72,128]{1,0:T(8,128)S(1)} %get-tuple-element.27), channel_id=1, source_target_pairs={{0,12},{2,14},{4,8},{6,10},{8,4},{10,6},{12,0},{14,2},{1,13},{3,15... | collective-permute-start | bytes 110600 | tf_op jit(solution)/shard_map/ppermute | solution.py:437
  21.6 5.9 %collective-permute-start.4 = (f32[72,128]{1,0:T(8,128)S(1)}, f32[72,128]{1,0:T(8,128)S(1)}, u32[]{:S(2)}, u32[]{:S(2)}) collective-permute-start(f32[72,128]{1,0:T(8,128)S(1)} %get-tuple-element.27), channel_id=1, source_target_pairs={{0,10},{2,8},{4,14},{6,12},{8,2},{10,0},{12,6},{14,4},{1,11},{3,9}... | collective-permute-start | bytes 110600 | tf_op jit(solution)/shard_map/ppermute | solution.py:437
  22.3 6.7 %collective-permute-start.3 = (f32[72,128]{1,0:T(8,128)S(1)}, f32[72,128]{1,0:T(8,128)S(1)}, u32[]{:S(2)}, u32[]{:S(2)}) collective-permute-start(f32[72,128]{1,0:T(8,128)S(1)} %get-tuple-element.27), channel_id=1, source_target_pairs={{0,8},{2,10},{4,12},{6,14},{8,0},{10,2},{12,4},{14,6},{1,9},{3,11}... | collective-permute-start | bytes 110600 | tf_op jit(solution)/shard_map/ppermute | solution.py:437
  27.4 12.4 %collective-permute-start.8 = (f32[384,128]{1,0:T(8,128)S(1)}, f32[384,128]{1,0:T(8,128)S(1)}, u32[]{:S(2)}, u32[]{:S(2)}) collective-permute-start(f32[384,128]{1,0:T(8,128)S(1)} %get-tuple-element.31), channel_id=1, source_target_pairs={{0,2},{2,0},{4,6},{6,4},{8,10},{10,8},{12,14},{14,12},{1,3},{3,1},... | collective-permute-start | bytes 589832 | tf_op jit(solution)/shard_map/ppermute | solution.py:427
  29.0 10.9 %collective-permute-start.9 = (f32[384,128]{1,0:T(8,128)S(1)}, f32[384,128]{1,0:T(8,128)S(1)}, u32[]{:S(2)}, u32[]{:S(2)}) collective-permute-start(f32[384,128]{1,0:T(8,128)S(1)} %get-tuple-element.32), channel_id=1, source_target_pairs={{0,4},{2,6},{4,0},{6,2},{8,12},{10,14},{12,8},{14,10},{1,5},{3,7},... | collective-permute-start | bytes 589832 | tf_op jit(solution)/shard_map/ppermute | solution.py:427
  29.4 10.5 %collective-permute-start.10 = (f32[384,128]{1,0:T(8,128)S(1)}, f32[384,128]{1,0:T(8,128)S(1)}, u32[]{:S(2)}, u32[]{:S(2)}) collective-permute-start(f32[384,128]{1,0:T(8,128)S(1)} %get-tuple-element.33), channel_id=1, source_target_pairs={{0,6},{2,4},{4,2},{6,0},{8,14},{10,12},{12,10},{14,8},{1,7},{3,5},... | collective-permute-start | bytes 589832 | tf_op jit(solution)/shard_map/ppermute | solution.py:427
  38.4 1.4 %collective-permute-start.7 = (f32[4,4,1792]{2,1,0:T(4,128)S(1)}, f32[4,4,1792]{2,1,0:T(4,128)S(1)}, u32[]{:S(2)}, u32[]{:S(2)}) collective-permute-start(f32[4,4,1792]{2,1,0:T(4,128)S(1)} %get-tuple-element.29), channel_id=1, source_target_pairs={{0,1},{1,0},{2,3},{3,2},{4,5},{5,4},{6,7},{7,6},{8,9},{9,8},{10,11... | collective-permute-start | bytes 344072 | tf_op jit(solution)/shard_map/ppermute | solution.py:442
  46.0 2.0 %collective-permute-start.11 = (f32[4,4,1792]{2,1,0:T(4,128)S(1)}, f32[4,4,1792]{2,1,0:T(4,128)S(1)}, u32[]{:S(2)}, u32[]{:S(2)}) collective-permute-start(f32[4,4,1792]{2,1,0:T(4,128)S(1)} %get-tuple-element.39), channel_id=1, source_target_pairs={{0,1},{1,0},{2,3},{3,2},{4,5},{5,4},{6,7},{7,6},{8,9},{9,8},{10,11... | collective-permute-start | bytes 344072 | tf_op jit(solution)/shard_map/ppermute | solution.py:446
  46.2 8.0 %collective-permute-start.12 = (f32[4,4,1792]{2,1,0:T(4,128)S(1)}, f32[4,4,1792]{2,1,0:T(4,128)S(1)}, u32[]{:S(2)}, u32[]{:S(2)}) collective-permute-start(f32[4,4,1792]{2,1,0:T(4,128)S(1)} %add.9), channel_id=1, source_target_pairs={{0,8},{2,10},{4,12},{6,14},{8,0},{10,2},{12,4},{14,6},{1,9},{3,11}... | collective-permute-start | bytes 344072 | tf_op jit(solution)/shard_map/ppermute | solution.py:444

commit v5 on v4

--- a/solution.py
+++ b/solution.py
@@ -180,55 +180,25 @@
     return block, outs[:half], outs[half:]
 
 
-def segment_kernel(shape, ahead, *refs):
-    parts, capacity, blocks, taps, per_block, half_taps, lags = shape
-    count = len(refs) - 14
+def slots_at_once(slot_count):
+    return next(n for n in (12, 8, 6, 4, 3, 2, 1) if slot_count % n == 0)
+
+
+def window_kernel(shape, place, *refs):
+    parts, capacity, blocks, taps = shape
     rows_in = refs[:parts]
-    near_in = refs[:parts] if count == 2 * parts else refs[parts : 2 * parts]
-    other_in = refs[count - parts : count]
-    keep, send = refs[count : count + 2]
-    (
-        x_sc, y_sc, s_sc, q_sc, inv_sc, h_sc, u_sc, acc, code_v, code_s, listed, sems,
-    ) = refs[count + 2 :]
-    size = 2 * parts
-    me = lax.axis_index("tm")
-    core = lax.axis_index("chan")
-    segment = lax.rem(me + ahead, size)
-    member, home = lax.rem(me, parts), lax.div(me, parts)
+    h_out, inv_out, tags_out, x_sc, y_sc, s_sc, q_sc = refs[-7:]
+    slot_first = place * capacity
     slot_count = parts * capacity
     rows = slot_count * blocks
-    pair_rows = per_block * half_taps
-    pair_count = STOPS * pair_rows
-    block_rows = u_sc.shape[1]
     stack_gain = (taps * TCH) ** 0.5 / TCH
-
     part_rows = capacity * blocks
     for k in range(parts):
-        index = jnp.bitwise_xor(member, k)
         x_sc[k * part_rows : (k + 1) * part_rows, :] = rows_in[k][:part_rows, :]
-        u_sc[home * parts + index] = near_in[k][part_rows:, :]
-        u_sc[(1 - home) * parts + index] = other_in[k][...]
     x_sc[rows:, :] = jnp.zeros((SUB, LANES), jnp.float32)
-    acc[...] = jnp.zeros_like(acc)
-
-    lane_p = lax.broadcasted_iota(jnp.int32, (1, LANES), 1)
-    chan_of = jnp.zeros((1, LANES), jnp.float32)
-    off_of = jnp.zeros((1, LANES), jnp.float32)
-    for s in range(STOPS):
-        maps = u_sc[lax.rem(segment - s + size, size), block_rows - SUB : block_rows, :][:1]
-        here = lax.div(lane_p, pair_rows) == s
-        chan_of = jnp.where(here, pltpu.roll(maps, (s * pair_rows) % LANES, 1), chan_of)
-        off_of = jnp.where(here, pltpu.roll(maps, ((s - 1) * pair_rows) % LANES, 1), off_of)
-    tags = x_sc[pl.ds(blocks - 1, slot_count, stride=blocks), :][:, LANES - 1 :]
-    match = (tags == chan_of).astype(jnp.float32)
-    slots = lax.broadcasted_iota(jnp.int32, (slot_count, LANES), 0).astype(jnp.float32)
-    slot_of = jnp.sum(match * slots, axis=0, keepdims=True)
-    held = jnp.sum(match, axis=0, keepdims=True)
-    code = lane_p.astype(jnp.float32) + slot_of * PAIR_STEP + off_of * (PAIR_STEP * SLOT_STEP)
-    code = jnp.where(held > 0, code, -1.0).astype(jnp.int32)
-    code_v[...] = jnp.broadcast_to(code, (SUB, LANES))
-    copy = pltpu.make_async_copy(code_v, code_s, sems.at[0])
-    copy.start()
+    tags_out[slot_first : slot_first + slot_count, :] = x_sc[
+        pl.ds(blocks - 1, slot_count, stride=blocks), :
+    ]
 
     row_i = lax.broadcasted_iota(jnp.int32, (LANES, LANES), 0)
     lane_i = lax.broadcasted_iota(jnp.int32, (LANES, LANES), 1)
@@ -237,7 +207,7 @@
     ones = jnp.ones((LANES, LANES), jnp.bfloat16)
     sums = jnp.concatenate([tail, ones], axis=1)
     sums = jnp.concatenate([sums, sums], axis=0)
-    chunk_slots = SUB if slot_count % SUB == 0 else 1
+    chunk_slots = slots_at_once(slot_count)
     chunk = chunk_slots * blocks
 
     def prepare(g, c):
@@ -264,20 +234,20 @@
         win_sum = window(s_sc)
         variance = window(q_sc) - win_sum * win_sum / taps
         inv = stack_gain / jnp.sqrt(jnp.maximum(variance, FLOOR_SHARE * taps))
-        inv_sc[pl.ds(base, chunk), :] = inv
+        inv_out[pl.ds(slot_first * blocks + base, chunk), :] = inv
         before = y_sc[pl.ds(base + SUB - 1, chunk), :]
         after = y_sc[pl.ds(base + SUB + 1, chunk), :]
         windows = (
             (jnp.where(left, x0, after), x_sc[pl.ds(base + 2, chunk), :]),
             (jnp.where(left, before, x0), after),
         )
-        slot0 = g * chunk_slots
+        slot0 = slot_first + g * chunk_slots
         for i, window_pair in enumerate(windows):
             for j, part in enumerate(window_pair):
                 lanes = slice(j * LANES, (j + 1) * LANES)
                 for k, piece in enumerate(split(part)):
                     first = (2 * i + k) * blocks
-                    h_sc[pl.ds(slot0, chunk_slots), first : first + blocks, lanes] = piece.reshape(
+                    h_out[pl.ds(slot0, chunk_slots), first : first + blocks, lanes] = piece.reshape(
                         chunk_slots, blocks, LANES
                     )
         return c
@@ -295,6 +265,73 @@
     y_sc[rows + SUB :, :] = jnp.zeros((SUB, LANES), jnp.float32)
     lax.fori_loop(0, slot_count // chunk_slots, turn, 0)
     lax.fori_loop(0, slot_count // chunk_slots, prepare, 0)
+
+
+def row_windows(rows, shape, place, earlier):
+    parts, capacity, blocks, _ = shape
+    total = parts * capacity
+    slot_count = len(rows) * capacity
+    chunk = slots_at_once(slot_count) * blocks
+    return pl.pallas_call(
+        functools.partial(window_kernel, (len(rows),) + shape[1:], place),
+        out_shape=(
+            pltpu.VMEM((total, 4 * blocks, 2 * LANES), jnp.bfloat16),
+            pltpu.VMEM((total * blocks, LANES), jnp.float32),
+            pltpu.VMEM((total, LANES), jnp.float32),
+        ),
+        in_specs=[VMEM] * (len(rows) + len(earlier)),
+        out_specs=(VMEM, VMEM, VMEM),
+        input_output_aliases={len(rows) + i: i for i in range(len(earlier))},
+        scratch_shapes=[
+            pltpu.VMEM((slot_count * blocks + SUB, LANES), jnp.float32),
+            pltpu.VMEM((slot_count * blocks + 2 * SUB, LANES), jnp.float32),
+            pltpu.VMEM((chunk + SUB, 2 * LANES), jnp.float32),
+            pltpu.VMEM((chunk + SUB, 2 * LANES), jnp.float32),
+        ],
+        compiler_params=pltpu.CompilerParams(vmem_limit_bytes=KERNEL_BYTES),
+        name="row_windows",
+    )(*on_chip((*rows, *earlier)))
+
+
+def segment_kernel(shape, ahead, h_in, inv_in, tags_in, *refs):
+    parts, capacity, blocks, _, per_block, half_taps, lags = shape
+    near_in = refs[:parts]
+    other_in = refs[parts : 2 * parts]
+    keep, send, u_sc, acc, code_v, code_s, listed, sems = refs[2 * parts :]
+    size = 2 * parts
+    me = lax.axis_index("tm")
+    core = lax.axis_index("chan")
+    segment = lax.rem(me + ahead, size)
+    member, home = lax.rem(me, parts), lax.div(me, parts)
+    slot_count = parts * capacity
+    pair_rows = per_block * half_taps
+    pair_count = STOPS * pair_rows
+    block_rows = u_sc.shape[1]
+    part_rows = capacity * blocks
+    for k in range(parts):
+        index = jnp.bitwise_xor(member, k)
+        u_sc[home * parts + index] = near_in[k][part_rows:, :]
+        u_sc[(1 - home) * parts + index] = other_in[k][...]
+    acc[...] = jnp.zeros_like(acc)
+
+    lane_p = lax.broadcasted_iota(jnp.int32, (1, LANES), 1)
+    chan_of = jnp.zeros((1, LANES), jnp.float32)
+    off_of = jnp.zeros((1, LANES), jnp.float32)
+    for s in range(STOPS):
+        maps = u_sc[lax.rem(segment - s + size, size), block_rows - SUB : block_rows, :][:1]
+        here = lax.div(lane_p, pair_rows) == s
+        chan_of = jnp.where(here, pltpu.roll(maps, (s * pair_rows) % LANES, 1), chan_of)
+        off_of = jnp.where(here, pltpu.roll(maps, ((s - 1) * pair_rows) % LANES, 1), off_of)
+    tags = tags_in[:, LANES - 1 :]
+    match = (tags == chan_of).astype(jnp.float32)
+    slots = lax.broadcasted_iota(jnp.int32, (slot_count, LANES), 0).astype(jnp.float32)
+    slot_of = jnp.sum(match * slots, axis=0, keepdims=True)
+    held = jnp.sum(match, axis=0, keepdims=True)
+    code = lane_p.astype(jnp.float32) + slot_of * PAIR_STEP + off_of * (PAIR_STEP * SLOT_STEP)
+    code = jnp.where(held > 0, code, -1.0).astype(jnp.int32)
+    code_v[...] = jnp.broadcast_to(code, (SUB, LANES))
+    copy = pltpu.make_async_copy(code_v, code_s, sems.at[0])
+    copy.start()
 
     copy.wait()
 
@@ -342,7 +379,7 @@
                 jnp.concatenate([jnp.where(mask, zero, y) for y in second], axis=1),
             ]
             terms = jnp.dot(
-                h_sc[slot, :, : 3 * HALF],
+                h_in[slot, :, : 3 * HALF],
                 jnp.concatenate(bands, axis=0),
                 preferred_element_type=jnp.float32,
             )
@@ -353,7 +390,7 @@
             )
             back = jnp.where(left_b, pltpu.roll(back, blocks - 1, 0), back)
             corr = front + pltpu.roll(back, HALF, 1)
-            ratio = corr * inv_sc[pl.ds(pl.multiple_of(slot * blocks, blocks), blocks), :]
+            ratio = corr * inv_in[pl.ds(pl.multiple_of(slot * blocks, blocks), blocks), :]
             by_lane = jnp.bitwise_and(off, LANES - 1)
             whole = off >= LANES
             here = pltpu.roll(ratio, lax.rem(LANES - by_lane, LANES), 1)
@@ -379,27 +416,18 @@
                 )
 
 
-def segment_stack(rows, near, other, ahead, shape):
-    parts, capacity, blocks, _, per_block, half_taps, lags = shape
-    slot_count = parts * capacity
+def segment_stack(windows, near, other, ahead, shape):
+    parts, _, blocks, _, per_block, half_taps, lags = shape
     stack_count = STOPS * per_block
     pair_count = stack_count * half_taps
-    chunk = (SUB if slot_count % SUB == 0 else 1) * blocks
     block_rows = other[0].shape[0]
     out = pltpu.VMEM((STOPS, per_block, lags // 2), jnp.float32)
-    operands = list(rows) + ([] if near is rows else list(near)) + list(other)
     return pl.pallas_call(
         functools.partial(segment_kernel, shape, ahead),
         out_shape=(out, out),
-        in_specs=[VMEM] * len(operands),
+        in_specs=[VMEM] * (2 * parts + 3),
         out_specs=(VMEM, VMEM),
         scratch_shapes=[
-            pltpu.VMEM((slot_count * blocks + SUB, LANES), jnp.float32),
-            pltpu.VMEM((slot_count * blocks + 2 * SUB, LANES), jnp.float32),
-            pltpu.VMEM((chunk + SUB, 2 * LANES), jnp.float32),
-            pltpu.VMEM((chunk + SUB, 2 * LANES), jnp.float32),
-            pltpu.VMEM((slot_count * blocks, LANES), jnp.float32),
-            pltpu.VMEM((slot_count, 4 * blocks, 2 * LANES), jnp.bfloat16),
             pltpu.VMEM((2 * parts, block_rows, LANES), jnp.float32),
             pltpu.VMEM((stack_count + 1, blocks, LANES), jnp.float32),
             pltpu.VMEM((SUB, LANES), jnp.int32),
@@ -409,7 +437,7 @@
         ],
         compiler_params=pltpu.CompilerParams(vmem_limit_bytes=KERNEL_BYTES),
         name="segment_stack",
-    )(*on_chip(operands))
+    )(*on_chip((*windows, *near, *other)))
 
 
 def local(records, row_dest, row_chan, row_len, templates, tmpl_chan, tmpl_off):
@@ -432,17 +460,25 @@
         records, row_dest, row_chan, row_len, templates, tmpl_chan, tmpl_off, half
     )
 
-    far_rows = [far_out[0]] + [within(far_out[k], k) for k in range(1, half)]
-    other = [
-        lax.ppermute(block, "tm", [(i, (i ^ k) ^ half) for i in range(size)])
-        for k in range(half)
-    ]
-    own_rows = [own_out[0]] + [within(own_out[k], k) for k in range(1, half)]
-    keep, send = segment_stack(far_rows, far_rows, other, half, shape)
-    far = keep + lax.ppermute(send, "chan", swap)
-    far, *own_rows = lax.optimization_barrier((far, *own_rows))
+    far_rows, other, own_rows = [far_out[0]], [], [own_out[0]]
+    for k in range(1, half):
+        far_rows.append(within(far_out[k], k))
+        own_rows.append(within(own_out[k], k))
+    for k in range(half):
+        other.append(
+            lax.ppermute(block, "tm", [(i, (i ^ k) ^ half) for i in range(size)])
+        )
+    own_windows = row_windows(own_rows[:1], shape[:4], 0, ())
+    windows = row_windows(far_rows[:-1], shape[:4], 0, ())
+    windows = row_windows(far_rows[-1:], shape[:4], half - 1, windows)
+    keep, send = segment_stack(windows, far_rows, other, half, shape)
+    recv = lax.ppermute(send, "chan", swap)
+    windows = row_windows(own_rows[1:-1], shape[:4], 1, own_windows)
+    far = keep + recv
+    far, *windows = lax.optimization_barrier((far, *windows))
     far = lax.ppermute(far, "tm", across)
-    keep, send = segment_stack(own_rows, far_rows, other, 0, shape)
+    windows = row_windows(own_rows[-1:], shape[:4], half - 1, windows)
+    keep, send = segment_stack(windows, far_rows, other, 0, shape)
     total = keep + lax.ppermute(send, "chan", swap) + far
     return total[None]
 

time: 55 us -> 53.7 us (0.976)
  waiting for transfers between devices: 18.7 us -> 16.2 us
  starting transfers between devices: 18.5 us -> 19.6 us
    pallas_call x0 -> x5, Pallas kernels: none -> 4.06 us  [row_windows(): pl.pallas_call(functools.partial(window_kernel, (len(rows),) + shape[1:],...]
    pallas_call x2, Pallas kernels: 13.6 us -> 9.6 us  [segment_stack(): pl.pallas_call(functools.partial(segment_kernel, shape, ahead), out_shape...]
    ppermute x4, waiting for transfers between devices: 11.2 us -> 8.61 us  [local(): lax.ppermute(block, 'tm', [(i, i ^ k ^ half) for i in range(size)])]
    ppermute x6, starting transfers between devices: 8.13 us -> 9.93 us  [within(): lax.ppermute(x, 'tm', [(i, i // half * half + (i % half ^ step)) for i in...]
    ppermute x1, starting transfers between devices: 1.76 us -> 0.01 us  [local(): far = lax.ppermute(far, 'tm', across)]
    ppermute x1, waiting for transfers between devices: 1.31 us -> 0.01 us  [local(): recv = lax.ppermute(send, 'chan', swap)]
    ppermute x1, waiting for transfers between devices: 0.01 us -> 0.96 us  [local(): total = keep + lax.ppermute(send, 'chan', swap) + far]
    ppermute x4, starting transfers between devices: 8.37 us -> 9.05 us  [local(): lax.ppermute(block, 'tm', [(i, i ^ k ^ half) for i in range(size)])]
  transfers between devices with their start and end apart: 13 -> 13, of which waited for: 5 -> 5; matrix products, arithmetic and copies ran while one was open for 0% -> 0% of each run, Pallas kernels for 14% -> 17%
where the time goes in v5:
time: 53.7 us; the launch traced here: 53.5 us
  starting transfers between devices  19.6 us (36%)
  Pallas kernels  16.9 us (31%)
  waiting for transfers between devices  16.2 us (30%)
  other arithmetic  0.72 us (1%)
    ppermute x6, starting transfers between devices, within(): lax.ppermute(x, 'tm', [(i, i // half * half + (i % half ^ step)) for i in...  9.93 us
    pallas_call x2, Pallas kernels, segment_stack(): pl.pallas_call(functools.partial(segment_kernel, shape, ahead), out_shape...  9.6 us
    ppermute x4, starting transfers between devices, local(): lax.ppermute(block, 'tm', [(i, i ^ k ^ half) for i in range(size)])  9.05 us
    ppermute x4, waiting for transfers between devices, local(): lax.ppermute(block, 'tm', [(i, i ^ k ^ half) for i in range(size)])  8.61 us
    ppermute x1, waiting for transfers between devices, local(): far = lax.ppermute(far, 'tm', across)  6.59 us
    pallas_call x5, Pallas kernels, row_windows(): pl.pallas_call(functools.partial(window_kernel, (len(rows),) + shape[1:],...  4.06 us
    pallas_call x1, Pallas kernels, pack(): pl.pallas_call(functools.partial(pack_kernel, half, capacity), out_shape=...  3.19 us
  transfers between devices with their start and end apart: 13, of which 5 were waited for; matrix products, arithmetic and copies ran while one was open for 0% of the time, Pallas kernels for 17%

profile of v5, /device:TPU:0, one launch (start us, length us, event | category | flops | bytes accessed | tf_op | source)
XLA Modules:
  0.0 53.5 jit_solution(12568111762240229292)
XLA Ops:
  0.0 3.2 %pack.1 = (f32[72,128]{1,0:T(8,128)S(1)}, f32[456,128]{1,0:T(8,128)S(1)}, f32[456,128]{1,0:T(8,128)S(1)}, f32[456,128]{1,0:T(8,128)S(1)}, f32[456,128]{1,0:T(8,1...) custom-call(s32[96]{0:T(128)} %dest.1, s32[96]{0:T(128)} %chan.1, ...), custom_call_target="tpu_custom_call" | custom-call | tf_op jit(solution)/shard_map/pack/pallas_call | solution.py:163
  3.2 3.1 %collective-permute-start.2 = (f32[456,128]{1,0:T(8,128)S(1)}, f32[456,128]{1,0:T(8,128)S(1)}, u32[]{:S(2)}, u32[]{:S(2)}) collective-permute-start(f32[456,128]{1,0:T(8,128)S(1)} %get-tuple-element.40), channel_id=1, source_target_pairs={{0,2},{2,0},{4,6},{6,4},{8,10},{10,8},{12,14},{14,12},{1,3},{3,1},... | collective-permute-start | bytes 700424 | tf_op jit(solution)/shard_map/ppermute | solution.py:455
  6.3 1.6 %collective-permute-start.3 = (f32[456,128]{1,0:T(8,128)S(1)}, f32[456,128]{1,0:T(8,128)S(1)}, u32[]{:S(2)}, u32[]{:S(2)}) collective-permute-start(f32[456,128]{1,0:T(8,128)S(1)} %get-tuple-element.41), channel_id=1, source_target_pairs={{0,4},{2,6},{4,0},{6,2},{8,12},{10,14},{12,8},{14,10},{1,5},{3,7},... | collective-permute-start | bytes 700424 | tf_op jit(solution)/shard_map/ppermute | solution.py:455
  7.8 0.0 collective-permute-start.1
  7.8 3.0 %collective-permute-start.4 = (f32[72,128]{1,0:T(8,128)S(1)}, f32[72,128]{1,0:T(8,128)S(1)}, u32[]{:S(2)}, u32[]{:S(2)}) collective-permute-start(f32[72,128]{1,0:T(8,128)S(1)} %get-tuple-element.48), channel_id=1, source_target_pairs={{0,8},{2,10},{4,12},{6,14},{8,0},{10,2},{12,4},{14,6},{1,9},{3,11}... | collective-permute-start | bytes 110600 | tf_op jit(solution)/shard_map/ppermute | solution.py:469
  10.8 1.3 %collective-permute-start.5 = (f32[72,128]{1,0:T(8,128)S(1)}, f32[72,128]{1,0:T(8,128)S(1)}, u32[]{:S(2)}, u32[]{:S(2)}) collective-permute-start(f32[72,128]{1,0:T(8,128)S(1)} %get-tuple-element.48), channel_id=1, source_target_pairs={{0,10},{2,8},{4,14},{6,12},{8,2},{10,0},{12,6},{14,4},{1,11},{3,9}... | collective-permute-start | bytes 110600 | tf_op jit(solution)/shard_map/ppermute | solution.py:469
  12.1 6.6 %collective-permute-done.4.refs_4_ = f32[72,128]{1,0:T(8,128)S(1)} collective-permute-done((f32[72,128]{1,0:T(8,128)S(1)}, f32[72,128]{1,0:T(8,128)S(1)}, u32[]{:S(2)}, u32[]{:S(2)}) %collective-permute-start.4) | collective-permute-done | bytes 36896 | tf_op jit(solution)/shard_map/ppermute | solution.py:469
  18.7 3.5 %collective-permute-start.10 = (f32[384,128]{1,0:T(8,128)S(1)}, f32[384,128]{1,0:T(8,128)S(1)}, u32[]{:S(2)}, u32[]{:S(2)}) collective-permute-start(f32[384,128]{1,0:T(8,128)S(1)} %get-tuple-element.52), channel_id=1, source_target_pairs={{0,4},{2,6},{4,0},{6,2},{8,12},{10,14},{12,8},{14,10},{1,5},{3,7},... | collective-permute-start | bytes 589832 | tf_op jit(solution)/shard_map/ppermute | solution.py:455
  22.2 0.0 collective-permute-done.5.refs_5_
  22.2 0.5 collective-permute-start.9
  22.7 0.0 collective-permute-done.2.refs_1_
  22.7 1.3 %collective-permute-start = (f32[384,128]{1,0:T(8,128)S(1)}, f32[384,128]{1,0:T(8,128)S(1)}, u32[]{:S(2)}, u32[]{:S(2)}) collective-permute-start(f32[384,128]{1,0:T(8,128)S(1)} %get-tuple-element.37), channel_id=1, source_target_pairs={{0,6},{2,4},{4,2},{6,0},{8,14},{10,12},{12,10},{14,8},{1,7},{3,5},... | collective-permute-start | bytes 589832 | tf_op jit(solution)/shard_map/ppermute | solution.py:455
  24.0 0.0 collective-permute-done.3.refs_2_
  24.0 1.3 %collective-permute-start.6 = (f32[72,128]{1,0:T(8,128)S(1)}, f32[72,128]{1,0:T(8,128)S(1)}, u32[]{:S(2)}, u32[]{:S(2)}) collective-permute-start(f32[72,128]{1,0:T(8,128)S(1)} %get-tuple-element.48), channel_id=1, source_target_pairs={{0,12},{2,14},{4,8},{6,10},{8,4},{10,6},{12,0},{14,2},{1,13},{3,15... | collective-permute-start | bytes 110600 | tf_op jit(solution)/shard_map/ppermute | solution.py:469
  25.3 0.0 collective-permute-done.1.refs_0_.refs_3_
  25.4 3.4 %collective-permute-start.7 = (f32[72,128]{1,0:T(8,128)S(1)}, f32[72,128]{1,0:T(8,128)S(1)}, u32[]{:S(2)}, u32[]{:S(2)}) collective-permute-start(f32[72,128]{1,0:T(8,128)S(1)} %get-tuple-element.48), channel_id=1, source_target_pairs={{0,14},{2,12},{4,10},{6,8},{8,6},{10,4},{12,2},{14,0},{1,15},{3,13... | collective-permute-start | bytes 110600 | tf_op jit(solution)/shard_map/ppermute | solution.py:469
  28.8 1.6 %row_windows.5 = (bf16[48,128,256]{2,1,0:T(8,128)(2,1)S(1)}, f32[1536,128]{1,0:T(8,128)S(1)}, f32[48,128]{1,0:T(8,128)S(1)}) custom-call(f32[456,128]{1,0:T(8,128)S(1)} %get-tuple-element.39.refs_0_, f32[456,128]{1,0:T(8,128)S(1)} %collective-permute-done.2.refs_1_, f32[456,128]{1,0:T(8,128)S(1)} %collective-permute-done.3.refs_2_), custom_call_target="tpu_custom_call" | custom-call | tf_op jit(solution)/shard_map/row_windows/pallas_call | solution.py:275
  30.4 0.5 row_windows.6
  30.9 1.5 %collective-permute-done.6.refs_6_ = f32[72,128]{1,0:T(8,128)S(1)} collective-permute-done((f32[72,128]{1,0:T(8,128)S(1)}, f32[72,128]{1,0:T(8,128)S(1)}, u32[]{:S(2)}, u32[]{:S(2)}) %collective-permute-start.6) | collective-permute-done | bytes 36896 | tf_op jit(solution)/shard_map/ppermute | solution.py:469
  32.4 0.5 %collective-permute-done.7.refs_7_ = f32[72,128]{1,0:T(8,128)S(1)} collective-permute-done((f32[72,128]{1,0:T(8,128)S(1)}, f32[72,128]{1,0:T(8,128)S(1)}, u32[]{:S(2)}, u32[]{:S(2)}) %collective-permute-start.7) | collective-permute-done | bytes 36896 | tf_op jit(solution)/shard_map/ppermute | solution.py:469
  32.9 5.5 %segment_stack.2 = (f32[4,4,1792]{2,1,0:T(4,128)S(1)}, f32[4,4,1792]{2,1,0:T(4,128)S(1)}) custom-call(bf16[48,128,256]{2,1,0:T(8,128)(2,1)S(1)} %get-tuple-element.45.h_in, f32[1536,128]{1,0:T(8,128)S(1)} %get-tuple-element.46.inv_in, f32[48,128]{1,0:T(8,128)S(1)} %get-tuple-element.47.tags_in, f32[456,128]{1,0:T(8,128)S(1)} %get-tuple-element.39.refs_0_, ...), custom_call_target="tpu_custom_call" | custom-call | tf_op jit(solution)/shard_map/segment_stack/pallas_call | solution.py:425
  38.4 0.1 collective-permute-start.8
  38.5 0.5 row_windows.7
  39.0 0.0 collective-permute-done.10.refs_1_
  39.0 0.0 collective-permute-done.9.refs_0_
  39.0 1.1 %row_windows.8 = (bf16[48,128,256]{2,1,0:T(8,128)(2,1)S(1)}, f32[1536,128]{1,0:T(8,128)S(1)}, f32[48,128]{1,0:T(8,128)S(1)}) custom-call(f32[384,128]{1,0:T(8,128)S(1)} %collective-permute-done.9.refs_0_, f32[384,128]{1,0:T(8,128)S(1)} %collective-permute-done.10.refs_1_, ...), custom_call_target="tpu_custom_call", output_to_operand_aliasing={{0}: (2, {}), {1}: (3, {}), {2}: (4, {})} | custom-call | tf_op jit(solution)/shard_map/row_windows/pallas_call | solution.py:275
  40.1 0.0 collective-permute-done.8
  40.1 0.0 collective-permute-done.refs_0_
  40.1 0.5 row_windows.9
  40.6 4.1 %segment_stack.3 = (f32[4,4,1792]{2,1,0:T(4,128)S(1)}, f32[4,4,1792]{2,1,0:T(4,128)S(1)}) custom-call(bf16[48,128,256]{2,1,0:T(8,128)(2,1)S(1)} %get-tuple-element.63.h_in, f32[1536,128]{1,0:T(8,128)S(1)} %get-tuple-element.64.inv_in, f32[48,128]{1,0:T(8,128)S(1)} %get-tuple-element.65.tags_in, f32[456,128]{1,0:T(8,128)S(1)} %get-tuple-element.39.refs_0_, ...), custom_call_target="tpu_custom_call" | custom-call | tf_op jit(solution)/shard_map/segment_stack/pallas_call | solution.py:425
  44.7 0.6 %collective-permute-start.11 = (f32[4,4,1792]{2,1,0:T(4,128)S(1)}, f32[4,4,1792]{2,1,0:T(4,128)S(1)}, u32[]{:S(2)}, u32[]{:S(2)}) collective-permute-start(f32[4,4,1792]{2,1,0:T(4,128)S(1)} %get-tuple-element.67), channel_id=1, source_target_pairs={{0,1},{1,0},{2,3},{3,2},{4,5},{5,4},{6,7},{7,6},{8,9},{9,8},{10,11... | collective-permute-start | bytes 344072 | tf_op jit(solution)/shard_map/ppermute | solution.py:482
  45.3 0.0 collective-permute-start.12
  45.3 1.0 %collective-permute-done.11 = f32[4,4,1792]{2,1,0:T(4,128)S(1)} collective-permute-done((f32[4,4,1792]{2,1,0:T(4,128)S(1)}, f32[4,4,1792]{2,1,0:T(4,128)S(1)}, u32[]{:S(2)}, u32[]{:S(2)}) %collective-permute-start.11) | collective-permute-done | bytes 114720 | tf_op jit(solution)/shard_map/ppermute | solution.py:482
  46.2 6.6 %collective-permute-done.12 = f32[4,4,1792]{2,1,0:T(4,128)S(1)} collective-permute-done((f32[4,4,1792]{2,1,0:T(4,128)S(1)}, f32[4,4,1792]{2,1,0:T(4,128)S(1)}, u32[]{:S(2)}, u32[]{:S(2)}) %collective-permute-start.12) | collective-permute-done | bytes 114720 | tf_op jit(solution)/shard_map/ppermute | solution.py:479
  52.8 0.7 %add_bitcast_fusion = f32[1,4,4,1792]{3,2,1,0:T(4,128)} fusion(f32[4,4,1792]{2,1,0:T(4,128)S(1)} %collective-permute-done.12, f32[4,4,1792]{2,1,0:T(4,128)S(1)} %get-tuple-element.66, f32[4,4,1792]{2,1,0:T(4,128)S(1)} %collective-permute-done.11), kind=kLoop, calls=%fused_computation | loop fusion | flops 57344 | bytes 458752 | tf_op jit(solution)/shard_map/broadcast_in_dim | solution.py:483
  (1 shorter events, 0.0 us)
Async XLA Ops:
  3.2 19.5 %collective-permute-start.2 = (f32[456,128]{1,0:T(8,128)S(1)}, f32[456,128]{1,0:T(8,128)S(1)}, u32[]{:S(2)}, u32[]{:S(2)}) collective-permute-start(f32[456,128]{1,0:T(8,128)S(1)} %get-tuple-element.40), channel_id=1, source_target_pairs={{0,2},{2,0},{4,6},{6,4},{8,10},{10,8},{12,14},{14,12},{1,3},{3,1},... | collective-permute-start | bytes 700424 | tf_op jit(solution)/shard_map/ppermute | solution.py:455
  6.3 17.7 %collective-permute-start.3 = (f32[456,128]{1,0:T(8,128)S(1)}, f32[456,128]{1,0:T(8,128)S(1)}, u32[]{:S(2)}, u32[]{:S(2)}) collective-permute-start(f32[456,128]{1,0:T(8,128)S(1)} %get-tuple-element.41), channel_id=1, source_target_pairs={{0,4},{2,6},{4,0},{6,2},{8,12},{10,14},{12,8},{14,10},{1,5},{3,7},... | collective-permute-start | bytes 700424 | tf_op jit(solution)/shard_map/ppermute | solution.py:455
  7.8 17.5 %collective-permute-start.1 = (f32[456,128]{1,0:T(8,128)S(1)}, f32[456,128]{1,0:T(8,128)S(1)}, u32[]{:S(2)}, u32[]{:S(2)}) collective-permute-start(f32[456,128]{1,0:T(8,128)S(1)} %get-tuple-element.38), channel_id=1, source_target_pairs={{0,6},{2,4},{4,2},{6,0},{8,14},{10,12},{12,10},{14,8},{1,7},{3,5},... | collective-permute-start | bytes 700424 | tf_op jit(solution)/shard_map/ppermute | solution.py:455
  7.8 10.9 %collective-permute-start.4 = (f32[72,128]{1,0:T(8,128)S(1)}, f32[72,128]{1,0:T(8,128)S(1)}, u32[]{:S(2)}, u32[]{:S(2)}) collective-permute-start(f32[72,128]{1,0:T(8,128)S(1)} %get-tuple-element.48), channel_id=1, source_target_pairs={{0,8},{2,10},{4,12},{6,14},{8,0},{10,2},{12,4},{14,6},{1,9},{3,11}... | collective-permute-start | bytes 110600 | tf_op jit(solution)/shard_map/ppermute | solution.py:469
  10.8 11.4 %collective-permute-start.5 = (f32[72,128]{1,0:T(8,128)S(1)}, f32[72,128]{1,0:T(8,128)S(1)}, u32[]{:S(2)}, u32[]{:S(2)}) collective-permute-start(f32[72,128]{1,0:T(8,128)S(1)} %get-tuple-element.48), channel_id=1, source_target_pairs={{0,10},{2,8},{4,14},{6,12},{8,2},{10,0},{12,6},{14,4},{1,11},{3,9}... | collective-permute-start | bytes 110600 | tf_op jit(solution)/shard_map/ppermute | solution.py:469
  18.7 20.3 %collective-permute-start.10 = (f32[384,128]{1,0:T(8,128)S(1)}, f32[384,128]{1,0:T(8,128)S(1)}, u32[]{:S(2)}, u32[]{:S(2)}) collective-permute-start(f32[384,128]{1,0:T(8,128)S(1)} %get-tuple-element.52), channel_id=1, source_target_pairs={{0,4},{2,6},{4,0},{6,2},{8,12},{10,14},{12,8},{14,10},{1,5},{3,7},... | collective-permute-start | bytes 589832 | tf_op jit(solution)/shard_map/ppermute | solution.py:455
  22.2 16.8 %collective-permute-start.9 = (f32[384,128]{1,0:T(8,128)S(1)}, f32[384,128]{1,0:T(8,128)S(1)}, u32[]{:S(2)}, u32[]{:S(2)}) collective-permute-start(f32[384,128]{1,0:T(8,128)S(1)} %get-tuple-element.51), channel_id=1, source_target_pairs={{0,2},{2,0},{4,6},{6,4},{8,10},{10,8},{12,14},{14,12},{1,3},{3,1},... | collective-permute-start | bytes 589832 | tf_op jit(solution)/shard_map/ppermute | solution.py:455
  22.7 17.4 %collective-permute-start = (f32[384,128]{1,0:T(8,128)S(1)}, f32[384,128]{1,0:T(8,128)S(1)}, u32[]{:S(2)}, u32[]{:S(2)}) collective-permute-start(f32[384,128]{1,0:T(8,128)S(1)} %get-tuple-element.37), channel_id=1, source_target_pairs={{0,6},{2,4},{4,2},{6,0},{8,14},{10,12},{12,10},{14,8},{1,7},{3,5},... | collective-permute-start | bytes 589832 | tf_op jit(solution)/shard_map/ppermute | solution.py:455
  24.0 8.4 %collective-permute-start.6 = (f32[72,128]{1,0:T(8,128)S(1)}, f32[72,128]{1,0:T(8,128)S(1)}, u32[]{:S(2)}, u32[]{:S(2)}) collective-permute-start(f32[72,128]{1,0:T(8,128)S(1)} %get-tuple-element.48), channel_id=1, source_target_pairs={{0,12},{2,14},{4,8},{6,10},{8,4},{10,6},{12,0},{14,2},{1,13},{3,15... | collective-permute-start | bytes 110600 | tf_op jit(solution)/shard_map/ppermute | solution.py:469
  25.4 7.5 %collective-permute-start.7 = (f32[72,128]{1,0:T(8,128)S(1)}, f32[72,128]{1,0:T(8,128)S(1)}, u32[]{:S(2)}, u32[]{:S(2)}) collective-permute-start(f32[72,128]{1,0:T(8,128)S(1)} %get-tuple-element.48), channel_id=1, source_target_pairs={{0,14},{2,12},{4,10},{6,8},{8,6},{10,4},{12,2},{14,0},{1,15},{3,13... | collective-permute-start | bytes 110600 | tf_op jit(solution)/shard_map/ppermute | solution.py:469
  38.4 1.7 %collective-permute-start.8 = (f32[4,4,1792]{2,1,0:T(4,128)S(1)}, f32[4,4,1792]{2,1,0:T(4,128)S(1)}, u32[]{:S(2)}, u32[]{:S(2)}) collective-permute-start(f32[4,4,1792]{2,1,0:T(4,128)S(1)} %get-tuple-element.50), channel_id=1, source_target_pairs={{0,1},{1,0},{2,3},{3,2},{4,5},{5,4},{6,7},{7,6},{8,9},{9,8},{10,11... | collective-permute-start | bytes 344072 | tf_op jit(solution)/shard_map/ppermute | solution.py:475
  44.7 1.5 %collective-permute-start.11 = (f32[4,4,1792]{2,1,0:T(4,128)S(1)}, f32[4,4,1792]{2,1,0:T(4,128)S(1)}, u32[]{:S(2)}, u32[]{:S(2)}) collective-permute-start(f32[4,4,1792]{2,1,0:T(4,128)S(1)} %get-tuple-element.67), channel_id=1, source_target_pairs={{0,1},{1,0},{2,3},{3,2},{4,5},{5,4},{6,7},{7,6},{8,9},{9,8},{10,11... | collective-permute-start | bytes 344072 | tf_op jit(solution)/shard_map/ppermute | solution.py:482
  45.3 7.6 %collective-permute-start.12 = (f32[4,4,1792]{2,1,0:T(4,128)S(1)}, f32[4,4,1792]{2,1,0:T(4,128)S(1)}, u32[]{:S(2)}, u32[]{:S(2)}) collective-permute-start(f32[4,4,1792]{2,1,0:T(4,128)S(1)} %add.9), channel_id=1, source_target_pairs={{0,8},{2,10},{4,12},{6,14},{8,0},{10,2},{12,4},{14,6},{1,9},{3,11}... | collective-permute-start | bytes 344072 | tf_op jit(solution)/shard_map/ppermute | solution.py:479

commit v6 on v5

--- a/solution.py
+++ b/solution.py
@@ -232,8 +232,8 @@
             )
 
         win_sum = window(s_sc)
-        variance = window(q_sc) - win_sum * win_sum / taps
-        inv = stack_gain / jnp.sqrt(jnp.maximum(variance, FLOOR_SHARE * taps))
+        variance = window(q_sc) - win_sum * win_sum * (1.0 / taps)
+        inv = stack_gain * lax.rsqrt(jnp.maximum(variance, FLOOR_SHARE * taps))
         inv_out[pl.ds(slot_first * blocks + base, chunk), :] = inv
         before = y_sc[pl.ds(base + SUB - 1, chunk), :]
         after = y_sc[pl.ds(base + SUB + 1, chunk), :]
@@ -468,12 +468,11 @@
         other.append(
             lax.ppermute(block, "tm", [(i, (i ^ k) ^ half) for i in range(size)])
         )
-    own_windows = row_windows(own_rows[:1], shape[:4], 0, ())
     windows = row_windows(far_rows[:-1], shape[:4], 0, ())
     windows = row_windows(far_rows[-1:], shape[:4], half - 1, windows)
     keep, send = segment_stack(windows, far_rows, other, half, shape)
     recv = lax.ppermute(send, "chan", swap)
-    windows = row_windows(own_rows[1:-1], shape[:4], 1, own_windows)
+    windows = row_windows(own_rows[:-1], shape[:4], 0, ())
     far = keep + recv
     far, *windows = lax.optimization_barrier((far, *windows))
     far = lax.ppermute(far, "tm", across)

time: 53.7 us -> 53.6 us (level)
    pallas_call x5 -> x4, Pallas kernels: 4.06 us -> 3.78 us  [row_windows(): pl.pallas_call(functools.partial(window_kernel, (len(rows),) + shape[1:],...]
where the time goes in v6:
time: 53.6 us; the launch traced here: 53.4 us
  starting transfers between devices  19.6 us (37%)
  Pallas kernels  16.6 us (31%)
  waiting for transfers between devices  16.4 us (31%)
  other arithmetic  0.73 us (1%)
    ppermute x6, starting transfers between devices, within(): lax.ppermute(x, 'tm', [(i, i // half * half + (i % half ^ step)) for i in...  9.93 us
    pallas_call x2, Pallas kernels, segment_stack(): pl.pallas_call(functools.partial(segment_kernel, shape, ahead), out_shape...  9.6 us
    ppermute x4, starting transfers between devices, local(): lax.ppermute(block, 'tm', [(i, i ^ k ^ half) for i in range(size)])  9.05 us
    ppermute x4, waiting for transfers between devices, local(): lax.ppermute(block, 'tm', [(i, i ^ k ^ half) for i in range(size)])  8.79 us
    ppermute x1, waiting for transfers between devices, local(): far = lax.ppermute(far, 'tm', across)  6.61 us
    pallas_call x4, Pallas kernels, row_windows(): pl.pallas_call(functools.partial(window_kernel, (len(rows),) + shape[1:],...  3.78 us
    pallas_call x1, Pallas kernels, pack(): pl.pallas_call(functools.partial(pack_kernel, half, capacity), out_shape=...  3.19 us
  transfers between devices with their start and end apart: 13, of which 5 were waited for; matrix products, arithmetic and copies ran while one was open for 0% of the time, Pallas kernels for 17%

profile of v6, /device:TPU:0, one launch (start us, length us, event | category | flops | bytes accessed | tf_op | source)
XLA Modules:
  0.0 53.4 jit_solution(2646762767077107284)
XLA Ops:
  0.0 3.2 %pack.1 = (f32[72,128]{1,0:T(8,128)S(1)}, f32[456,128]{1,0:T(8,128)S(1)}, f32[456,128]{1,0:T(8,128)S(1)}, f32[456,128]{1,0:T(8,128)S(1)}, f32[456,128]{1,0:T(8,1...) custom-call(s32[96]{0:T(128)} %dest.1, s32[96]{0:T(128)} %chan.1, ...), custom_call_target="tpu_custom_call" | custom-call | tf_op jit(solution)/shard_map/pack/pallas_call | solution.py:163
  3.2 3.1 %collective-permute-start.2 = (f32[456,128]{1,0:T(8,128)S(1)}, f32[456,128]{1,0:T(8,128)S(1)}, u32[]{:S(2)}, u32[]{:S(2)}) collective-permute-start(f32[456,128]{1,0:T(8,128)S(1)} %get-tuple-element.37), channel_id=1, source_target_pairs={{0,2},{2,0},{4,6},{6,4},{8,10},{10,8},{12,14},{14,12},{1,3},{3,1},... | collective-permute-start | bytes 700424 | tf_op jit(solution)/shard_map/ppermute | solution.py:455
  6.3 1.6 %collective-permute-start.3 = (f32[456,128]{1,0:T(8,128)S(1)}, f32[456,128]{1,0:T(8,128)S(1)}, u32[]{:S(2)}, u32[]{:S(2)}) collective-permute-start(f32[456,128]{1,0:T(8,128)S(1)} %get-tuple-element.38), channel_id=1, source_target_pairs={{0,4},{2,6},{4,0},{6,2},{8,12},{10,14},{12,8},{14,10},{1,5},{3,7},... | collective-permute-start | bytes 700424 | tf_op jit(solution)/shard_map/ppermute | solution.py:455
  7.8 0.0 collective-permute-start.1
  7.8 3.0 %collective-permute-start.4 = (f32[72,128]{1,0:T(8,128)S(1)}, f32[72,128]{1,0:T(8,128)S(1)}, u32[]{:S(2)}, u32[]{:S(2)}) collective-permute-start(f32[72,128]{1,0:T(8,128)S(1)} %get-tuple-element.45), channel_id=1, source_target_pairs={{0,8},{2,10},{4,12},{6,14},{8,0},{10,2},{12,4},{14,6},{1,9},{3,11}... | collective-permute-start | bytes 110600 | tf_op jit(solution)/shard_map/ppermute | solution.py:469
  10.8 1.3 %collective-permute-start.5 = (f32[72,128]{1,0:T(8,128)S(1)}, f32[72,128]{1,0:T(8,128)S(1)}, u32[]{:S(2)}, u32[]{:S(2)}) collective-permute-start(f32[72,128]{1,0:T(8,128)S(1)} %get-tuple-element.45), channel_id=1, source_target_pairs={{0,10},{2,8},{4,14},{6,12},{8,2},{10,0},{12,6},{14,4},{1,11},{3,9}... | collective-permute-start | bytes 110600 | tf_op jit(solution)/shard_map/ppermute | solution.py:469
  12.1 6.6 %collective-permute-done.4.refs_4_ = f32[72,128]{1,0:T(8,128)S(1)} collective-permute-done((f32[72,128]{1,0:T(8,128)S(1)}, f32[72,128]{1,0:T(8,128)S(1)}, u32[]{:S(2)}, u32[]{:S(2)}) %collective-permute-start.4) | collective-permute-done | bytes 36896 | tf_op jit(solution)/shard_map/ppermute | solution.py:469
  18.7 3.5 %collective-permute-start.10 = (f32[384,128]{1,0:T(8,128)S(1)}, f32[384,128]{1,0:T(8,128)S(1)}, u32[]{:S(2)}, u32[]{:S(2)}) collective-permute-start(f32[384,128]{1,0:T(8,128)S(1)} %get-tuple-element.50), channel_id=1, source_target_pairs={{0,4},{2,6},{4,0},{6,2},{8,12},{10,14},{12,8},{14,10},{1,5},{3,7},... | collective-permute-start | bytes 589832 | tf_op jit(solution)/shard_map/ppermute | solution.py:455
  22.2 0.0 collective-permute-done.5.refs_5_
  22.2 0.5 collective-permute-start.9
  22.7 0.0 collective-permute-done.2.refs_1_
  22.7 1.3 %collective-permute-start = (f32[384,128]{1,0:T(8,128)S(1)}, f32[384,128]{1,0:T(8,128)S(1)}, u32[]{:S(2)}, u32[]{:S(2)}) collective-permute-start(f32[384,128]{1,0:T(8,128)S(1)} %get-tuple-element.34), channel_id=1, source_target_pairs={{0,6},{2,4},{4,2},{6,0},{8,14},{10,12},{12,10},{14,8},{1,7},{3,5},... | collective-permute-start | bytes 589832 | tf_op jit(solution)/shard_map/ppermute | solution.py:455
  24.0 0.0 collective-permute-done.3.refs_2_
  24.0 1.3 %collective-permute-start.6 = (f32[72,128]{1,0:T(8,128)S(1)}, f32[72,128]{1,0:T(8,128)S(1)}, u32[]{:S(2)}, u32[]{:S(2)}) collective-permute-start(f32[72,128]{1,0:T(8,128)S(1)} %get-tuple-element.45), channel_id=1, source_target_pairs={{0,12},{2,14},{4,8},{6,10},{8,4},{10,6},{12,0},{14,2},{1,13},{3,15... | collective-permute-start | bytes 110600 | tf_op jit(solution)/shard_map/ppermute | solution.py:469
  25.3 0.0 collective-permute-done.1.refs_0_.refs_3_
  25.4 3.4 %collective-permute-start.7 = (f32[72,128]{1,0:T(8,128)S(1)}, f32[72,128]{1,0:T(8,128)S(1)}, u32[]{:S(2)}, u32[]{:S(2)}) collective-permute-start(f32[72,128]{1,0:T(8,128)S(1)} %get-tuple-element.45), channel_id=1, source_target_pairs={{0,14},{2,12},{4,10},{6,8},{8,6},{10,4},{12,2},{14,0},{1,15},{3,13... | collective-permute-start | bytes 110600 | tf_op jit(solution)/shard_map/ppermute | solution.py:469
  28.8 1.5 %row_windows.4 = (bf16[48,128,256]{2,1,0:T(8,128)(2,1)S(1)}, f32[1536,128]{1,0:T(8,128)S(1)}, f32[48,128]{1,0:T(8,128)S(1)}) custom-call(f32[456,128]{1,0:T(8,128)S(1)} %get-tuple-element.36.refs_0_, f32[456,128]{1,0:T(8,128)S(1)} %collective-permute-done.2.refs_1_, f32[456,128]{1,0:T(8,128)S(1)} %collective-permute-done.3.refs_2_), custom_call_target="tpu_custom_call" | custom-call | tf_op jit(solution)/shard_map/row_windows/pallas_call | solution.py:275
  30.3 0.4 row_windows.5
  30.7 1.7 %collective-permute-done.6.refs_6_ = f32[72,128]{1,0:T(8,128)S(1)} collective-permute-done((f32[72,128]{1,0:T(8,128)S(1)}, f32[72,128]{1,0:T(8,128)S(1)}, u32[]{:S(2)}, u32[]{:S(2)}) %collective-permute-start.6) | collective-permute-done | bytes 36896 | tf_op jit(solution)/shard_map/ppermute | solution.py:469
  32.4 0.5 %collective-permute-done.7.refs_7_ = f32[72,128]{1,0:T(8,128)S(1)} collective-permute-done((f32[72,128]{1,0:T(8,128)S(1)}, f32[72,128]{1,0:T(8,128)S(1)}, u32[]{:S(2)}, u32[]{:S(2)}) %collective-permute-start.7) | collective-permute-done | bytes 36896 | tf_op jit(solution)/shard_map/ppermute | solution.py:469
  32.9 5.5 %segment_stack.2 = (f32[4,4,1792]{2,1,0:T(4,128)S(1)}, f32[4,4,1792]{2,1,0:T(4,128)S(1)}) custom-call(bf16[48,128,256]{2,1,0:T(8,128)(2,1)S(1)} %get-tuple-element.42.h_in, f32[1536,128]{1,0:T(8,128)S(1)} %get-tuple-element.43.inv_in, f32[48,128]{1,0:T(8,128)S(1)} %get-tuple-element.44.tags_in, f32[456,128]{1,0:T(8,128)S(1)} %get-tuple-element.36.refs_0_, ...), custom_call_target="tpu_custom_call" | custom-call | tf_op jit(solution)/shard_map/segment_stack/pallas_call | solution.py:425
  38.4 0.1 collective-permute-start.8
  38.5 0.0 collective-permute-done.10.refs_2_
  38.5 0.0 collective-permute-done.9.refs_1_
  38.5 1.5 %row_windows.6 = (bf16[48,128,256]{2,1,0:T(8,128)(2,1)S(1)}, f32[1536,128]{1,0:T(8,128)S(1)}, f32[48,128]{1,0:T(8,128)S(1)}) custom-call(f32[384,128]{1,0:T(8,128)S(1)} %get-tuple-element.48.refs_0_, f32[384,128]{1,0:T(8,128)S(1)} %collective-permute-done.9.refs_1_, f32[384,128]{1,0:T(8,128)S(1)} %collective-permute-done.10.refs_2_), custom_call_target="tpu_custom_call" | custom-call | tf_op jit(solution)/shard_map/row_windows/pallas_call | solution.py:275
  40.0 0.0 collective-permute-done.8
  40.0 0.0 collective-permute-done.refs_0_
  40.1 0.4 row_windows.7
  40.5 4.1 %segment_stack.3 = (f32[4,4,1792]{2,1,0:T(4,128)S(1)}, f32[4,4,1792]{2,1,0:T(4,128)S(1)}) custom-call(bf16[48,128,256]{2,1,0:T(8,128)(2,1)S(1)} %get-tuple-element.57.h_in, f32[1536,128]{1,0:T(8,128)S(1)} %get-tuple-element.58.inv_in, f32[48,128]{1,0:T(8,128)S(1)} %get-tuple-element.59.tags_in, f32[456,128]{1,0:T(8,128)S(1)} %get-tuple-element.36.refs_0_, ...), custom_call_target="tpu_custom_call" | custom-call | tf_op jit(solution)/shard_map/segment_stack/pallas_call | solution.py:425
  44.6 0.5 %collective-permute-start.11 = (f32[4,4,1792]{2,1,0:T(4,128)S(1)}, f32[4,4,1792]{2,1,0:T(4,128)S(1)}, u32[]{:S(2)}, u32[]{:S(2)}) collective-permute-start(f32[4,4,1792]{2,1,0:T(4,128)S(1)} %get-tuple-element.61), channel_id=1, source_target_pairs={{0,1},{1,0},{2,3},{3,2},{4,5},{5,4},{6,7},{7,6},{8,9},{9,8},{10,11... | collective-permute-start | bytes 344072 | tf_op jit(solution)/shard_map/ppermute | solution.py:481
  45.1 0.0 collective-permute-start.12
  45.1 1.0 %collective-permute-done.11 = f32[4,4,1792]{2,1,0:T(4,128)S(1)} collective-permute-done((f32[4,4,1792]{2,1,0:T(4,128)S(1)}, f32[4,4,1792]{2,1,0:T(4,128)S(1)}, u32[]{:S(2)}, u32[]{:S(2)}) %collective-permute-start.11) | collective-permute-done | bytes 114720 | tf_op jit(solution)/shard_map/ppermute | solution.py:481
  46.1 6.6 %collective-permute-done.12 = f32[4,4,1792]{2,1,0:T(4,128)S(1)} collective-permute-done((f32[4,4,1792]{2,1,0:T(4,128)S(1)}, f32[4,4,1792]{2,1,0:T(4,128)S(1)}, u32[]{:S(2)}, u32[]{:S(2)}) %collective-permute-start.12) | collective-permute-done | bytes 114720 | tf_op jit(solution)/shard_map/ppermute | solution.py:478
  52.7 0.7 %add_bitcast_fusion = f32[1,4,4,1792]{3,2,1,0:T(4,128)} fusion(f32[4,4,1792]{2,1,0:T(4,128)S(1)} %collective-permute-done.12, f32[4,4,1792]{2,1,0:T(4,128)S(1)} %get-tuple-element.60, f32[4,4,1792]{2,1,0:T(4,128)S(1)} %collective-permute-done.11), kind=kLoop, calls=%fused_computation | loop fusion | flops 57344 | bytes 458752 | tf_op jit(solution)/shard_map/broadcast_in_dim | solution.py:482
  (1 shorter events, 0.0 us)
Async XLA Ops:
  3.2 19.5 %collective-permute-start.2 = (f32[456,128]{1,0:T(8,128)S(1)}, f32[456,128]{1,0:T(8,128)S(1)}, u32[]{:S(2)}, u32[]{:S(2)}) collective-permute-start(f32[456,128]{1,0:T(8,128)S(1)} %get-tuple-element.37), channel_id=1, source_target_pairs={{0,2},{2,0},{4,6},{6,4},{8,10},{10,8},{12,14},{14,12},{1,3},{3,1},... | collective-permute-start | bytes 700424 | tf_op jit(solution)/shard_map/ppermute | solution.py:455
  6.3 17.7 %collective-permute-start.3 = (f32[456,128]{1,0:T(8,128)S(1)}, f32[456,128]{1,0:T(8,128)S(1)}, u32[]{:S(2)}, u32[]{:S(2)}) collective-permute-start(f32[456,128]{1,0:T(8,128)S(1)} %get-tuple-element.38), channel_id=1, source_target_pairs={{0,4},{2,6},{4,0},{6,2},{8,12},{10,14},{12,8},{14,10},{1,5},{3,7},... | collective-permute-start | bytes 700424 | tf_op jit(solution)/shard_map/ppermute | solution.py:455
  7.8 17.5 %collective-permute-start.1 = (f32[456,128]{1,0:T(8,128)S(1)}, f32[456,128]{1,0:T(8,128)S(1)}, u32[]{:S(2)}, u32[]{:S(2)}) collective-permute-start(f32[456,128]{1,0:T(8,128)S(1)} %get-tuple-element.35), channel_id=1, source_target_pairs={{0,6},{2,4},{4,2},{6,0},{8,14},{10,12},{12,10},{14,8},{1,7},{3,5},... | collective-permute-start | bytes 700424 | tf_op jit(solution)/shard_map/ppermute | solution.py:455
  7.8 10.9 %collective-permute-start.4 = (f32[72,128]{1,0:T(8,128)S(1)}, f32[72,128]{1,0:T(8,128)S(1)}, u32[]{:S(2)}, u32[]{:S(2)}) collective-permute-start(f32[72,128]{1,0:T(8,128)S(1)} %get-tuple-element.45), channel_id=1, source_target_pairs={{0,8},{2,10},{4,12},{6,14},{8,0},{10,2},{12,4},{14,6},{1,9},{3,11}... | collective-permute-start | bytes 110600 | tf_op jit(solution)/shard_map/ppermute | solution.py:469
  10.8 11.4 %collective-permute-start.5 = (f32[72,128]{1,0:T(8,128)S(1)}, f32[72,128]{1,0:T(8,128)S(1)}, u32[]{:S(2)}, u32[]{:S(2)}) collective-permute-start(f32[72,128]{1,0:T(8,128)S(1)} %get-tuple-element.45), channel_id=1, source_target_pairs={{0,10},{2,8},{4,14},{6,12},{8,2},{10,0},{12,6},{14,4},{1,11},{3,9}... | collective-permute-start | bytes 110600 | tf_op jit(solution)/shard_map/ppermute | solution.py:469
  18.7 19.8 %collective-permute-start.10 = (f32[384,128]{1,0:T(8,128)S(1)}, f32[384,128]{1,0:T(8,128)S(1)}, u32[]{:S(2)}, u32[]{:S(2)}) collective-permute-start(f32[384,128]{1,0:T(8,128)S(1)} %get-tuple-element.50), channel_id=1, source_target_pairs={{0,4},{2,6},{4,0},{6,2},{8,12},{10,14},{12,8},{14,10},{1,5},{3,7},... | collective-permute-start | bytes 589832 | tf_op jit(solution)/shard_map/ppermute | solution.py:455
  22.2 16.3 %collective-permute-start.9 = (f32[384,128]{1,0:T(8,128)S(1)}, f32[384,128]{1,0:T(8,128)S(1)}, u32[]{:S(2)}, u32[]{:S(2)}) collective-permute-start(f32[384,128]{1,0:T(8,128)S(1)} %get-tuple-element.49), channel_id=1, source_target_pairs={{0,2},{2,0},{4,6},{6,4},{8,10},{10,8},{12,14},{14,12},{1,3},{3,1},... | collective-permute-start | bytes 589832 | tf_op jit(solution)/shard_map/ppermute | solution.py:455
  22.7 17.3 %collective-permute-start = (f32[384,128]{1,0:T(8,128)S(1)}, f32[384,128]{1,0:T(8,128)S(1)}, u32[]{:S(2)}, u32[]{:S(2)}) collective-permute-start(f32[384,128]{1,0:T(8,128)S(1)} %get-tuple-element.34), channel_id=1, source_target_pairs={{0,6},{2,4},{4,2},{6,0},{8,14},{10,12},{12,10},{14,8},{1,7},{3,5},... | collective-permute-start | bytes 589832 | tf_op jit(solution)/shard_map/ppermute | solution.py:455
  24.0 8.4 %collective-permute-start.6 = (f32[72,128]{1,0:T(8,128)S(1)}, f32[72,128]{1,0:T(8,128)S(1)}, u32[]{:S(2)}, u32[]{:S(2)}) collective-permute-start(f32[72,128]{1,0:T(8,128)S(1)} %get-tuple-element.45), channel_id=1, source_target_pairs={{0,12},{2,14},{4,8},{6,10},{8,4},{10,6},{12,0},{14,2},{1,13},{3,15... | collective-permute-start | bytes 110600 | tf_op jit(solution)/shard_map/ppermute | solution.py:469
  25.4 7.5 %collective-permute-start.7 = (f32[72,128]{1,0:T(8,128)S(1)}, f32[72,128]{1,0:T(8,128)S(1)}, u32[]{:S(2)}, u32[]{:S(2)}) collective-permute-start(f32[72,128]{1,0:T(8,128)S(1)} %get-tuple-element.45), channel_id=1, source_target_pairs={{0,14},{2,12},{4,10},{6,8},{8,6},{10,4},{12,2},{14,0},{1,15},{3,13... | collective-permute-start | bytes 110600 | tf_op jit(solution)/shard_map/ppermute | solution.py:469
  38.4 1.6 %collective-permute-start.8 = (f32[4,4,1792]{2,1,0:T(4,128)S(1)}, f32[4,4,1792]{2,1,0:T(4,128)S(1)}, u32[]{:S(2)}, u32[]{:S(2)}) collective-permute-start(f32[4,4,1792]{2,1,0:T(4,128)S(1)} %get-tuple-element.47), channel_id=1, source_target_pairs={{0,1},{1,0},{2,3},{3,2},{4,5},{5,4},{6,7},{7,6},{8,9},{9,8},{10,11... | collective-permute-start | bytes 344072 | tf_op jit(solution)/shard_map/ppermute | solution.py:474
  44.6 1.5 %collective-permute-start.11 = (f32[4,4,1792]{2,1,0:T(4,128)S(1)}, f32[4,4,1792]{2,1,0:T(4,128)S(1)}, u32[]{:S(2)}, u32[]{:S(2)}) collective-permute-start(f32[4,4,1792]{2,1,0:T(4,128)S(1)} %get-tuple-element.61), channel_id=1, source_target_pairs={{0,1},{1,0},{2,3},{3,2},{4,5},{5,4},{6,7},{7,6},{8,9},{9,8},{10,11... | collective-permute-start | bytes 344072 | tf_op jit(solution)/shard_map/ppermute | solution.py:481
  45.1 7.6 %collective-permute-start.12 = (f32[4,4,1792]{2,1,0:T(4,128)S(1)}, f32[4,4,1792]{2,1,0:T(4,128)S(1)}, u32[]{:S(2)}, u32[]{:S(2)}) collective-permute-start(f32[4,4,1792]{2,1,0:T(4,128)S(1)} %add.9), channel_id=1, source_target_pairs={{0,8},{2,10},{4,12},{6,14},{8,0},{10,2},{12,4},{14,6},{1,9},{3,11}... | collective-permute-start | bytes 344072 | tf_op jit(solution)/shard_map/ppermute | solution.py:478
